TPU v7x, 128 devices: a whole 4x4x4 slice. The times are simulated.
128 devices in a mesh: role: 2 (over core), dev: 64 (over z, y, x).
Axes of the slice: x: 4, y: 4, z: 4, core: 2. Of those that a mesh axis runs over, the one named last changes fastest.
Arguments:
- moe_rows: bfloat16 [4096, 3584], P(('role', 'dev')), may hold values from -6 to 6
- expert_ids: int32 [4096, 8], P(('role', 'dev')), may hold values from 0 to 63, all different within a row; in each aligned block of 32 rows (0 to 31, 32 to 63, ...) at most 8 rows name the same one
- gate_weights: float32 [4096, 8], P(('role', 'dev')), may hold values from 0.05 to 0.6
- w_gate: bfloat16 [64, 3584, 1024], P('dev', None, 'role'), may hold values from -0.09375 to 0.09375
- w_up: bfloat16 [64, 3584, 1024], P('dev', None, 'role'), may hold values from -0.09375 to 0.09375
- w_down: bfloat16 [64, 3584, 1024], P('dev', None, 'role'), may hold values from -0.1875 to 0.1875
- q_latent: bfloat16 [512, 64, 512], P(('role', 'dev')), may hold values from -40 to 40
- q_rope: bfloat16 [512, 4096], P(('role', 'dev')), may hold values from -4 to 4
- latent_cache: bfloat16 [512, 2048, 512], P(('role', 'dev')), may hold values from -4 to 4
- rope_cache: bfloat16 [512, 64, 2048], P(('role', 'dev')), may hold values from -4 to 4
- lengths: int32 [512], P(('role', 'dev')), may hold values from 2 to 2048, as said below
Outputs:
- moe_out: bfloat16 [4096, 3584], P(('role', 'dev'))
- attended: bfloat16 [512, 64, 512], P(('role', 'dev'))
Inputs may be any that keep to these rules, and one draw needn't show every extreme that they name: `expert_ids`: each row names 8 different experts; among the rows of one device no expert is named more than 8 times. `lengths`: the first row holds all 2048 cached tokens.
All inputs are finite; a program needn't handle non-finite values.
Results may differ from a plain program's by a relative error of at most 0.0057.
Values may be sent and summed in bfloat16 or wider, within the bound.
A program may use at most 128 MiB of HBM per device.

v0:
```python
import jax
import jax.numpy as jnp
from jax import lax
from jax.sharding import PartitionSpec as P

score_scale = 192.0 ** (-0.5)


def expert_block(chosen, gate_matrix, up_matrix, down_matrix):
    gate_part = jnp.dot(chosen, gate_matrix, preferred_element_type=jnp.float32)
    up_part = jnp.dot(chosen, up_matrix, preferred_element_type=jnp.float32)
    hidden_units = (jax.nn.silu(gate_part) * up_part).astype(jnp.bfloat16)
    return lax.dot_general(
        hidden_units, down_matrix, (((1,), (1,)), ((), ())), preferred_element_type=jnp.float32
    )


def attend_row(query_lat, query_rope, cache_lat, cache_rope, length):
    head_count = query_lat.shape[0]
    rope_width = cache_rope.shape[0]
    scores = lax.dot_general(
        query_lat, cache_lat, (((1,), (1,)), ((), ())), preferred_element_type=jnp.float32
    )
    scores = scores + jnp.dot(
        query_rope.reshape(head_count, rope_width), cache_rope, preferred_element_type=jnp.float32
    )
    scores = scores * score_scale
    positions = jnp.arange(cache_lat.shape[0], dtype=jnp.int32)
    valid = (positions < length)[None, :]
    scores = jnp.where(valid, scores, jnp.float32(-1e30))
    highest = jnp.max(scores, axis=1, keepdims=True)
    weights = jnp.where(valid, jnp.exp(scores - highest), jnp.float32(0.0))
    probs = (weights / jnp.sum(weights, axis=1, keepdims=True)).astype(jnp.bfloat16)
    return jnp.dot(probs, cache_lat, preferred_element_type=jnp.float32).astype(jnp.bfloat16)


def per_device(
    moe_rows,
    expert_ids,
    gate_weights,
    w_gate,
    w_up,
    w_down,
    q_latent,
    q_rope,
    latent_cache,
    rope_cache,
    lengths,
):
    tok_count = moe_rows.shape[0]
    width = moe_rows.shape[1]
    topk_count = expert_ids.shape[1]
    experts = lax.axis_size("dev")
    capacity = min(tok_count, 2 * tok_count * topk_count // experts)
    flat_ids = expert_ids.reshape(-1)
    pair_count = flat_ids.shape[0]
    one_hot = (flat_ids[:, None] == jnp.arange(experts, dtype=jnp.int32)[None, :]).astype(jnp.int32)
    earlier = jnp.cumsum(one_hot, axis=0) - one_hot
    slot_index = jnp.sum(earlier * one_hot, axis=1)
    destination = flat_ids * capacity + slot_index
    source_row = jnp.full((experts * capacity,), tok_count, jnp.int32)
    source_row = source_row.at[destination].set(
        jnp.arange(pair_count, dtype=jnp.int32) // topk_count
    )
    padded_rows = jnp.concatenate([moe_rows, jnp.zeros((1, width), jnp.bfloat16)], axis=0)
    outgoing = padded_rows[source_row].reshape(experts, capacity, width)
    arrived = lax.all_to_all(outgoing, "dev", split_axis=0, concat_axis=0, tiled=True)
    own_rows = arrived.reshape(experts * capacity, width)
    both_rows = lax.all_gather(own_rows, "role", axis=0, tiled=True)
    expert_sum = lax.psum_scatter(
        expert_block(both_rows, w_gate[0], w_up[0], w_down[0]),
        "role",
        scatter_dimension=0,
        tiled=True,
    )
    finished = expert_sum.astype(jnp.bfloat16).reshape(experts, capacity, width)
    returned = lax.all_to_all(finished, "dev", split_axis=0, concat_axis=0, tiled=True)
    flat_back = returned.reshape(experts * capacity, width)
    picked = flat_back[destination].reshape(tok_count, topk_count, width).astype(jnp.float32)
    moe_out = jnp.sum(picked * gate_weights[:, :, None], axis=1).astype(jnp.bfloat16)
    attended = jax.vmap(attend_row)(q_latent, q_rope, latent_cache, rope_cache, lengths)
    return (moe_out, attended)


def solution(mesh):
    placed = (
        P(("role", "dev"), None),
        P(("role", "dev"), None),
        P(("role", "dev"), None),
        P("dev", None, "role"),
        P("dev", None, "role"),
        P("dev", None, "role"),
        P(("role", "dev"), None, None),
        P(("role", "dev"), None),
        P(("role", "dev"), None, None),
        P(("role", "dev"), None, None),
        P(("role", "dev")),
    )
    return jax.shard_map(
        per_device,
        mesh=mesh,
        in_specs=placed,
        out_specs=(P(("role", "dev"), None), P(("role", "dev"), None, None)),
        check_vma=False,
    )
```

profile of v0, /device:TPU:0, one launch (start us, length us, event | category | flops | bytes accessed | tf_op | source)
XLA Modules:
  0.0 223.4 jit_solution(7646429509567561305)
XLA Ops:
  7.2 0.0 copy-start
  7.2 0.0 all-gather.2.cloned.1.call-start
  7.2 0.8 copy.15
  8.1 0.1 eq.29
  8.2 0.1 eq.25
  8.2 0.7 broadcast_multiply_fusion
  9.0 0.6 reduce-window.6
  9.6 0.2 slice_reduce_fusion
  9.8 0.1 copy.14
  9.9 0.1 mul.42
  10.0 0.1 fusion.21
  10.1 1.4 scatter_custom_fusion
  11.5 1.0 concatenate.3
  12.5 4.2 %gather_fusion = bf16[512,3584]{1,0:T(8,128)(2,1)} fusion(bf16[33,3584]{1,0:T(8,128)(2,1)S(1)} %concatenate.3, s32[1024]{0:T(1024)S(1)} %pad_clamp_fusion.1), kind=kCustom, calls=%fused_computation | custom fusion | bytes 7342080 | tf_op jit(solution)/shard_map/gather | solution.py:66
  16.7 58.5 %all_to_all.10 = bf16[64,8,3584]{2,1,0:T(8,128)(2,1)} all-to-all(bf16[64,8,3584]{2,1,0:T(8,128)(2,1)} %bitcast.49), channel_id=1, replica_groups=mesh['role'=2,'dev'=64] {'dev'}, dimensions={0} | all-to-all | bytes 7340032 | tf_op jit(solution)/shard_map/all_to_all | solution.py:67
  75.2 0.0 all-gather.2.cloned.1.call-update
  75.2 0.0 reduce-scatter.2.cloned.1.call-start
  75.3 17.3 %all-gather.2.cloned.1.call-done = bf16[1024,3584]{1,0:T(8,128)(2,1)} async-done(((bf16[512,3584]{1,0:T(8,128)(2,1)}), bf16[1024,3584]{1,0:T(8,128)(2,1)}) %all-gather.2.cloned.1.call-update) | async-done | bytes 7340048 | tf_op jit(solution)/shard_map/all_gather | solution.py:69
  92.6 7.3 %fusion.4 = f32[1024,512]{1,0:T(8,128)S(1)} fusion(bf16[1024,3584]{1,0:T(8,128)(2,1)} %all-gather.2.cloned.1.call-done, bf16[1,3584,512]{2,1,0:T(8,128)(2,1)} %param.15), kind=kOutput, calls=%fused_computation.8 | convolution fusion | flops 3758096384 | bytes 13107200 | tf_op jit(solution)/shard_map/dot_general | solution.py:11
  99.9 15.5 %fusion.2 = f32[1024,3584]{1,0:T(8,128)} fusion(bf16[1,3584,512]{2,1,0:T(8,128)(2,1)} %param.16, f32[1024,512]{1,0:T(8,128)S(1)} %fusion.4, bf16[1024,3584]{1,0:T(8,128)(2,1)} %all-gather.2.cloned.1.call-done, bf16[1,3584,512]{2,1,0:T(8,128)(2,1)} %param.14), kind=kOutput, calls=%fused_computation.6 | convolution fusion | flops 7519338496 | bytes 31457280 | tf_op jit(solution)/shard_map/dot_general | solution.py:13
  115.4 0.0 reduce-scatter.2.cloned.1.call-update
  115.4 28.0 %reduce-scatter.2.cloned.1.call-done = f32[512,3584]{1,0:T(8,128)} async-done(((f32[1024,3584]{1,0:T(8,128)}), f32[512,3584]{1,0:T(8,128)}) %reduce-scatter.2.cloned.1.call-update) | async-done | bytes 7340048 | tf_op jit(solution)/shard_map/reduce_scatter | solution.py:70
  143.4 5.3 %convert_bitcast_fusion = bf16[64,8,3584]{2,1,0:T(8,128)(2,1)} fusion(f32[512,3584]{1,0:T(8,128)} %reduce-scatter.2.cloned.1.call-done), kind=kLoop, calls=%fused_computation.12 | loop fusion | flops 1835008 | bytes 11010048 | tf_op jit(solution)/shard_map/reshape | solution.py:76
  148.7 0.0 copy-start.3
  148.7 0.0 copy-start.2
  148.7 0.0 copy-start.4
  148.7 0.0 copy-start.1
  148.7 11.0 %all-to-all-start.1 = ((bf16[64,8,3584]{2,1,0:T(8,128)(2,1)}), bf16[64,8,3584]{2,1,0:T(8,128)(2,1)}, u32[]{:S(2)}, u32[]{:S(2)}) async-start(bf16[64,8,3584]{2,1,0:T(8,128)(2,1)} %convert_bitcast_fusion), calls=%async_computation.2 | async-start | bytes 7340032 | tf_op jit(solution)/shard_map/all_to_all | solution.py:77
  159.7 0.0 copy-done.3
  159.7 0.1 copy.18
  159.8 0.0 copy-done.2
  159.8 0.1 reshape.93
  159.9 0.0 copy-done.4
  159.9 0.1 iota_compare_fusion.2
  160.0 0.0 copy-done.1
  160.0 6.0 %fusion.27 = f32[4,64,2048]{2,1,0:T(8,128)S(1)} fusion(bf16[4,64,512]{2,1,0:T(8,128)(2,1)S(1)} %copy-done.1, bf16[4,2048,512]{2,1,0:T(8,128)(2,1)} %param.19), kind=kOutput, calls=%fused_computation.47 | convolution fusion | flops 536870912 | bytes 10747904 | tf_op jit(solution)/shard_map/vmap()/dot_general | solution.py:21
  166.0 0.0 copy-done
  166.0 2.4 %fusion.26 = (f32[4,64]{1,0:T(4,128)S(1)}, f32[4,64,2048]{2,1,0:T(8,128)}) fusion(pred[4,2048]{1,0:T(4,128)(4,1)S(1)} %iota_compare_fusion.2, f32[4,64,2048]{2,1,0:T(8,128)S(1)} %fusion.27, bf16[4,64,64]{2,1,0:T(8,128)(2,1)S(1)} %reshape.93, bf16[4,64,2048]{2,1,0:T(8,128)(2,1)S(1)} %copy-done), kind=kOutput, calls=%fused_computation.46 | convolution fusion | flops 70256640 | bytes 5284864 | tf_op jit(solution)/shard_map/vmap()/sub | solution.py:32
  168.4 6.3 %convolution_convert_fusion = bf16[4,64,512]{2,1,0:T(8,128)(2,1)} fusion(bf16[4,2048,512]{2,1,0:T(8,128)(2,1)} %param.19, f32[4,64,2048]{2,1,0:T(8,128)} %get-tuple-element.3, f32[4,64]{1,0:T(4,128)S(1)} %get-tuple-element.2), kind=kOutput, calls=%fused_computation.21 | convolution fusion | flops 538050560 | bytes 10748928 | tf_op jit(solution)/shard_map/vmap()/dot_general | solution.py:34
  174.7 33.6 %all-to-all-done.1 = bf16[64,8,3584]{2,1,0:T(8,128)(2,1)} async-done(((bf16[64,8,3584]{2,1,0:T(8,128)(2,1)}), bf16[64,8,3584]{2,1,0:T(8,128)(2,1)}, u32[]{:S(2)}, u32[]{:S(2)}) %all-to-all-start.1) | async-done | bytes 3670048 | tf_op jit(solution)/shard_map/all_to_all | solution.py:77
  208.4 6.0 %gather_fusion.1 = bf16[256,3584]{1,0:T(8,128)(2,1)S(1)} fusion(bf16[512,3584]{1,0:T(8,128)(2,1)} %bitcast.9, s32[1024]{0:T(1024)S(1)} %pad_clamp_fusion), kind=kCustom, calls=%fused_computation.1 | custom fusion | bytes 3671040 | tf_op jit(solution)/shard_map/gather | solution.py:79
  214.4 2.1 fusion.1
  (8 shorter events, 0.1 us)
Async XLA Ops:
  7.2 158.9 %copy-start = (bf16[4,64,2048]{2,1,0:T(8,128)(2,1)S(1)}, bf16[4,64,2048]{2,1,0:T(8,128)(2,1)}, u32[]{:S(2)}) copy-start(bf16[4,64,2048]{2,1,0:T(8,128)(2,1)} %param.20) | copy-start | bytes 3145732
  7.2 85.4 %all-gather.2.cloned.1.call-start = ((), (), s32[]{:S(2)}) async-start(), calls=%async_computation.3 | async-start | bytes 11010048 | tf_op jit(solution)/shard_map/all_gather | solution.py:69
  75.2 68.2 %reduce-scatter.2.cloned.1.call-start = ((), (), s32[]{:S(2)}) async-start(), calls=%async_computation.4 | async-start | bytes 22020096 | tf_op jit(solution)/shard_map/reduce_scatter | solution.py:70
  148.7 11.0 %copy-start.3 = (f32[32,8]{0,1:T(8,128)S(1)}, f32[32,8]{0,1:T(8,128)}, u32[]{:S(2)}) copy-start(f32[32,8]{0,1:T(8,128)} %param.13) | copy-start | bytes 3076
  148.7 11.1 %copy-start.2 = (bf16[4,4096]{1,0:T(4,128)(2,1)S(1)}, bf16[4,4096]{1,0:T(4,128)(2,1)}, u32[]{:S(2)}) copy-start(bf16[4,4096]{1,0:T(4,128)(2,1)} %param.18) | copy-start | bytes 98308
  148.7 11.2 %copy-start.4 = (s32[4]{0:T(128)S(1)}, s32[4]{0:T(128)}, u32[]{:S(2)}) copy-start(s32[4]{0:T(128)} %param.21) | copy-start | bytes 52
  148.7 11.3 %copy-start.1 = (bf16[4,64,512]{2,1,0:T(8,128)(2,1)S(1)}, bf16[4,64,512]{2,1,0:T(8,128)(2,1)}, u32[]{:S(2)}) copy-start(bf16[4,64,512]{2,1,0:T(8,128)(2,1)} %param.17) | copy-start | bytes 786436
  148.7 59.7 %all-to-all-start.1 = ((bf16[64,8,3584]{2,1,0:T(8,128)(2,1)}), bf16[64,8,3584]{2,1,0:T(8,128)(2,1)}, u32[]{:S(2)}, u32[]{:S(2)}) async-start(bf16[64,8,3584]{2,1,0:T(8,128)(2,1)} %convert_bitcast_fusion), calls=%async_computation.2 | async-start | bytes 7340032 | tf_op jit(solution)/shard_map/all_to_all | solution.py:77
Sparse Core Ops, SparseCore 0:
  75.3 17.2 all-gather.1
  115.5 27.8 reduce-scatter.1
where the time goes:
time: 224 us; the launch traced here: 223 us
  waiting for transfers between devices  79 us (35%)
  blocking collectives  58.5 us (26%)
  matrix products  37.5 us (17%)
  local copies, waits for them, and re-layouts  14.2 us (6%)
  between operations  14.2 us (6%)
  starting transfers between devices  11.1 us (5%)
  other arithmetic  8.97 us (4%)
    all_to_all x1, blocking collectives, per_device(): lax.all_to_all(outgoing, 'dev', split_axis=0, concat_axis=0, tiled=True)  58.5 us
    all_to_all x1, waiting for transfers between devices, per_device(): lax.all_to_all(finished, 'dev', split_axis=0, concat_axis=0, tiled=True)  33.6 us
    reduce_scatter x1, waiting for transfers between devices, per_device(): lax.psum_scatter(expert_block(both_rows, w_gate[0], w_up[0], w_down[0]),...  28 us
    all_gather x1, waiting for transfers between devices, per_device(): both_rows = lax.all_gather(own_rows, 'role', axis=0, tiled=True)  17.3 us
    dot_general x1, matrix products, expert_block(): lax.dot_general(hidden_units, down_matrix, (((1,), (1,)), ((), ())), pref...  15.5 us
    all_to_all x1, starting transfers between devices, per_device(): lax.all_to_all(finished, 'dev', split_axis=0, concat_axis=0, tiled=True)  11 us
    dot_general x1, matrix products, expert_block(): up_part = jnp.dot(chosen, up_matrix, preferred_element_type=jnp.float32)  7.28 us
    dot_general x1, matrix products, attend_row(): jnp.dot(probs, cache_lat, preferred_element_type=jnp.float32)  6.34 us
  transfers between devices with their start and end apart: 3, of which 3 were waited for; matrix products, arithmetic and copies ran while one was open for 7% of the time, Pallas kernels for 0%

commit v1 on v0

--- a/solution.py
+++ b/solution.py
@@ -13,6 +13,22 @@
     return lax.dot_general(
         hidden_units, down_matrix, (((1,), (1,)), ((), ())), preferred_element_type=jnp.float32
     )
+
+
+def full_expert(rows, w_gate, w_up, w_down):
+    gate_both = lax.all_gather(w_gate[0], "role", axis=0)
+    up_both = lax.all_gather(w_up[0], "role", axis=0)
+    down_both = lax.all_gather(w_down[0], "role", axis=0)
+    total = None
+    for half in range(gate_both.shape[0]):
+        gate_part = jnp.dot(rows, gate_both[half], preferred_element_type=jnp.float32)
+        up_part = jnp.dot(rows, up_both[half], preferred_element_type=jnp.float32)
+        hidden_units = (jax.nn.silu(gate_part) * up_part).astype(jnp.bfloat16)
+        term = lax.dot_general(
+            hidden_units, down_both[half], (((1,), (1,)), ((), ())), preferred_element_type=jnp.float32
+        )
+        total = term if total is None else total + term
+    return total
 
 
 def attend_row(query_lat, query_rope, cache_lat, cache_rope, length):
@@ -66,13 +82,7 @@
     outgoing = padded_rows[source_row].reshape(experts, capacity, width)
     arrived = lax.all_to_all(outgoing, "dev", split_axis=0, concat_axis=0, tiled=True)
     own_rows = arrived.reshape(experts * capacity, width)
-    both_rows = lax.all_gather(own_rows, "role", axis=0, tiled=True)
-    expert_sum = lax.psum_scatter(
-        expert_block(both_rows, w_gate[0], w_up[0], w_down[0]),
-        "role",
-        scatter_dimension=0,
-        tiled=True,
-    )
+    expert_sum = full_expert(own_rows, w_gate, w_up, w_down)
     finished = expert_sum.astype(jnp.bfloat16).reshape(experts, capacity, width)
     returned = lax.all_to_all(finished, "dev", split_axis=0, concat_axis=0, tiled=True)
     flat_back = returned.reshape(experts * capacity, width)

time: 224 us -> 179 us (0.80)
  waiting for transfers between devices: 79 us -> 35.6 us
  matrix products: 37.5 us -> 46.5 us
  other arithmetic: 8.97 us -> 3 us
  starting transfers between devices: 11.1 us -> 7.8 us
    reduce_scatter x1 -> x0, waiting for transfers between devices: 28 us -> none  [per_device(): lax.psum_scatter(expert_block(both_rows, w_gate[0], w_up[0], w_down[0]),...]
    all_gather x1 -> x3, waiting for transfers between devices: 17.3 us -> 0.04 us  [the longest x1 0.02 us: full_expert(): up_both = lax.all_gather(w_up[0], 'role', axis=0)]
    dot_general x2 -> x4, matrix products: 22.8 us -> 31.8 us  [the longest x2 23.3 us: full_expert(): lax.dot_general(hidden_units, down_both[half], (((1,), (1,)), ((), ())),...]
    reshape x1 -> x0, other arithmetic: 5.27 us -> none  [per_device(): finished = expert_sum.astype(jnp.bfloat16).reshape(experts, capacity, width)]
    all_to_all x1, starting transfers between devices: 11 us -> 7.69 us  [per_device(): lax.all_to_all(finished, 'dev', split_axis=0, concat_axis=0, tiled=True)]
  transfers between devices with their start and end apart: 3 -> 4, of which waited for: 3 -> 1; matrix products, arithmetic and copies ran while one was open for 7% -> 17% of each run, Pallas kernels for 0% -> 0%
where the time goes in v1:
time: 179 us
  blocking collectives  58.5 us (33%)
  matrix products  46.5 us (26%)
  waiting for transfers between devices  35.6 us (20%)
  between operations  13.9 us (8%)
  local copies, waits for them, and re-layouts  13.6 us (8%)
  starting transfers between devices  7.8 us (4%)
  other arithmetic  3 us (2%)
    all_to_all x1, blocking collectives, per_device(): lax.all_to_all(outgoing, 'dev', split_axis=0, concat_axis=0, tiled=True)  58.5 us
    all_to_all x1, waiting for transfers between devices, per_device(): lax.all_to_all(finished, 'dev', split_axis=0, concat_axis=0, tiled=True)  33.5 us
    dot_general x2, matrix products, full_expert(): lax.dot_general(hidden_units, down_both[half], (((1,), (1,)), ((), ())),...  23.3 us
    dot_general x2, matrix products, full_expert(): jnp.dot(rows, gate_both[half], preferred_element_type=jnp.float32)  8.48 us
    all_to_all x1, starting transfers between devices, per_device(): lax.all_to_all(finished, 'dev', split_axis=0, concat_axis=0, tiled=True)  7.69 us
    dot_general x1, matrix products, attend_row(): jnp.dot(probs, cache_lat, preferred_element_type=jnp.float32)  6.34 us
    gather x1, local copies, waits for them, and re-layouts, per_device(): flat_back[destination].reshape(tok_count, topk_count, width)  6.04 us
    dot_general x1, matrix products, attend_row(): lax.dot_general(query_lat, cache_lat, (((1,), (1,)), ((), ())), preferred...  6 us
  transfers between devices with their start and end apart: 4, of which 1 were waited for; matrix products, arithmetic and copies ran while one was open for 17% of the time, Pallas kernels for 0%

profile of v1, /device:TPU:0, one launch (start us, length us, event | category | flops | bytes accessed | tf_op | source)
XLA Modules:
  0.0 178.8 jit_solution(1586354353643577461)
XLA Ops:
  7.2 0.0 copy-start
  7.2 0.0 all-gather.4.cloned.1.call-start
  7.2 0.7 all-gather.4.cloned.1.call-update
  7.9 0.0 copy-start.5
  7.9 0.0 copy-start.3
  7.9 0.0 all-gather.6.cloned.1.call-start
  8.0 0.7 all-gather.6.cloned.1.call-update
  8.7 0.0 all-gather.8.cloned.1.call-start
  8.7 0.7 all-gather.8.cloned.1.call-update
  9.4 0.0 copy-done.5
  9.4 0.1 copy.20
  9.5 0.1 eq.29
  9.6 0.1 eq.25
  9.7 0.1 copy.19
  9.8 0.1 mul.48
  9.9 0.6 reduce-window.6
  10.5 0.2 slice_reduce_fusion
  10.7 0.0 copy-done.3
  10.8 0.1 fusion.38
  10.9 1.4 scatter_custom_fusion
  12.3 4.2 %gather_fusion = bf16[512,3584]{1,0:T(8,128)(2,1)} fusion(bf16[33,3584]{1,0:T(8,128)(2,1)S(1)} %concatenate.3, s32[1024]{0:T(1024)S(1)} %pad_clamp_fusion.1), kind=kCustom, calls=%fused_computation | custom fusion | bytes 7342080 | tf_op jit(solution)/shard_map/gather | solution.py:82
  16.5 58.5 %all_to_all.10 = bf16[64,8,3584]{2,1,0:T(8,128)(2,1)} all-to-all(bf16[64,8,3584]{2,1,0:T(8,128)(2,1)} %bitcast.85), channel_id=1, replica_groups=mesh['role'=2,'dev'=64] {'dev'}, dimensions={0} | all-to-all | bytes 7340032 | tf_op jit(solution)/shard_map/all_to_all | solution.py:83
  75.0 0.0 all-gather.4.cloned.1.call-done
  75.0 0.0 copy-start.1
  75.0 0.0 copy-start.8
  75.0 6.4 %fusion.3 = f32[512,512]{1,0:T(8,128)S(1)} fusion(bf16[2,3584,512]{2,1,0:T(8,128)(2,1)} %all-gather.4.cloned.1.call-done, bf16[64,8,3584]{2,1,0:T(8,128)(2,1)} %all_to_all.10), kind=kOutput, calls=%fused_computation.10 | convolution fusion | flops 1879048192 | bytes 8388608 | tf_op jit(solution)/shard_map/dot_general | solution.py:24
  81.5 0.0 copy-done.1
  81.5 1.0 copy-done.8
  82.5 2.0 %fusion.6 = f32[512,512]{1,0:T(8,128)S(1)} fusion(bf16[2,3584,512]{2,1,0:T(8,128)(2,1)S(1)} %copy-done.8, bf16[64,8,3584]{2,1,0:T(8,128)(2,1)S(1)} %copy-done.1), kind=kOutput, calls=%fused_computation.16 | convolution fusion | flops 1879048192 | bytes 8388608 | tf_op jit(solution)/shard_map/dot_general | solution.py:24
  84.6 0.0 all-gather.6.cloned.1.call-done
  84.6 0.0 all-gather.8.cloned.1.call-done
  84.6 11.2 %fusion.4 = f32[512,3584]{1,0:T(8,128)} fusion(bf16[2,3584,512]{2,1,0:T(8,128)(2,1)} %all-gather.8.cloned.1.call-done, bf16[2,3584,512]{2,1,0:T(8,128)(2,1)} %all-gather.6.cloned.1.call-done, bf16[64,8,3584]{2,1,0:T(8,128)(2,1)} %all_to_all.10, f32[512,512]{1,0:T(8,128)S(1)} %fusion.6), kind=kOutput, calls=%fused_computation.12 | convolution fusion | flops 3759669248 | bytes 19398656 | tf_op jit(solution)/shard_map/dot_general | solution.py:27
  95.8 12.2 %fusion.1 = bf16[64,8,3584]{2,1,0:T(8,128)(2,1)} fusion(f32[512,3584]{1,0:T(8,128)} %fusion.4, bf16[2,3584,512]{2,1,0:T(8,128)(2,1)} %all-gather.8.cloned.1.call-done, bf16[2,3584,512]{2,1,0:T(8,128)(2,1)} %all-gather.6.cloned.1.call-done, bf16[64,8,3584]{2,1,0:T(8,128)(2,1)} %all_to_all.10, f32[512,512]{1,0:T(8,128)S(1)} %fusion.3), kind=kOutput, calls=%fused_computation.5 | convolution fusion | flops 3763339264 | bytes 23068672 | tf_op jit(solution)/shard_map/dot_general | solution.py:27
  108.0 0.0 copy-start.6
  108.0 0.0 copy-start.4
  108.0 0.0 copy-start.7
  108.0 0.0 copy-start.2
  108.0 7.7 %all-to-all-start.1 = ((bf16[64,8,3584]{2,1,0:T(8,128)(2,1)}), bf16[64,8,3584]{2,1,0:T(8,128)(2,1)}, u32[]{:S(2)}, u32[]{:S(2)}) async-start(bf16[64,8,3584]{2,1,0:T(8,128)(2,1)} %fusion.1), calls=%async_computation.1 | async-start | bytes 7340032 | tf_op jit(solution)/shard_map/all_to_all | solution.py:87
  115.7 0.0 copy-done.6
  115.7 0.1 copy.23
  115.8 0.0 copy-done.4
  115.8 0.1 reshape.93
  115.9 0.0 copy-done.7
  115.9 0.1 iota_compare_fusion.2
  116.0 0.0 copy-done.2
  116.0 6.0 %fusion.45 = f32[4,64,2048]{2,1,0:T(8,128)S(1)} fusion(bf16[4,64,512]{2,1,0:T(8,128)(2,1)S(1)} %copy-done.2, bf16[4,2048,512]{2,1,0:T(8,128)(2,1)} %param.19), kind=kOutput, calls=%fused_computation.62 | convolution fusion | flops 536870912 | bytes 10747904 | tf_op jit(solution)/shard_map/vmap()/dot_general | solution.py:37
  122.0 0.0 copy-done
  122.0 2.3 %fusion.44 = (f32[4,64]{1,0:T(4,128)S(1)}, f32[4,64,2048]{2,1,0:T(8,128)}) fusion(pred[4,2048]{1,0:T(4,128)(4,1)S(1)} %iota_compare_fusion.2, f32[4,64,2048]{2,1,0:T(8,128)S(1)} %fusion.45, bf16[4,64,64]{2,1,0:T(8,128)(2,1)S(1)} %reshape.93, bf16[4,64,2048]{2,1,0:T(8,128)(2,1)S(1)} %copy-done), kind=kOutput, calls=%fused_computation.61 | convolution fusion | flops 70256640 | bytes 5284864 | tf_op jit(solution)/shard_map/vmap()/sub | solution.py:48
  124.3 6.3 %convolution_convert_fusion = bf16[4,64,512]{2,1,0:T(8,128)(2,1)} fusion(bf16[4,2048,512]{2,1,0:T(8,128)(2,1)} %param.19, f32[4,64,2048]{2,1,0:T(8,128)} %get-tuple-element.3, f32[4,64]{1,0:T(4,128)S(1)} %get-tuple-element.2), kind=kOutput, calls=%fused_computation.34 | convolution fusion | flops 538050560 | bytes 10748928 | tf_op jit(solution)/shard_map/vmap()/dot_general | solution.py:50
  130.7 33.5 %all-to-all-done.1 = bf16[64,8,3584]{2,1,0:T(8,128)(2,1)} async-done(((bf16[64,8,3584]{2,1,0:T(8,128)(2,1)}), bf16[64,8,3584]{2,1,0:T(8,128)(2,1)}, u32[]{:S(2)}, u32[]{:S(2)}) %all-to-all-start.1) | async-done | bytes 3670048 | tf_op jit(solution)/shard_map/all_to_all | solution.py:87
  164.1 6.0 %gather_fusion.1 = bf16[256,3584]{1,0:T(8,128)(2,1)S(1)} fusion(bf16[512,3584]{1,0:T(8,128)(2,1)} %bitcast.12, s32[1024]{0:T(1024)S(1)} %pad_clamp_fusion), kind=kCustom, calls=%fused_computation.1 | custom fusion | bytes 3671040 | tf_op jit(solution)/shard_map/gather | solution.py:89
  170.2 2.1 %fusion.7 = bf16[32,3584]{1,0:T(8,128)(2,1)} fusion(bf16[256,3584]{1,0:T(8,128)(2,1)S(1)} %gather_fusion.1, f32[32,8]{1,0:T(8,128)S(1)} %copy.23), kind=kLoop, calls=%fused_computation.18 | loop fusion | flops 2637824 | bytes 2065408 | tf_op jit(solution)/shard_map/reduce_sum | solution.py:90
  (10 shorter events, 0.1 us)
Async XLA Ops:
  7.2 114.8 %copy-start = (bf16[4,64,2048]{2,1,0:T(8,128)(2,1)S(1)}, bf16[4,64,2048]{2,1,0:T(8,128)(2,1)}, u32[]{:S(2)}) copy-start(bf16[4,64,2048]{2,1,0:T(8,128)(2,1)} %param.20) | copy-start | bytes 3145732
  7.2 67.9 %all-gather.4.cloned.1.call-start = ((), (), s32[]{:S(2)}) async-start(), calls=%async_computation.2 | async-start | bytes 11010048 | tf_op jit(solution)/shard_map/all_gather | solution.py:19
  7.9 1.5 copy-start.5
  7.9 2.8 %copy-start.3 = (bf16[32,3584]{1,0:T(8,128)(2,1)S(1)}, bf16[32,3584]{1,0:T(8,128)(2,1)}, u32[]{:S(2)}) copy-start(bf16[32,3584]{1,0:T(8,128)(2,1)} %param.11) | copy-start | bytes 688132
  7.9 76.6 %all-gather.6.cloned.1.call-start = ((), (), s32[]{:S(2)}) async-start(), calls=%async_computation.3 | async-start | bytes 11010048 | tf_op jit(solution)/shard_map/all_gather | solution.py:20
  8.7 75.9 %all-gather.8.cloned.1.call-start = ((), (), s32[]{:S(2)}) async-start(), calls=%async_computation.4 | async-start | bytes 11010048 | tf_op jit(solution)/shard_map/all_gather | solution.py:21
  75.0 6.4 %copy-start.1 = (bf16[64,8,3584]{2,1,0:T(8,128)(2,1)S(1)}, bf16[64,8,3584]{2,1,0:T(8,128)(2,1)}, u32[]{:S(2)}) copy-start(bf16[64,8,3584]{2,1,0:T(8,128)(2,1)} %all_to_all.10) | copy-start | bytes 11010052
  75.0 7.5 %copy-start.8 = (bf16[2,3584,512]{2,1,0:T(8,128)(2,1)S(1)}, bf16[2,3584,512]{2,1,0:T(8,128)(2,1)}, u32[]{:S(2)}) copy-start(bf16[2,3584,512]{2,1,0:T(8,128)(2,1)} %all-gather.4.cloned.1.call-done) | copy-start | bytes 22020100
  108.0 7.7 %copy-start.6 = (f32[32,8]{0,1:T(8,128)S(1)}, f32[32,8]{0,1:T(8,128)}, u32[]{:S(2)}) copy-start(f32[32,8]{0,1:T(8,128)} %param.13) | copy-start | bytes 3076
  108.0 7.8 %copy-start.4 = (bf16[4,4096]{1,0:T(4,128)(2,1)S(1)}, bf16[4,4096]{1,0:T(4,128)(2,1)}, u32[]{:S(2)}) copy-start(bf16[4,4096]{1,0:T(4,128)(2,1)} %param.18) | copy-start | bytes 98308
  108.0 7.9 %copy-start.7 = (s32[4]{0:T(128)S(1)}, s32[4]{0:T(128)}, u32[]{:S(2)}) copy-start(s32[4]{0:T(128)} %param.21) | copy-start | bytes 52
  108.0 8.0 %copy-start.2 = (bf16[4,64,512]{2,1,0:T(8,128)(2,1)S(1)}, bf16[4,64,512]{2,1,0:T(8,128)(2,1)}, u32[]{:S(2)}) copy-start(bf16[4,64,512]{2,1,0:T(8,128)(2,1)} %param.17) | copy-start | bytes 786436
  108.0 56.1 %all-to-all-start.1 = ((bf16[64,8,3584]{2,1,0:T(8,128)(2,1)}), bf16[64,8,3584]{2,1,0:T(8,128)(2,1)}, u32[]{:S(2)}, u32[]{:S(2)}) async-start(bf16[64,8,3584]{2,1,0:T(8,128)(2,1)} %fusion.1), calls=%async_computation.1 | async-start | bytes 7340032 | tf_op jit(solution)/shard_map/all_to_all | solution.py:87
Sparse Core Ops, SparseCore 0:
  9.7 23.4 all-gather.3
  34.8 22.3 all-gather.5
  58.8 22.3 all-gather.7

commit v2 on v1

--- a/solution.py
+++ b/solution.py
@@ -2,6 +2,58 @@
 import jax.numpy as jnp
 from jax import lax
 from jax.sharding import PartitionSpec as P
+from jax.experimental import pallas as pl
+from jax.experimental.pallas import tpu as pltpu
+import functools
+
+MESH = pl.DeviceIdType.MESH
+
+def a2a_kernel(n, x_ref, o_ref, send_sems, recv_sems, local_sem):
+    me = lax.axis_index("dev")
+    core = lax.axis_index("role")
+    local = pltpu.make_async_copy(x_ref.at[me], o_ref.at[me], local_sem)
+    local.start()
+
+    def describe(k):
+        peer = lax.rem(me + k, n)
+        return pltpu.make_async_remote_copy(
+            src_ref=x_ref.at[peer],
+            dst_ref=o_ref.at[me],
+            send_sem=send_sems.at[k],
+            recv_sem=recv_sems.at[k],
+            device_id=(core, peer),
+            device_id_type=MESH,
+        )
+
+    def issue(k, carry):
+        describe(k).start()
+        return carry
+
+    lax.fori_loop(1, n, issue, 0)
+
+    def finish(k, carry):
+        describe(k).wait()
+        return carry
+
+    lax.fori_loop(1, n, finish, 0)
+    local.wait()
+
+
+def all_to_all_dev(x):
+    n = lax.axis_size("dev")
+    return pl.pallas_call(
+        functools.partial(a2a_kernel, n),
+        out_shape=jax.ShapeDtypeStruct(x.shape, x.dtype),
+        in_specs=[pl.BlockSpec(memory_space=pl.ANY)],
+        out_specs=pl.BlockSpec(memory_space=pl.ANY),
+        scratch_shapes=[
+            pltpu.SemaphoreType.DMA((n,)),
+            pltpu.SemaphoreType.DMA((n,)),
+            pltpu.SemaphoreType.DMA(()),
+        ],
+        compiler_params=pltpu.CompilerParams(has_side_effects=True),
+    )(x)
+
 
 score_scale = 192.0 ** (-0.5)
 
@@ -80,7 +132,7 @@
     )
     padded_rows = jnp.concatenate([moe_rows, jnp.zeros((1, width), jnp.bfloat16)], axis=0)
     outgoing = padded_rows[source_row].reshape(experts, capacity, width)
-    arrived = lax.all_to_all(outgoing, "dev", split_axis=0, concat_axis=0, tiled=True)
+    arrived = all_to_all_dev(outgoing)
     own_rows = arrived.reshape(experts * capacity, width)
     expert_sum = full_expert(own_rows, w_gate, w_up, w_down)
     finished = expert_sum.astype(jnp.bfloat16).reshape(experts, capacity, width)

time: 179 us -> 192 us (1.073)
  Pallas kernels: 0 us -> 71.4 us
  blocking collectives: 58.5 us -> 0 us
  starting transfers between devices: 7.8 us -> 10.7 us
    pallas_call x0 -> x1, Pallas kernels: none -> 71.4 us  [all_to_all_dev(): pl.pallas_call(functools.partial(a2a_kernel, n), out_shape=jax.ShapeDtype...]
    all_to_all x1 -> x0, blocking collectives: 58.5 us -> none  [per_device(): lax.all_to_all(outgoing, 'dev', split_axis=0, concat_axis=0, tiled=True)]
    all_to_all x1, starting transfers between devices: 7.69 us -> 10.6 us  [per_device(): lax.all_to_all(finished, 'dev', split_axis=0, concat_axis=0, tiled=True)]
  transfers between devices with their start and end apart: 4 -> 4, of which waited for: 1 -> 1; matrix products, arithmetic and copies ran while one was open for 17% -> 15% of each run, Pallas kernels for 0% -> 37%
where the time goes in v2:
time: 192 us
  Pallas kernels  71.4 us (37%)
  matrix products  45.5 us (24%)
  waiting for transfers between devices  34 us (18%)
  between operations  14 us (7%)
  local copies, waits for them, and re-layouts  13.5 us (7%)
  starting transfers between devices  10.7 us (6%)
  other arithmetic  3.01 us (2%)
    pallas_call x1, Pallas kernels, all_to_all_dev(): pl.pallas_call(functools.partial(a2a_kernel, n), out_shape=jax.ShapeDtype...  71.4 us
    all_to_all x1, waiting for transfers between devices, per_device(): lax.all_to_all(finished, 'dev', split_axis=0, concat_axis=0, tiled=True)  31.9 us
    dot_general x2, matrix products, full_expert(): lax.dot_general(hidden_units, down_both[half], (((1,), (1,)), ((), ())),...  23.4 us
    all_to_all x1, starting transfers between devices, per_device(): lax.all_to_all(finished, 'dev', split_axis=0, concat_axis=0, tiled=True)  10.6 us
    dot_general x2, matrix products, full_expert(): jnp.dot(rows, gate_both[half], preferred_element_type=jnp.float32)  7.39 us
    dot_general x1, matrix products, attend_row(): jnp.dot(probs, cache_lat, preferred_element_type=jnp.float32)  6.34 us
    gather x1, local copies, waits for them, and re-layouts, per_device(): flat_back[destination].reshape(tok_count, topk_count, width)  6.04 us
    dot_general x1, matrix products, attend_row(): lax.dot_general(query_lat, cache_lat, (((1,), (1,)), ((), ())), preferred...  6 us
  transfers between devices with their start and end apart: 4, of which 1 were waited for; matrix products, arithmetic and copies ran while one was open for 15% of the time, Pallas kernels for 37%

profile of v2, /device:TPU:0, one launch (start us, length us, event | category | flops | bytes accessed | tf_op | source)
XLA Modules:
  0.0 192.1 jit_solution(773849166107758450)
XLA Ops:
  7.2 0.0 copy-start
  7.2 0.0 all-gather.4.cloned.1.call-start
  7.2 0.7 all-gather.4.cloned.1.call-update
  7.9 0.0 copy-start.5
  7.9 0.0 copy-start.3
  7.9 0.0 all-gather.6.cloned.1.call-start
  8.0 0.7 all-gather.6.cloned.1.call-update
  8.7 0.0 all-gather.8.cloned.1.call-start
  8.7 0.7 all-gather.8.cloned.1.call-update
  9.4 0.0 copy-done.5
  9.4 0.1 copy.20
  9.5 0.1 eq.29
  9.6 0.1 eq.25
  9.7 0.1 copy.19
  9.8 0.1 mul.48
  9.9 0.6 reduce-window.6
  10.5 0.2 slice_reduce_fusion
  10.7 0.0 copy-done.3
  10.8 0.1 fusion.38
  10.9 1.4 scatter_custom_fusion
  12.3 4.3 %gather_fusion = bf16[512,3584]{1,0:T(8,128)(2,1)} fusion(bf16[33,3584]{1,0:T(8,128)(2,1)S(1)} %concatenate.3, s32[1024]{0:T(1024)S(1)} %pad_clamp_fusion.1), kind=kCustom, calls=%fused_computation | custom fusion | bytes 7342080 | tf_op jit(solution)/shard_map/gather | solution.py:134
  16.6 71.4 %shard_map.122 = bf16[64,8,3584]{2,1,0:T(8,128)(2,1)} custom-call(bf16[64,8,3584]{2,1,0:T(8,128)(2,1)} %bitcast.85), custom_call_target="tpu_custom_call" | custom-call | tf_op jit(solution)/shard_map/pallas_call | solution.py:44
  87.9 0.0 all-gather.4.cloned.1.call-done
  87.9 0.0 copy-start.1
  88.0 0.0 copy-start.8
  88.0 5.3 %fusion.3 = f32[512,512]{1,0:T(8,128)S(1)} fusion(bf16[2,3584,512]{2,1,0:T(8,128)(2,1)} %all-gather.4.cloned.1.call-done, bf16[64,8,3584]{2,1,0:T(8,128)(2,1)} %shard_map.122), kind=kOutput, calls=%fused_computation.10 | convolution fusion | flops 1879048192 | bytes 8388608 | tf_op jit(solution)/shard_map/dot_general | solution.py:76
  93.3 0.0 copy-done.1
  93.3 1.0 copy-done.8
  94.3 2.0 %fusion.6 = f32[512,512]{1,0:T(8,128)S(1)} fusion(bf16[2,3584,512]{2,1,0:T(8,128)(2,1)S(1)} %copy-done.8, bf16[64,8,3584]{2,1,0:T(8,128)(2,1)S(1)} %copy-done.1), kind=kOutput, calls=%fused_computation.16 | convolution fusion | flops 1879048192 | bytes 8388608 | tf_op jit(solution)/shard_map/dot_general | solution.py:76
  96.4 0.0 all-gather.6.cloned.1.call-done
  96.4 0.0 all-gather.8.cloned.1.call-done
  96.4 11.2 %fusion.4 = f32[512,3584]{1,0:T(8,128)} fusion(bf16[2,3584,512]{2,1,0:T(8,128)(2,1)} %all-gather.8.cloned.1.call-done, bf16[2,3584,512]{2,1,0:T(8,128)(2,1)} %all-gather.6.cloned.1.call-done, bf16[64,8,3584]{2,1,0:T(8,128)(2,1)} %shard_map.122, f32[512,512]{1,0:T(8,128)S(1)} %fusion.6), kind=kOutput, calls=%fused_computation.12 | convolution fusion | flops 3759669248 | bytes 19398656 | tf_op jit(solution)/shard_map/dot_general | solution.py:79
  107.6 12.2 %fusion.1 = bf16[64,8,3584]{2,1,0:T(8,128)(2,1)} fusion(f32[512,3584]{1,0:T(8,128)} %fusion.4, bf16[2,3584,512]{2,1,0:T(8,128)(2,1)} %all-gather.8.cloned.1.call-done, bf16[2,3584,512]{2,1,0:T(8,128)(2,1)} %all-gather.6.cloned.1.call-done, bf16[64,8,3584]{2,1,0:T(8,128)(2,1)} %shard_map.122, f32[512,512]{1,0:T(8,128)S(1)} %fusion.3), kind=kOutput, calls=%fused_computation.5 | convolution fusion | flops 3763339264 | bytes 23068672 | tf_op jit(solution)/shard_map/dot_general | solution.py:79
  119.8 0.0 copy-start.6
  119.8 0.0 copy-start.4
  119.8 0.0 copy-start.7
  119.8 0.0 copy-start.2
  119.9 10.6 %all-to-all-start = ((bf16[64,8,3584]{2,1,0:T(8,128)(2,1)}), bf16[64,8,3584]{2,1,0:T(8,128)(2,1)}, u32[]{:S(2)}, u32[]{:S(2)}) async-start(bf16[64,8,3584]{2,1,0:T(8,128)(2,1)} %fusion.1), calls=%async_computation | async-start | bytes 7340032 | tf_op jit(solution)/shard_map/all_to_all | solution.py:139
  130.4 0.0 copy-done.6
  130.5 0.1 copy.23
  130.5 0.0 copy-done.4
  130.5 0.1 reshape.93
  130.7 0.0 copy-done.7
  130.7 0.1 iota_compare_fusion.2
  130.8 0.0 copy-done.2
  130.8 6.0 %fusion.45 = f32[4,64,2048]{2,1,0:T(8,128)S(1)} fusion(bf16[4,64,512]{2,1,0:T(8,128)(2,1)S(1)} %copy-done.2, bf16[4,2048,512]{2,1,0:T(8,128)(2,1)} %param.19), kind=kOutput, calls=%fused_computation.62 | convolution fusion | flops 536870912 | bytes 10747904 | tf_op jit(solution)/shard_map/vmap()/dot_general | solution.py:89
  136.8 0.0 copy-done
  136.8 2.3 %fusion.44 = (f32[4,64]{1,0:T(4,128)S(1)}, f32[4,64,2048]{2,1,0:T(8,128)}) fusion(pred[4,2048]{1,0:T(4,128)(4,1)S(1)} %iota_compare_fusion.2, f32[4,64,2048]{2,1,0:T(8,128)S(1)} %fusion.45, bf16[4,64,64]{2,1,0:T(8,128)(2,1)S(1)} %reshape.93, bf16[4,64,2048]{2,1,0:T(8,128)(2,1)S(1)} %copy-done), kind=kOutput, calls=%fused_computation.61 | convolution fusion | flops 70256640 | bytes 5284864 | tf_op jit(solution)/shard_map/vmap()/sub | solution.py:100
  139.1 6.3 %convolution_convert_fusion = bf16[4,64,512]{2,1,0:T(8,128)(2,1)} fusion(bf16[4,2048,512]{2,1,0:T(8,128)(2,1)} %param.19, f32[4,64,2048]{2,1,0:T(8,128)} %get-tuple-element.3, f32[4,64]{1,0:T(4,128)S(1)} %get-tuple-element.2), kind=kOutput, calls=%fused_computation.34 | convolution fusion | flops 538050560 | bytes 10748928 | tf_op jit(solution)/shard_map/vmap()/dot_general | solution.py:102
  145.5 31.9 %all-to-all-done = bf16[64,8,3584]{2,1,0:T(8,128)(2,1)} async-done(((bf16[64,8,3584]{2,1,0:T(8,128)(2,1)}), bf16[64,8,3584]{2,1,0:T(8,128)(2,1)}, u32[]{:S(2)}, u32[]{:S(2)}) %all-to-all-start) | async-done | bytes 3670048 | tf_op jit(solution)/shard_map/all_to_all | solution.py:139
  177.3 6.0 %gather_fusion.1 = bf16[256,3584]{1,0:T(8,128)(2,1)S(1)} fusion(bf16[512,3584]{1,0:T(8,128)(2,1)} %bitcast.12, s32[1024]{0:T(1024)S(1)} %pad_clamp_fusion), kind=kCustom, calls=%fused_computation.1 | custom fusion | bytes 3671040 | tf_op jit(solution)/shard_map/gather | solution.py:141
  183.4 2.1 %fusion.7 = bf16[32,3584]{1,0:T(8,128)(2,1)} fusion(bf16[256,3584]{1,0:T(8,128)(2,1)S(1)} %gather_fusion.1, f32[32,8]{1,0:T(8,128)S(1)} %copy.23), kind=kLoop, calls=%fused_computation.18 | loop fusion | flops 2637824 | bytes 2065408 | tf_op jit(solution)/shard_map/reduce_sum | solution.py:142
  (10 shorter events, 0.1 us)
Async XLA Ops:
  7.2 129.6 %copy-start = (bf16[4,64,2048]{2,1,0:T(8,128)(2,1)S(1)}, bf16[4,64,2048]{2,1,0:T(8,128)(2,1)}, u32[]{:S(2)}) copy-start(bf16[4,64,2048]{2,1,0:T(8,128)(2,1)} %param.20) | copy-start | bytes 3145732
  7.2 80.8 %all-gather.4.cloned.1.call-start = ((), (), s32[]{:S(2)}) async-start(), calls=%async_computation.1 | async-start | bytes 11010048 | tf_op jit(solution)/shard_map/all_gather | solution.py:71
  7.9 1.5 copy-start.5
  7.9 2.8 %copy-start.3 = (bf16[32,3584]{1,0:T(8,128)(2,1)S(1)}, bf16[32,3584]{1,0:T(8,128)(2,1)}, u32[]{:S(2)}) copy-start(bf16[32,3584]{1,0:T(8,128)(2,1)} %param.11) | copy-start | bytes 688132
  7.9 88.4 %all-gather.6.cloned.1.call-start = ((), (), s32[]{:S(2)}) async-start(), calls=%async_computation.2 | async-start | bytes 11010048 | tf_op jit(solution)/shard_map/all_gather | solution.py:72
  8.7 87.7 %all-gather.8.cloned.1.call-start = ((), (), s32[]{:S(2)}) async-start(), calls=%async_computation.3 | async-start | bytes 11010048 | tf_op jit(solution)/shard_map/all_gather | solution.py:73
  87.9 5.4 %copy-start.1 = (bf16[64,8,3584]{2,1,0:T(8,128)(2,1)S(1)}, bf16[64,8,3584]{2,1,0:T(8,128)(2,1)}, u32[]{:S(2)}) copy-start(bf16[64,8,3584]{2,1,0:T(8,128)(2,1)} %shard_map.122) | copy-start | bytes 11010052
  88.0 6.3 %copy-start.8 = (bf16[2,3584,512]{2,1,0:T(8,128)(2,1)S(1)}, bf16[2,3584,512]{2,1,0:T(8,128)(2,1)}, u32[]{:S(2)}) copy-start(bf16[2,3584,512]{2,1,0:T(8,128)(2,1)} %all-gather.4.cloned.1.call-done) | copy-start | bytes 22020100
  119.8 10.6 %copy-start.6 = (f32[32,8]{0,1:T(8,128)S(1)}, f32[32,8]{0,1:T(8,128)}, u32[]{:S(2)}) copy-start(f32[32,8]{0,1:T(8,128)} %param.13) | copy-start | bytes 3076
  119.8 10.7 %copy-start.4 = (bf16[4,4096]{1,0:T(4,128)(2,1)S(1)}, bf16[4,4096]{1,0:T(4,128)(2,1)}, u32[]{:S(2)}) copy-start(bf16[4,4096]{1,0:T(4,128)(2,1)} %param.18) | copy-start | bytes 98308
  119.8 10.8 %copy-start.7 = (s32[4]{0:T(128)S(1)}, s32[4]{0:T(128)}, u32[]{:S(2)}) copy-start(s32[4]{0:T(128)} %param.21) | copy-start | bytes 52
  119.8 10.9 %copy-start.2 = (bf16[4,64,512]{2,1,0:T(8,128)(2,1)S(1)}, bf16[4,64,512]{2,1,0:T(8,128)(2,1)}, u32[]{:S(2)}) copy-start(bf16[4,64,512]{2,1,0:T(8,128)(2,1)} %param.17) | copy-start | bytes 786436
  119.9 57.5 %all-to-all-start = ((bf16[64,8,3584]{2,1,0:T(8,128)(2,1)}), bf16[64,8,3584]{2,1,0:T(8,128)(2,1)}, u32[]{:S(2)}, u32[]{:S(2)}) async-start(bf16[64,8,3584]{2,1,0:T(8,128)(2,1)} %fusion.1), calls=%async_computation | async-start | bytes 7340032 | tf_op jit(solution)/shard_map/all_to_all | solution.py:139
Sparse Core Ops, SparseCore 0:
  9.7 23.4 all-gather.3
  34.8 22.3 all-gather.5
  58.8 22.3 all-gather.7

commit v3 on v2

--- a/solution.py
+++ b/solution.py
@@ -14,25 +14,28 @@
     local = pltpu.make_async_copy(x_ref.at[me], o_ref.at[me], local_sem)
     local.start()
 
-    def describe(k):
-        peer = lax.rem(me + k, n)
+    def offset_of(k):
+        return lax.rem((k - 1) * 2 + me, n - 1) + 1
+
+    def describe(offset):
+        peer = lax.rem(me + offset, n)
         return pltpu.make_async_remote_copy(
             src_ref=x_ref.at[peer],
             dst_ref=o_ref.at[me],
-            send_sem=send_sems.at[k],
-            recv_sem=recv_sems.at[k],
+            send_sem=send_sems.at[offset],
+            recv_sem=recv_sems.at[offset],
             device_id=(core, peer),
             device_id_type=MESH,
         )
 
     def issue(k, carry):
-        describe(k).start()
+        describe(offset_of(k)).start()
         return carry
 
     lax.fori_loop(1, n, issue, 0)
 
-    def finish(k, carry):
-        describe(k).wait()
+    def finish(offset, carry):
+        describe(offset).wait()
         return carry
 
     lax.fori_loop(1, n, finish, 0)

time: 192 us -> 200 us (1.042)
  starting transfers between devices: 10.7 us -> 23.7 us
  Pallas kernels: 71.4 us -> 66.7 us
    all_to_all x1, starting transfers between devices: 10.6 us -> 23.6 us  [per_device(): lax.all_to_all(finished, 'dev', split_axis=0, concat_axis=0, tiled=True)]
    pallas_call x1, Pallas kernels: 71.4 us -> 66.7 us  [all_to_all_dev(): pl.pallas_call(functools.partial(a2a_kernel, n), out_shape=jax.ShapeDtype...]
  transfers between devices with their start and end apart: 4 -> 4, of which waited for: 1 -> 1; matrix products, arithmetic and copies ran while one was open for 15% -> 15% of each run, Pallas kernels for 37% -> 33%
where the time goes in v3:
time: 200 us
  Pallas kernels  66.7 us (33%)
  matrix products  45.5 us (23%)
  waiting for transfers between devices  33.8 us (17%)
  starting transfers between devices  23.7 us (12%)
  between operations  14 us (7%)
  local copies, waits for them, and re-layouts  13.5 us (7%)
  other arithmetic  3.01 us (2%)
    pallas_call x1, Pallas kernels, all_to_all_dev(): pl.pallas_call(functools.partial(a2a_kernel, n), out_shape=jax.ShapeDtype...  66.7 us
    all_to_all x1, waiting for transfers between devices, per_device(): lax.all_to_all(finished, 'dev', split_axis=0, concat_axis=0, tiled=True)  31.6 us
    all_to_all x1, starting transfers between devices, per_device(): lax.all_to_all(finished, 'dev', split_axis=0, concat_axis=0, tiled=True)  23.6 us
    dot_general x2, matrix products, full_expert(): lax.dot_general(hidden_units, down_both[half], (((1,), (1,)), ((), ())),...  23.4 us
    dot_general x2, matrix products, full_expert(): jnp.dot(rows, gate_both[half], preferred_element_type=jnp.float32)  7.39 us
    dot_general x1, matrix products, attend_row(): jnp.dot(probs, cache_lat, preferred_element_type=jnp.float32)  6.34 us
    gather x1, local copies, waits for them, and re-layouts, per_device(): flat_back[destination].reshape(tok_count, topk_count, width)  6.04 us
    dot_general x1, matrix products, attend_row(): lax.dot_general(query_lat, cache_lat, (((1,), (1,)), ((), ())), preferred...  6 us
  transfers between devices with their start and end apart: 4, of which 1 were waited for; matrix products, arithmetic and copies ran while one was open for 15% of the time, Pallas kernels for 33%

profile of v3, /device:TPU:0, one launch (start us, length us, event | category | flops | bytes accessed | tf_op | source)
XLA Modules:
  0.0 200.2 jit_solution(7367063047076121291)
XLA Ops:
  7.2 0.0 copy-start
  7.2 0.0 all-gather.4.cloned.1.call-start
  7.2 0.7 all-gather.4.cloned.1.call-update
  7.9 0.0 copy-start.5
  7.9 0.0 copy-start.3
  7.9 0.0 all-gather.6.cloned.1.call-start
  8.0 0.7 all-gather.6.cloned.1.call-update
  8.7 0.0 all-gather.8.cloned.1.call-start
  8.7 0.7 all-gather.8.cloned.1.call-update
  9.4 0.0 copy-done.5
  9.4 0.1 copy.20
  9.5 0.1 eq.29
  9.6 0.1 eq.25
  9.7 0.1 copy.19
  9.8 0.1 mul.48
  9.9 0.6 reduce-window.6
  10.5 0.2 slice_reduce_fusion
  10.7 0.0 copy-done.3
  10.8 0.1 fusion.38
  10.9 1.4 scatter_custom_fusion
  12.3 4.3 %gather_fusion = bf16[512,3584]{1,0:T(8,128)(2,1)} fusion(bf16[33,3584]{1,0:T(8,128)(2,1)S(1)} %concatenate.3, s32[1024]{0:T(1024)S(1)} %pad_clamp_fusion.1), kind=kCustom, calls=%fused_computation | custom fusion | bytes 7342080 | tf_op jit(solution)/shard_map/gather | solution.py:137
  16.6 66.7 %shard_map.122 = bf16[64,8,3584]{2,1,0:T(8,128)(2,1)} custom-call(bf16[64,8,3584]{2,1,0:T(8,128)(2,1)} %bitcast.85), custom_call_target="tpu_custom_call" | custom-call | tf_op jit(solution)/shard_map/pallas_call | solution.py:47
  83.3 0.0 all-gather.4.cloned.1.call-done
  83.3 0.0 copy-start.1
  83.3 0.0 copy-start.8
  83.3 5.3 %fusion.3 = f32[512,512]{1,0:T(8,128)S(1)} fusion(bf16[2,3584,512]{2,1,0:T(8,128)(2,1)} %all-gather.4.cloned.1.call-done, bf16[64,8,3584]{2,1,0:T(8,128)(2,1)} %shard_map.122), kind=kOutput, calls=%fused_computation.10 | convolution fusion | flops 1879048192 | bytes 8388608 | tf_op jit(solution)/shard_map/dot_general | solution.py:79
  88.7 0.0 copy-done.1
  88.7 1.0 copy-done.8
  89.7 2.0 %fusion.6 = f32[512,512]{1,0:T(8,128)S(1)} fusion(bf16[2,3584,512]{2,1,0:T(8,128)(2,1)S(1)} %copy-done.8, bf16[64,8,3584]{2,1,0:T(8,128)(2,1)S(1)} %copy-done.1), kind=kOutput, calls=%fused_computation.16 | convolution fusion | flops 1879048192 | bytes 8388608 | tf_op jit(solution)/shard_map/dot_general | solution.py:79
  91.7 0.0 all-gather.6.cloned.1.call-done
  91.7 0.0 all-gather.8.cloned.1.call-done
  91.8 11.2 %fusion.4 = f32[512,3584]{1,0:T(8,128)} fusion(bf16[2,3584,512]{2,1,0:T(8,128)(2,1)} %all-gather.8.cloned.1.call-done, bf16[2,3584,512]{2,1,0:T(8,128)(2,1)} %all-gather.6.cloned.1.call-done, bf16[64,8,3584]{2,1,0:T(8,128)(2,1)} %shard_map.122, f32[512,512]{1,0:T(8,128)S(1)} %fusion.6), kind=kOutput, calls=%fused_computation.12 | convolution fusion | flops 3759669248 | bytes 19398656 | tf_op jit(solution)/shard_map/dot_general | solution.py:82
  103.0 12.2 %fusion.1 = bf16[64,8,3584]{2,1,0:T(8,128)(2,1)} fusion(f32[512,3584]{1,0:T(8,128)} %fusion.4, bf16[2,3584,512]{2,1,0:T(8,128)(2,1)} %all-gather.8.cloned.1.call-done, bf16[2,3584,512]{2,1,0:T(8,128)(2,1)} %all-gather.6.cloned.1.call-done, bf16[64,8,3584]{2,1,0:T(8,128)(2,1)} %shard_map.122, f32[512,512]{1,0:T(8,128)S(1)} %fusion.3), kind=kOutput, calls=%fused_computation.5 | convolution fusion | flops 3763339264 | bytes 23068672 | tf_op jit(solution)/shard_map/dot_general | solution.py:82
  115.2 0.0 copy-start.6
  115.2 0.0 copy-start.4
  115.2 0.0 copy-start.7
  115.2 0.0 copy-start.2
  115.2 23.6 %all-to-all-start = ((bf16[64,8,3584]{2,1,0:T(8,128)(2,1)}), bf16[64,8,3584]{2,1,0:T(8,128)(2,1)}, u32[]{:S(2)}, u32[]{:S(2)}) async-start(bf16[64,8,3584]{2,1,0:T(8,128)(2,1)} %fusion.1), calls=%async_computation | async-start | bytes 7340032 | tf_op jit(solution)/shard_map/all_to_all | solution.py:142
  138.8 0.0 copy-done.6
  138.8 0.1 copy.23
  138.9 0.0 copy-done.4
  138.9 0.1 reshape.93
  139.0 0.0 copy-done.7
  139.0 0.1 iota_compare_fusion.2
  139.1 0.0 copy-done.2
  139.1 6.0 %fusion.45 = f32[4,64,2048]{2,1,0:T(8,128)S(1)} fusion(bf16[4,64,512]{2,1,0:T(8,128)(2,1)S(1)} %copy-done.2, bf16[4,2048,512]{2,1,0:T(8,128)(2,1)} %param.19), kind=kOutput, calls=%fused_computation.62 | convolution fusion | flops 536870912 | bytes 10747904 | tf_op jit(solution)/shard_map/vmap()/dot_general | solution.py:92
  145.1 0.0 copy-done
  145.1 2.3 %fusion.44 = (f32[4,64]{1,0:T(4,128)S(1)}, f32[4,64,2048]{2,1,0:T(8,128)}) fusion(pred[4,2048]{1,0:T(4,128)(4,1)S(1)} %iota_compare_fusion.2, f32[4,64,2048]{2,1,0:T(8,128)S(1)} %fusion.45, bf16[4,64,64]{2,1,0:T(8,128)(2,1)S(1)} %reshape.93, bf16[4,64,2048]{2,1,0:T(8,128)(2,1)S(1)} %copy-done), kind=kOutput, calls=%fused_computation.61 | convolution fusion | flops 70256640 | bytes 5284864 | tf_op jit(solution)/shard_map/vmap()/sub | solution.py:103
  147.5 6.3 %convolution_convert_fusion = bf16[4,64,512]{2,1,0:T(8,128)(2,1)} fusion(bf16[4,2048,512]{2,1,0:T(8,128)(2,1)} %param.19, f32[4,64,2048]{2,1,0:T(8,128)} %get-tuple-element.3, f32[4,64]{1,0:T(4,128)S(1)} %get-tuple-element.2), kind=kOutput, calls=%fused_computation.34 | convolution fusion | flops 538050560 | bytes 10748928 | tf_op jit(solution)/shard_map/vmap()/dot_general | solution.py:105
  153.8 31.6 %all-to-all-done = bf16[64,8,3584]{2,1,0:T(8,128)(2,1)} async-done(((bf16[64,8,3584]{2,1,0:T(8,128)(2,1)}), bf16[64,8,3584]{2,1,0:T(8,128)(2,1)}, u32[]{:S(2)}, u32[]{:S(2)}) %all-to-all-start) | async-done | bytes 3670048 | tf_op jit(solution)/shard_map/all_to_all | solution.py:142
  185.4 6.0 %gather_fusion.1 = bf16[256,3584]{1,0:T(8,128)(2,1)S(1)} fusion(bf16[512,3584]{1,0:T(8,128)(2,1)} %bitcast.12, s32[1024]{0:T(1024)S(1)} %pad_clamp_fusion), kind=kCustom, calls=%fused_computation.1 | custom fusion | bytes 3671040 | tf_op jit(solution)/shard_map/gather | solution.py:144
  191.5 2.1 %fusion.7 = bf16[32,3584]{1,0:T(8,128)(2,1)} fusion(bf16[256,3584]{1,0:T(8,128)(2,1)S(1)} %gather_fusion.1, f32[32,8]{1,0:T(8,128)S(1)} %copy.23), kind=kLoop, calls=%fused_computation.18 | loop fusion | flops 2637824 | bytes 2065408 | tf_op jit(solution)/shard_map/reduce_sum | solution.py:145
  (10 shorter events, 0.1 us)
Async XLA Ops:
  7.2 138.0 %copy-start = (bf16[4,64,2048]{2,1,0:T(8,128)(2,1)S(1)}, bf16[4,64,2048]{2,1,0:T(8,128)(2,1)}, u32[]{:S(2)}) copy-start(bf16[4,64,2048]{2,1,0:T(8,128)(2,1)} %param.20) | copy-start | bytes 3145732
  7.2 76.1 %all-gather.4.cloned.1.call-start = ((), (), s32[]{:S(2)}) async-start(), calls=%async_computation.1 | async-start | bytes 11010048 | tf_op jit(solution)/shard_map/all_gather | solution.py:74
  7.9 1.5 copy-start.5
  7.9 2.8 %copy-start.3 = (bf16[32,3584]{1,0:T(8,128)(2,1)S(1)}, bf16[32,3584]{1,0:T(8,128)(2,1)}, u32[]{:S(2)}) copy-start(bf16[32,3584]{1,0:T(8,128)(2,1)} %param.11) | copy-start | bytes 688132
  7.9 83.8 %all-gather.6.cloned.1.call-start = ((), (), s32[]{:S(2)}) async-start(), calls=%async_computation.2 | async-start | bytes 11010048 | tf_op jit(solution)/shard_map/all_gather | solution.py:75
  8.7 83.1 %all-gather.8.cloned.1.call-start = ((), (), s32[]{:S(2)}) async-start(), calls=%async_computation.3 | async-start | bytes 11010048 | tf_op jit(solution)/shard_map/all_gather | solution.py:76
  83.3 5.4 %copy-start.1 = (bf16[64,8,3584]{2,1,0:T(8,128)(2,1)S(1)}, bf16[64,8,3584]{2,1,0:T(8,128)(2,1)}, u32[]{:S(2)}) copy-start(bf16[64,8,3584]{2,1,0:T(8,128)(2,1)} %shard_map.122) | copy-start | bytes 11010052
  83.3 6.3 %copy-start.8 = (bf16[2,3584,512]{2,1,0:T(8,128)(2,1)S(1)}, bf16[2,3584,512]{2,1,0:T(8,128)(2,1)}, u32[]{:S(2)}) copy-start(bf16[2,3584,512]{2,1,0:T(8,128)(2,1)} %all-gather.4.cloned.1.call-done) | copy-start | bytes 22020100
  115.2 23.6 %copy-start.6 = (f32[32,8]{0,1:T(8,128)S(1)}, f32[32,8]{0,1:T(8,128)}, u32[]{:S(2)}) copy-start(f32[32,8]{0,1:T(8,128)} %param.13) | copy-start | bytes 3076
  115.2 23.7 %copy-start.4 = (bf16[4,4096]{1,0:T(4,128)(2,1)S(1)}, bf16[4,4096]{1,0:T(4,128)(2,1)}, u32[]{:S(2)}) copy-start(bf16[4,4096]{1,0:T(4,128)(2,1)} %param.18) | copy-start | bytes 98308
  115.2 23.8 %copy-start.7 = (s32[4]{0:T(128)S(1)}, s32[4]{0:T(128)}, u32[]{:S(2)}) copy-start(s32[4]{0:T(128)} %param.21) | copy-start | bytes 52
  115.2 23.9 %copy-start.2 = (bf16[4,64,512]{2,1,0:T(8,128)(2,1)S(1)}, bf16[4,64,512]{2,1,0:T(8,128)(2,1)}, u32[]{:S(2)}) copy-start(bf16[4,64,512]{2,1,0:T(8,128)(2,1)} %param.17) | copy-start | bytes 786436
  115.2 70.2 %all-to-all-start = ((bf16[64,8,3584]{2,1,0:T(8,128)(2,1)}), bf16[64,8,3584]{2,1,0:T(8,128)(2,1)}, u32[]{:S(2)}, u32[]{:S(2)}) async-start(bf16[64,8,3584]{2,1,0:T(8,128)(2,1)} %fusion.1), calls=%async_computation | async-start | bytes 7340032 | tf_op jit(solution)/shard_map/all_to_all | solution.py:142
Sparse Core Ops, SparseCore 0:
  9.7 23.4 all-gather.3
  34.8 22.3 all-gather.5
  58.8 22.3 all-gather.7

commit v4 on v1

--- a/solution.py
+++ b/solution.py
@@ -2,6 +2,70 @@
 import jax.numpy as jnp
 from jax import lax
 from jax.sharding import PartitionSpec as P
+from jax.experimental import pallas as pl
+from jax.experimental.pallas import tpu as pltpu
+import functools
+
+def gate_up_kernel(x_ref, g_ref, u_ref, h_ref):
+    x = x_ref[...]
+    gate_part = jnp.dot(x, g_ref[0], preferred_element_type=jnp.float32)
+    up_part = jnp.dot(x, u_ref[0], preferred_element_type=jnp.float32)
+    h_ref[...] = (jax.nn.silu(gate_part) * up_part).astype(h_ref.dtype)
+
+
+def down_kernel(halves, h_ref, d_ref, o_ref):
+    width = d_ref.shape[2]
+    total = None
+    for half in range(halves):
+        term = lax.dot_general(
+            h_ref[:, half * width:(half + 1) * width],
+            d_ref[half],
+            (((1,), (1,)), ((), ())),
+            preferred_element_type=jnp.float32,
+        )
+        total = term if total is None else total + term
+    o_ref[...] = total.astype(o_ref.dtype)
+
+
+def expert_ffn(rows, gate_both, up_both, down_both, unit_tile=256, out_tile=512):
+    count, width = rows.shape
+    halves, _, units = gate_both.shape
+    steps = units // unit_tile
+    hidden = pl.pallas_call(
+        gate_up_kernel,
+        out_shape=jax.ShapeDtypeStruct((count, halves * units), jnp.bfloat16),
+        grid=(halves, steps),
+        in_specs=[
+            pl.BlockSpec((count, width), lambda c, j: (0, 0)),
+            pl.BlockSpec((1, width, unit_tile), lambda c, j: (c, 0, j)),
+            pl.BlockSpec((1, width, unit_tile), lambda c, j: (c, 0, j)),
+        ],
+        out_specs=pl.BlockSpec((count, unit_tile), lambda c, j: (0, c * steps + j)),
+        compiler_params=pltpu.CompilerParams(vmem_limit_bytes=48 * 1024 * 1024),
+        cost_estimate=pl.CostEstimate(
+            flops=4 * count * width * halves * units,
+            transcendentals=count * halves * units,
+            bytes_accessed=2 * (count * width + 2 * width * halves * units + count * halves * units),
+        ),
+    )(rows, gate_both, up_both)
+    out_steps = width // out_tile
+    return pl.pallas_call(
+        functools.partial(down_kernel, halves),
+        out_shape=jax.ShapeDtypeStruct((count, width), jnp.bfloat16),
+        grid=(out_steps,),
+        in_specs=[
+            pl.BlockSpec((count, halves * units), lambda j: (0, 0)),
+            pl.BlockSpec((halves, out_tile, units), lambda j: (0, j, 0)),
+        ],
+        out_specs=pl.BlockSpec((count, out_tile), lambda j: (0, j)),
+        compiler_params=pltpu.CompilerParams(vmem_limit_bytes=48 * 1024 * 1024),
+        cost_estimate=pl.CostEstimate(
+            flops=2 * count * width * halves * units,
+            transcendentals=0,
+            bytes_accessed=2 * (count * width + width * halves * units + count * halves * units),
+        ),
+    )(hidden, down_both)
+
 
 score_scale = 192.0 ** (-0.5)
 
@@ -19,16 +83,7 @@
     gate_both = lax.all_gather(w_gate[0], "role", axis=0)
     up_both = lax.all_gather(w_up[0], "role", axis=0)
     down_both = lax.all_gather(w_down[0], "role", axis=0)
-    total = None
-    for half in range(gate_both.shape[0]):
-        gate_part = jnp.dot(rows, gate_both[half], preferred_element_type=jnp.float32)
-        up_part = jnp.dot(rows, up_both[half], preferred_element_type=jnp.float32)
-        hidden_units = (jax.nn.silu(gate_part) * up_part).astype(jnp.bfloat16)
-        term = lax.dot_general(
-            hidden_units, down_both[half], (((1,), (1,)), ((), ())), preferred_element_type=jnp.float32
-        )
-        total = term if total is None else total + term
-    return total
+    return expert_ffn(rows, gate_both, up_both, down_both)
 
 
 def attend_row(query_lat, query_rope, cache_lat, cache_rope, length):
@@ -83,7 +138,7 @@
     arrived = lax.all_to_all(outgoing, "dev", split_axis=0, concat_axis=0, tiled=True)
     own_rows = arrived.reshape(experts * capacity, width)
     expert_sum = full_expert(own_rows, w_gate, w_up, w_down)
-    finished = expert_sum.astype(jnp.bfloat16).reshape(experts, capacity, width)
+    finished = expert_sum.reshape(experts, capacity, width)
     returned = lax.all_to_all(finished, "dev", split_axis=0, concat_axis=0, tiled=True)
     flat_back = returned.reshape(experts * capacity, width)
     picked = flat_back[destination].reshape(tok_count, topk_count, width).astype(jnp.float32)

time: 179 us -> 167 us (0.933)
  matrix products: 46.5 us -> 14.7 us
  Pallas kernels: 0 us -> 18.5 us
  local copies, waits for them, and re-layouts: 13.6 us -> 17.1 us
    dot_general x4 -> x0, matrix products: 31.8 us -> none  [the longest x2 23.3 us: full_expert(): lax.dot_general(hidden_units, down_both[half], (((1,), (1,)), ((), ())),...]
    pallas_call x0 -> x2, Pallas kernels: none -> 18.5 us  [the longest x1 10.5 us: expert_ffn(): pl.pallas_call(gate_up_kernel, out_shape=jax.ShapeDtypeStruct((count, hal...]
    unnamed x20, local copies, waits for them, and re-layouts: 1.2 us -> 4.74 us
  transfers between devices with their start and end apart: 4 -> 4, of which waited for: 1 -> 1; matrix products, arithmetic and copies ran while one was open for 17% -> 13% of each run, Pallas kernels for 0% -> 6%
where the time goes in v4:
time: 167 us
  blocking collectives  58.5 us (35%)
  waiting for transfers between devices  34.3 us (21%)
  Pallas kernels  18.5 us (11%)
  local copies, waits for them, and re-layouts  17.1 us (10%)
  matrix products  14.7 us (9%)
  between operations  13.9 us (8%)
  starting transfers between devices  6.62 us (4%)
  other arithmetic  3.01 us (2%)
    all_to_all x1, blocking collectives, per_device(): lax.all_to_all(outgoing, 'dev', split_axis=0, concat_axis=0, tiled=True)  58.5 us
    all_to_all x1, waiting for transfers between devices, per_device(): lax.all_to_all(finished, 'dev', split_axis=0, concat_axis=0, tiled=True)  32.3 us
    pallas_call x1, Pallas kernels, expert_ffn(): pl.pallas_call(gate_up_kernel, out_shape=jax.ShapeDtypeStruct((count, hal...  10.5 us
    pallas_call x1, Pallas kernels, expert_ffn(): pl.pallas_call(functools.partial(down_kernel, halves), out_shape=jax.Shap...  8.06 us
    all_to_all x1, starting transfers between devices, per_device(): lax.all_to_all(finished, 'dev', split_axis=0, concat_axis=0, tiled=True)  6.51 us
    dot_general x1, matrix products, attend_row(): jnp.dot(probs, cache_lat, preferred_element_type=jnp.float32)  6.34 us
    gather x1, local copies, waits for them, and re-layouts, per_device(): flat_back[destination].reshape(tok_count, topk_count, width)  6.04 us
    dot_general x1, matrix products, attend_row(): lax.dot_general(query_lat, cache_lat, (((1,), (1,)), ((), ())), preferred...  6 us
  transfers between devices with their start and end apart: 4, of which 1 were waited for; matrix products, arithmetic and copies ran while one was open for 13% of the time, Pallas kernels for 6%

profile of v4, /device:TPU:0, one launch (start us, length us, event | category | flops | bytes accessed | tf_op | source)
XLA Modules:
  0.0 166.8 jit_solution(16053515946701879186)
XLA Ops:
  7.2 0.0 copy-start
  7.2 0.0 all-gather.4.cloned.1.call-start
  7.2 0.7 all-gather.4.cloned.1.call-update
  7.9 0.0 all-gather.6.cloned.1.call-start
  8.0 0.7 all-gather.6.cloned.1.call-update
  8.7 0.0 copy-start.6
  8.7 0.0 copy-start.4
  8.7 0.0 all-gather.8.cloned.1.call-start
  8.7 0.7 all-gather.8.cloned.1.call-update
  9.4 0.0 copy-done.6
  9.4 0.1 copy.20
  9.5 0.1 eq.29
  9.6 0.1 eq.25
  9.7 0.6 reduce-window.6
  10.3 0.2 slice_reduce_fusion
  10.5 0.1 copy.19
  10.6 0.1 mul.35
  10.7 0.0 copy-done.4
  10.8 0.1 fusion.10
  10.9 1.4 scatter_custom_fusion
  12.3 4.3 %gather_fusion = bf16[512,3584]{1,0:T(8,128)(2,1)} fusion(bf16[33,3584]{1,0:T(8,128)(2,1)S(1)} %concatenate.3, s32[1024]{0:T(1024)S(1)} %pad_clamp_fusion.1), kind=kCustom, calls=%fused_computation | custom fusion | bytes 7342080 | tf_op jit(solution)/shard_map/gather | solution.py:137
  16.6 58.5 %all_to_all.10 = bf16[64,8,3584]{2,1,0:T(8,128)(2,1)} all-to-all(bf16[64,8,3584]{2,1,0:T(8,128)(2,1)} %bitcast.35), channel_id=1, replica_groups=mesh['role'=2,'dev'=64] {'dev'}, dimensions={0} | all-to-all | bytes 7340032 | tf_op jit(solution)/shard_map/all_to_all | solution.py:138
  75.1 0.0 all-gather.4.cloned.1.call-done.g_ref
  75.1 0.0 all-gather.6.cloned.1.call-done.u_ref
  75.1 0.0 copy-start.2
  75.1 2.7 %copy-done.2 = bf16[64,8,3584]{2,1,0:T(8,128)(2,1)S(1)} copy-done((bf16[64,8,3584]{2,1,0:T(8,128)(2,1)S(1)}, bf16[64,8,3584]{2,1,0:T(8,128)(2,1)}, u32[]{:S(2)}) %copy-start.2) | copy-done | bytes 3670040
  77.8 10.5 %shard_map.122.h_ref = bf16[512,1024]{1,0:T(8,128)(2,1)S(1)} custom-call(bf16[512,3584]{1,0:T(8,128)(2,1)S(1)} %bitcast.34, bf16[2,3584,512]{2,1,0:T(8,128)(2,1)} %all-gather.4.cloned.1.call-done.g_ref, bf16[2,3584,512]{2,1,0:T(8,128)(2,1)} %all-gather.6.cloned.1.call-done.u_ref), custom_call_target="tpu_custom_call" | custom-call | flops 7516192768 | bytes 19398656 | tf_op jit(solution)/shard_map/pallas_call | solution.py:34
  88.3 0.0 all-gather.8.cloned.1.call-done.d_ref
  88.3 8.1 %shard_map.123 = bf16[512,3584]{1,0:T(8,128)(2,1)S(1)} custom-call(bf16[512,1024]{1,0:T(8,128)(2,1)S(1)} %shard_map.122.h_ref, bf16[2,3584,512]{2,1,0:T(8,128)(2,1)} %all-gather.8.cloned.1.call-done.d_ref), custom_call_target="tpu_custom_call" | custom-call | flops 3758096384 | bytes 12058624 | tf_op jit(solution)/shard_map/pallas_call | solution.py:52
  96.4 0.0 copy-start.1
  96.4 1.8 %copy-done.1 = bf16[512,3584]{1,0:T(8,128)(2,1)} copy-done((bf16[512,3584]{1,0:T(8,128)(2,1)}, bf16[512,3584]{1,0:T(8,128)(2,1)S(1)}, u32[]{:S(2)}) %copy-start.1) | copy-done | bytes 3670040
  98.2 0.0 copy-start.7
  98.2 0.0 copy-start.5
  98.2 0.0 copy-start.8
  98.2 0.0 copy-start.3
  98.2 6.5 %all-to-all-start.1 = ((bf16[64,8,3584]{2,1,0:T(8,128)(2,1)}), bf16[64,8,3584]{2,1,0:T(8,128)(2,1)}, u32[]{:S(2)}, u32[]{:S(2)}) async-start(bf16[64,8,3584]{2,1,0:T(8,128)(2,1)} %bitcast.33), calls=%async_computation.1 | async-start | bytes 7340032 | tf_op jit(solution)/shard_map/all_to_all | solution.py:142
  104.7 0.0 copy-done.7
  104.7 0.1 copy.23
  104.8 0.0 copy-done.5
  104.8 0.1 reshape.93
  105.0 0.0 copy-done.8
  105.0 0.1 iota_compare_fusion.2
  105.0 0.0 copy-done.3
  105.1 6.0 %fusion.15 = f32[4,64,2048]{2,1,0:T(8,128)S(1)} fusion(bf16[4,64,512]{2,1,0:T(8,128)(2,1)S(1)} %copy-done.3, bf16[4,2048,512]{2,1,0:T(8,128)(2,1)} %param.19), kind=kOutput, calls=%fused_computation.37 | convolution fusion | flops 536870912 | bytes 10747904 | tf_op jit(solution)/shard_map/vmap()/dot_general | solution.py:92
  111.1 0.0 copy-done
  111.1 2.4 %fusion.14 = (f32[4,64]{1,0:T(4,128)S(1)}, f32[4,64,2048]{2,1,0:T(8,128)}) fusion(pred[4,2048]{1,0:T(4,128)(4,1)S(1)} %iota_compare_fusion.2, f32[4,64,2048]{2,1,0:T(8,128)S(1)} %fusion.15, bf16[4,64,64]{2,1,0:T(8,128)(2,1)S(1)} %reshape.93, bf16[4,64,2048]{2,1,0:T(8,128)(2,1)S(1)} %copy-done), kind=kOutput, calls=%fused_computation.36 | convolution fusion | flops 70256640 | bytes 5284864 | tf_op jit(solution)/shard_map/vmap()/sub | solution.py:103
  113.4 6.3 %convolution_convert_fusion = bf16[4,64,512]{2,1,0:T(8,128)(2,1)} fusion(bf16[4,2048,512]{2,1,0:T(8,128)(2,1)} %param.19, f32[4,64,2048]{2,1,0:T(8,128)} %get-tuple-element.3, f32[4,64]{1,0:T(4,128)S(1)} %get-tuple-element.2), kind=kOutput, calls=%fused_computation.13 | convolution fusion | flops 538050560 | bytes 10748928 | tf_op jit(solution)/shard_map/vmap()/dot_general | solution.py:105
  119.8 32.3 %all-to-all-done.1 = bf16[64,8,3584]{2,1,0:T(8,128)(2,1)} async-done(((bf16[64,8,3584]{2,1,0:T(8,128)(2,1)}), bf16[64,8,3584]{2,1,0:T(8,128)(2,1)}, u32[]{:S(2)}, u32[]{:S(2)}) %all-to-all-start.1) | async-done | bytes 3670048 | tf_op jit(solution)/shard_map/all_to_all | solution.py:142
  152.0 6.0 %gather_fusion.1 = bf16[256,3584]{1,0:T(8,128)(2,1)S(1)} fusion(bf16[512,3584]{1,0:T(8,128)(2,1)} %bitcast.6, s32[1024]{0:T(1024)S(1)} %pad_clamp_fusion), kind=kCustom, calls=%fused_computation.1 | custom fusion | bytes 3671040 | tf_op jit(solution)/shard_map/gather | solution.py:144
  158.1 2.1 %fusion.1 = bf16[32,3584]{1,0:T(8,128)(2,1)} fusion(bf16[256,3584]{1,0:T(8,128)(2,1)S(1)} %gather_fusion.1, f32[32,8]{1,0:T(8,128)S(1)} %copy.23), kind=kLoop, calls=%fused_computation.5 | loop fusion | flops 2637824 | bytes 2065408 | tf_op jit(solution)/shard_map/reduce_sum | solution.py:145
  (10 shorter events, 0.1 us)
Async XLA Ops:
  7.2 103.9 %copy-start = (bf16[4,64,2048]{2,1,0:T(8,128)(2,1)S(1)}, bf16[4,64,2048]{2,1,0:T(8,128)(2,1)}, u32[]{:S(2)}) copy-start(bf16[4,64,2048]{2,1,0:T(8,128)(2,1)} %param.20) | copy-start | bytes 3145732
  7.2 67.9 %all-gather.4.cloned.1.call-start = ((), (), s32[]{:S(2)}) async-start(), calls=%async_computation.2 | async-start | bytes 11010048 | tf_op jit(solution)/shard_map/all_gather | solution.py:83
  7.9 67.1 %all-gather.6.cloned.1.call-start = ((), (), s32[]{:S(2)}) async-start(), calls=%async_computation.3 | async-start | bytes 11010048 | tf_op jit(solution)/shard_map/all_gather | solution.py:84
  8.7 0.8 copy-start.6
  8.7 2.1 %copy-start.4 = (bf16[32,3584]{1,0:T(8,128)(2,1)S(1)}, bf16[32,3584]{1,0:T(8,128)(2,1)}, u32[]{:S(2)}) copy-start(bf16[32,3584]{1,0:T(8,128)(2,1)} %param.11) | copy-start | bytes 688132
  8.7 79.6 %all-gather.8.cloned.1.call-start = ((), (), s32[]{:S(2)}) async-start(), calls=%async_computation.4 | async-start | bytes 11010048 | tf_op jit(solution)/shard_map/all_gather | solution.py:85
  75.1 2.7 %copy-start.2 = (bf16[64,8,3584]{2,1,0:T(8,128)(2,1)S(1)}, bf16[64,8,3584]{2,1,0:T(8,128)(2,1)}, u32[]{:S(2)}) copy-start(bf16[64,8,3584]{2,1,0:T(8,128)(2,1)} %all_to_all.10) | copy-start | bytes 11010052
  96.4 1.8 %copy-start.1 = (bf16[512,3584]{1,0:T(8,128)(2,1)}, bf16[512,3584]{1,0:T(8,128)(2,1)S(1)}, u32[]{:S(2)}) copy-start(bf16[512,3584]{1,0:T(8,128)(2,1)S(1)} %shard_map.123) | copy-start | bytes 11010052
  98.2 6.5 %copy-start.7 = (f32[32,8]{0,1:T(8,128)S(1)}, f32[32,8]{0,1:T(8,128)}, u32[]{:S(2)}) copy-start(f32[32,8]{0,1:T(8,128)} %param.13) | copy-start | bytes 3076
  98.2 6.6 %copy-start.5 = (bf16[4,4096]{1,0:T(4,128)(2,1)S(1)}, bf16[4,4096]{1,0:T(4,128)(2,1)}, u32[]{:S(2)}) copy-start(bf16[4,4096]{1,0:T(4,128)(2,1)} %param.18) | copy-start | bytes 98308
  98.2 6.7 %copy-start.8 = (s32[4]{0:T(128)S(1)}, s32[4]{0:T(128)}, u32[]{:S(2)}) copy-start(s32[4]{0:T(128)} %param.21) | copy-start | bytes 52
  98.2 6.8 %copy-start.3 = (bf16[4,64,512]{2,1,0:T(8,128)(2,1)S(1)}, bf16[4,64,512]{2,1,0:T(8,128)(2,1)}, u32[]{:S(2)}) copy-start(bf16[4,64,512]{2,1,0:T(8,128)(2,1)} %param.17) | copy-start | bytes 786436
  98.2 53.8 %all-to-all-start.1 = ((bf16[64,8,3584]{2,1,0:T(8,128)(2,1)}), bf16[64,8,3584]{2,1,0:T(8,128)(2,1)}, u32[]{:S(2)}, u32[]{:S(2)}) async-start(bf16[64,8,3584]{2,1,0:T(8,128)(2,1)} %bitcast.33), calls=%async_computation.1 | async-start | bytes 7340032 | tf_op jit(solution)/shard_map/all_to_all | solution.py:142
Sparse Core Ops, SparseCore 0:
  9.7 23.4 all-gather.3
  34.8 22.3 all-gather.5
  58.8 22.3 all-gather.7

commit v5 on v4

--- a/solution.py
+++ b/solution.py
@@ -125,23 +125,29 @@
     capacity = min(tok_count, 2 * tok_count * topk_count // experts)
     flat_ids = expert_ids.reshape(-1)
     pair_count = flat_ids.shape[0]
-    one_hot = (flat_ids[:, None] == jnp.arange(experts, dtype=jnp.int32)[None, :]).astype(jnp.int32)
-    earlier = jnp.cumsum(one_hot, axis=0) - one_hot
-    slot_index = jnp.sum(earlier * one_hot, axis=1)
+    slot_count = experts * capacity
+    one_hot = flat_ids[:, None] == jnp.arange(experts, dtype=jnp.int32)[None, :]
+    pair_iota = jnp.arange(pair_count, dtype=jnp.int32)
+    lower = (pair_iota[:, None] > pair_iota[None, :]).astype(jnp.bfloat16)
+    earlier = jnp.dot(lower, one_hot.astype(jnp.bfloat16), preferred_element_type=jnp.float32)
+    slot_index = jnp.sum(jnp.where(one_hot, earlier, 0.0), axis=1).astype(jnp.int32)
     destination = flat_ids * capacity + slot_index
-    source_row = jnp.full((experts * capacity,), tok_count, jnp.int32)
-    source_row = source_row.at[destination].set(
-        jnp.arange(pair_count, dtype=jnp.int32) // topk_count
-    )
-    padded_rows = jnp.concatenate([moe_rows, jnp.zeros((1, width), jnp.bfloat16)], axis=0)
-    outgoing = padded_rows[source_row].reshape(experts, capacity, width)
+    slot_iota = jnp.arange(slot_count, dtype=jnp.int32)
+    picks = destination[:, None] == slot_iota[None, :]
+    dispatch = jnp.any(picks.reshape(tok_count, topk_count, slot_count), axis=1)
+    outgoing = lax.dot_general(
+        dispatch.astype(jnp.bfloat16), moe_rows, (((0,), (0,)), ((), ())),
+        preferred_element_type=jnp.float32,
+    ).astype(jnp.bfloat16).reshape(experts, capacity, width)
     arrived = lax.all_to_all(outgoing, "dev", split_axis=0, concat_axis=0, tiled=True)
     own_rows = arrived.reshape(experts * capacity, width)
     expert_sum = full_expert(own_rows, w_gate, w_up, w_down)
     finished = expert_sum.reshape(experts, capacity, width)
     returned = lax.all_to_all(finished, "dev", split_axis=0, concat_axis=0, tiled=True)
-    flat_back = returned.reshape(experts * capacity, width)
-    picked = flat_back[destination].reshape(tok_count, topk_count, width).astype(jnp.float32)
+    flat_back = returned.reshape(slot_count, width)
+    picked = jnp.dot(
+        picks.astype(jnp.bfloat16), flat_back, preferred_element_type=jnp.float32
+    ).reshape(tok_count, topk_count, width)
     moe_out = jnp.sum(picked * gate_weights[:, :, None], axis=1).astype(jnp.bfloat16)
     attended = jax.vmap(attend_row)(q_latent, q_rope, latent_cache, rope_cache, lengths)
     return (moe_out, attended)

time: 167 us -> 162 us (0.970)
  local copies, waits for them, and re-layouts: 17.1 us -> 4.95 us
  matrix products: 14.7 us -> 20.1 us
  other arithmetic: 3.01 us -> 0.33 us
  starting transfers between devices: 6.62 us -> 8.58 us
    gather x2 -> x0, local copies, waits for them, and re-layouts: 10.3 us -> none  [the longest x1 6.04 us: per_device(): flat_back[destination].reshape(tok_count, topk_count, width)]
    dot_general x0 -> x3, matrix products: none -> 5.44 us  [the longest x1 4.06 us: per_device(): jnp.dot(picks.astype(jnp.bfloat16), flat_back, preferred_element_type=jnp...]
    reduce_sum x2 -> x0, other arithmetic: 2.24 us -> none  [the longest x1 2.14 us: per_device(): jnp.sum(picked * gate_weights[:, :, None], axis=1).astype(jnp.bfloat16)]
    all_to_all x1, starting transfers between devices: 6.51 us -> 8.47 us  [per_device(): lax.all_to_all(finished, 'dev', split_axis=0, concat_axis=0, tiled=True)]
  transfers between devices with their start and end apart: 4 -> 4, of which waited for: 1 -> 1; matrix products, arithmetic and copies ran while one was open for 13% -> 10% of each run, Pallas kernels for 6% -> 7%
where the time goes in v5:
time: 162 us; the launch traced here: 161 us
  blocking collectives  58.3 us (36%)
  waiting for transfers between devices  35.9 us (22%)
  matrix products  20.1 us (12%)
  Pallas kernels  19.2 us (12%)
  between operations  13.9 us (9%)
  starting transfers between devices  8.58 us (5%)
  local copies, waits for them, and re-layouts  4.95 us (3%)
    all_to_all x1, blocking collectives, per_device(): lax.all_to_all(outgoing, 'dev', split_axis=0, concat_axis=0, tiled=True)  58.3 us
    all_to_all x1, waiting for transfers between devices, per_device(): lax.all_to_all(finished, 'dev', split_axis=0, concat_axis=0, tiled=True)  33.8 us
    pallas_call x1, Pallas kernels, expert_ffn(): pl.pallas_call(gate_up_kernel, out_shape=jax.ShapeDtypeStruct((count, hal...  11.2 us
    all_to_all x1, starting transfers between devices, per_device(): lax.all_to_all(finished, 'dev', split_axis=0, concat_axis=0, tiled=True)  8.47 us
    pallas_call x1, Pallas kernels, expert_ffn(): pl.pallas_call(functools.partial(down_kernel, halves), out_shape=jax.Shap...  8.05 us
    dot_general x1, matrix products, attend_row(): jnp.dot(probs, cache_lat, preferred_element_type=jnp.float32)  6.34 us
    dot_general x1, matrix products, attend_row(): lax.dot_general(query_lat, cache_lat, (((1,), (1,)), ((), ())), preferred...  6 us
    unnamed x20, local copies, waits for them, and re-layouts  4.66 us
  transfers between devices with their start and end apart: 4, of which 1 were waited for; matrix products, arithmetic and copies ran while one was open for 10% of the time, Pallas kernels for 7%

profile of v5, /device:TPU:0, one launch (start us, length us, event | category | flops | bytes accessed | tf_op | source)
XLA Modules:
  0.0 161.3 jit_solution(1887821603526834528)
XLA Ops:
  7.2 0.0 copy-start
  7.2 0.0 all-gather.4.cloned.1.call-start
  7.2 0.7 all-gather.4.cloned.1.call-update
  7.9 0.0 copy-start.6
  7.9 0.0 copy-start.4
  7.9 0.0 all-gather.6.cloned.1.call-start
  8.0 0.7 all-gather.6.cloned.1.call-update
  8.7 0.0 all-gather.8.cloned.1.call-start
  8.7 0.7 all-gather.8.cloned.1.call-update
  9.4 0.0 copy-done.6
  9.4 0.1 copy.22
  9.5 0.1 eq.51
  9.6 0.2 fusion.11
  9.8 0.1 convert_element_type.27
  9.9 0.2 fusion.15
  10.2 0.0 copy-done.4
  10.2 1.2 fusion.1
  11.3 58.3 %all_to_all.10 = bf16[64,8,3584]{2,1,0:T(8,128)(2,1)} all-to-all(bf16[64,8,3584]{2,1,0:T(8,128)(2,1)S(1)} %fusion.1), channel_id=1, replica_groups=mesh['role'=2,'dev'=64] {'dev'}, dimensions={0} | all-to-all | bytes 7340032 | tf_op jit(solution)/shard_map/all_to_all | solution.py:142
  69.6 0.0 all-gather.4.cloned.1.call-done.g_ref
  69.6 0.0 all-gather.6.cloned.1.call-done.u_ref
  69.6 0.0 copy-start.2
  69.6 2.6 %copy-done.2 = bf16[64,8,3584]{2,1,0:T(8,128)(2,1)S(1)} copy-done((bf16[64,8,3584]{2,1,0:T(8,128)(2,1)S(1)}, bf16[64,8,3584]{2,1,0:T(8,128)(2,1)}, u32[]{:S(2)}) %copy-start.2) | copy-done | bytes 3670040
  72.3 11.2 %shard_map.122.h_ref = bf16[512,1024]{1,0:T(8,128)(2,1)S(1)} custom-call(bf16[512,3584]{1,0:T(8,128)(2,1)S(1)} %bitcast.22, bf16[2,3584,512]{2,1,0:T(8,128)(2,1)} %all-gather.4.cloned.1.call-done.g_ref, bf16[2,3584,512]{2,1,0:T(8,128)(2,1)} %all-gather.6.cloned.1.call-done.u_ref), custom_call_target="tpu_custom_call" | custom-call | flops 7516192768 | bytes 19398656 | tf_op jit(solution)/shard_map/pallas_call | solution.py:34
  83.5 0.0 all-gather.8.cloned.1.call-done.d_ref
  83.5 8.1 %shard_map.123 = bf16[512,3584]{1,0:T(8,128)(2,1)S(1)} custom-call(bf16[512,1024]{1,0:T(8,128)(2,1)S(1)} %shard_map.122.h_ref, bf16[2,3584,512]{2,1,0:T(8,128)(2,1)} %all-gather.8.cloned.1.call-done.d_ref), custom_call_target="tpu_custom_call" | custom-call | flops 3758096384 | bytes 12058624 | tf_op jit(solution)/shard_map/pallas_call | solution.py:52
  91.6 0.0 copy-start.1
  91.6 1.8 %copy-done.1 = bf16[512,3584]{1,0:T(8,128)(2,1)} copy-done((bf16[512,3584]{1,0:T(8,128)(2,1)}, bf16[512,3584]{1,0:T(8,128)(2,1)S(1)}, u32[]{:S(2)}) %copy-start.1) | copy-done | bytes 3670040
  93.4 0.0 copy-start.7
  93.4 0.0 copy-start.5
  93.4 0.0 copy-start.8
  93.4 0.0 copy-start.3
  93.4 8.5 %all-to-all-start.1 = ((bf16[64,8,3584]{2,1,0:T(8,128)(2,1)}), bf16[64,8,3584]{2,1,0:T(8,128)(2,1)}, u32[]{:S(2)}, u32[]{:S(2)}) async-start(bf16[64,8,3584]{2,1,0:T(8,128)(2,1)} %bitcast.21), calls=%async_computation.1 | async-start | bytes 7340032 | tf_op jit(solution)/shard_map/all_to_all | solution.py:146
  101.9 0.0 copy-done.7
  101.9 0.1 copy.24
  102.0 0.0 copy-done.5
  102.0 0.1 reshape.88
  102.1 0.0 copy-done.8
  102.1 0.1 iota_compare_fusion.6
  102.2 0.0 copy-done.3
  102.2 6.0 %fusion.19 = f32[4,64,2048]{2,1,0:T(8,128)S(1)} fusion(bf16[4,64,512]{2,1,0:T(8,128)(2,1)S(1)} %copy-done.3, bf16[4,2048,512]{2,1,0:T(8,128)(2,1)} %param.19), kind=kOutput, calls=%fused_computation.28 | convolution fusion | flops 536870912 | bytes 10747904 | tf_op jit(solution)/shard_map/vmap()/dot_general | solution.py:92
  108.2 0.0 copy-done
  108.2 2.3 %fusion.18 = (f32[4,64]{1,0:T(4,128)S(1)}, f32[4,64,2048]{2,1,0:T(8,128)}) fusion(pred[4,2048]{1,0:T(4,128)(4,1)S(1)} %iota_compare_fusion.6, f32[4,64,2048]{2,1,0:T(8,128)S(1)} %fusion.19, bf16[4,64,64]{2,1,0:T(8,128)(2,1)S(1)} %reshape.88, bf16[4,64,2048]{2,1,0:T(8,128)(2,1)S(1)} %copy-done), kind=kOutput, calls=%fused_computation.27 | convolution fusion | flops 70256640 | bytes 5284864 | tf_op jit(solution)/shard_map/vmap()/sub | solution.py:103
  110.6 6.3 %convolution_convert_fusion.1 = bf16[4,64,512]{2,1,0:T(8,128)(2,1)} fusion(bf16[4,2048,512]{2,1,0:T(8,128)(2,1)} %param.19, f32[4,64,2048]{2,1,0:T(8,128)} %get-tuple-element.3, f32[4,64]{1,0:T(4,128)S(1)} %get-tuple-element.2), kind=kOutput, calls=%fused_computation.13 | convolution fusion | flops 538050560 | bytes 10748928 | tf_op jit(solution)/shard_map/vmap()/dot_general | solution.py:105
  116.9 33.8 %all-to-all-done.1 = bf16[64,8,3584]{2,1,0:T(8,128)(2,1)} async-done(((bf16[64,8,3584]{2,1,0:T(8,128)(2,1)}), bf16[64,8,3584]{2,1,0:T(8,128)(2,1)}, u32[]{:S(2)}, u32[]{:S(2)}) %all-to-all-start.1) | async-done | bytes 3670048 | tf_op jit(solution)/shard_map/all_to_all | solution.py:146
  150.7 4.1 %fusion.8 = bf16[32,3584]{1,0:T(8,128)(2,1)} fusion(f32[32,8]{1,0:T(8,128)S(1)} %copy.24, bf16[64,8,3584]{2,1,0:T(8,128)(2,1)} %all-to-all-done.1, s32[32,8]{1,0:T(8,128)S(1)} %multiply_add_fusion), kind=kOutput, calls=%fused_computation.12 | convolution fusion | flops 941375488 | bytes 3901440 | tf_op jit(solution)/shard_map/dot_general | solution.py:148
  (2 shorter events, 0.0 us)
Async XLA Ops:
  7.2 101.0 %copy-start = (bf16[4,64,2048]{2,1,0:T(8,128)(2,1)S(1)}, bf16[4,64,2048]{2,1,0:T(8,128)(2,1)}, u32[]{:S(2)}) copy-start(bf16[4,64,2048]{2,1,0:T(8,128)(2,1)} %param.20) | copy-start | bytes 3145732
  7.2 62.4 %all-gather.4.cloned.1.call-start = ((), (), s32[]{:S(2)}) async-start(), calls=%async_computation.2 | async-start | bytes 11010048 | tf_op jit(solution)/shard_map/all_gather | solution.py:83
  7.9 1.5 copy-start.6
  7.9 2.2 %copy-start.4 = (bf16[32,3584]{1,0:T(8,128)(2,1)S(1)}, bf16[32,3584]{1,0:T(8,128)(2,1)}, u32[]{:S(2)}) copy-start(bf16[32,3584]{1,0:T(8,128)(2,1)} %param.11) | copy-start | bytes 688132
  7.9 61.7 %all-gather.6.cloned.1.call-start = ((), (), s32[]{:S(2)}) async-start(), calls=%async_computation.3 | async-start | bytes 11010048 | tf_op jit(solution)/shard_map/all_gather | solution.py:84
  8.7 74.8 %all-gather.8.cloned.1.call-start = ((), (), s32[]{:S(2)}) async-start(), calls=%async_computation.4 | async-start | bytes 11010048 | tf_op jit(solution)/shard_map/all_gather | solution.py:85
  69.6 2.7 %copy-start.2 = (bf16[64,8,3584]{2,1,0:T(8,128)(2,1)S(1)}, bf16[64,8,3584]{2,1,0:T(8,128)(2,1)}, u32[]{:S(2)}) copy-start(bf16[64,8,3584]{2,1,0:T(8,128)(2,1)} %all_to_all.10) | copy-start | bytes 11010052
  91.6 1.8 %copy-start.1 = (bf16[512,3584]{1,0:T(8,128)(2,1)}, bf16[512,3584]{1,0:T(8,128)(2,1)S(1)}, u32[]{:S(2)}) copy-start(bf16[512,3584]{1,0:T(8,128)(2,1)S(1)} %shard_map.123) | copy-start | bytes 11010052
  93.4 8.5 %copy-start.7 = (f32[32,8]{0,1:T(8,128)S(1)}, f32[32,8]{0,1:T(8,128)}, u32[]{:S(2)}) copy-start(f32[32,8]{0,1:T(8,128)} %param.13) | copy-start | bytes 3076
  93.4 8.6 %copy-start.5 = (bf16[4,4096]{1,0:T(4,128)(2,1)S(1)}, bf16[4,4096]{1,0:T(4,128)(2,1)}, u32[]{:S(2)}) copy-start(bf16[4,4096]{1,0:T(4,128)(2,1)} %param.18) | copy-start | bytes 98308
  93.4 8.7 %copy-start.8 = (s32[4]{0:T(128)S(1)}, s32[4]{0:T(128)}, u32[]{:S(2)}) copy-start(s32[4]{0:T(128)} %param.21) | copy-start | bytes 52
  93.4 8.8 %copy-start.3 = (bf16[4,64,512]{2,1,0:T(8,128)(2,1)S(1)}, bf16[4,64,512]{2,1,0:T(8,128)(2,1)}, u32[]{:S(2)}) copy-start(bf16[4,64,512]{2,1,0:T(8,128)(2,1)} %param.17) | copy-start | bytes 786436
  93.4 57.3 %all-to-all-start.1 = ((bf16[64,8,3584]{2,1,0:T(8,128)(2,1)}), bf16[64,8,3584]{2,1,0:T(8,128)(2,1)}, u32[]{:S(2)}, u32[]{:S(2)}) async-start(bf16[64,8,3584]{2,1,0:T(8,128)(2,1)} %bitcast.21), calls=%async_computation.1 | async-start | bytes 7340032 | tf_op jit(solution)/shard_map/all_to_all | solution.py:146
Sparse Core Ops, SparseCore 0:
  9.7 23.4 all-gather.3
  34.8 22.3 all-gather.5
  58.8 22.3 all-gather.7

commit v6 on v5

--- a/solution.py
+++ b/solution.py
@@ -8,82 +8,79 @@
 
 def gate_up_kernel(x_ref, g_ref, u_ref, h_ref):
     x = x_ref[...]
-    gate_part = jnp.dot(x, g_ref[0], preferred_element_type=jnp.float32)
-    up_part = jnp.dot(x, u_ref[0], preferred_element_type=jnp.float32)
+    gate_part = jnp.dot(x, g_ref[...], preferred_element_type=jnp.float32)
+    up_part = jnp.dot(x, u_ref[...], preferred_element_type=jnp.float32)
     h_ref[...] = (jax.nn.silu(gate_part) * up_part).astype(h_ref.dtype)
 
 
-def down_kernel(halves, h_ref, d_ref, o_ref):
-    width = d_ref.shape[2]
+def down_kernel(h0_ref, h1_ref, d0_ref, d1_ref, o_ref):
     total = None
-    for half in range(halves):
+    for h_ref, d_ref in ((h0_ref, d0_ref), (h1_ref, d1_ref)):
         term = lax.dot_general(
-            h_ref[:, half * width:(half + 1) * width],
-            d_ref[half],
-            (((1,), (1,)), ((), ())),
-            preferred_element_type=jnp.float32,
+            h_ref[...], d_ref[...], (((1,), (1,)), ((), ())), preferred_element_type=jnp.float32
         )
         total = term if total is None else total + term
     o_ref[...] = total.astype(o_ref.dtype)
 
 
-def expert_ffn(rows, gate_both, up_both, down_both, unit_tile=256, out_tile=512):
+def gate_up(rows, gate_matrix, up_matrix, unit_tile=256):
     count, width = rows.shape
-    halves, _, units = gate_both.shape
-    steps = units // unit_tile
-    hidden = pl.pallas_call(
+    units = gate_matrix.shape[1]
+    return pl.pallas_call(
         gate_up_kernel,
-        out_shape=jax.ShapeDtypeStruct((count, halves * units), jnp.bfloat16),
-        grid=(halves, steps),
+        out_shape=jax.ShapeDtypeStruct((count, units), jnp.bfloat16),
+        grid=(units // unit_tile,),
         in_specs=[
-            pl.BlockSpec((count, width), lambda c, j: (0, 0)),
-            pl.BlockSpec((1, width, unit_tile), lambda c, j: (c, 0, j)),
-            pl.BlockSpec((1, width, unit_tile), lambda c, j: (c, 0, j)),
+            pl.BlockSpec((count, width), lambda j: (0, 0)),
+            pl.BlockSpec((width, unit_tile), lambda j: (0, j)),
+            pl.BlockSpec((width, unit_tile), lambda j: (0, j)),
         ],
-        out_specs=pl.BlockSpec((count, unit_tile), lambda c, j: (0, c * steps + j)),
+        out_specs=pl.BlockSpec((count, unit_tile), lambda j: (0, j)),
         compiler_params=pltpu.CompilerParams(vmem_limit_bytes=48 * 1024 * 1024),
         cost_estimate=pl.CostEstimate(
-            flops=4 * count * width * halves * units,
-            transcendentals=count * halves * units,
-            bytes_accessed=2 * (count * width + 2 * width * halves * units + count * halves * units),
+            flops=4 * count * width * units,
+            transcendentals=count * units,
+            bytes_accessed=2 * (count * width + 2 * width * units + count * units),
         ),
-    )(rows, gate_both, up_both)
-    out_steps = width // out_tile
+    )(rows, gate_matrix, up_matrix)
+
+
+def down(h0, h1, d0, d1, out_tile=512):
+    count, units = h0.shape
+    width = d0.shape[0]
     return pl.pallas_call(
-        functools.partial(down_kernel, halves),
+        down_kernel,
         out_shape=jax.ShapeDtypeStruct((count, width), jnp.bfloat16),
-        grid=(out_steps,),
+        grid=(width // out_tile,),
         in_specs=[
-            pl.BlockSpec((count, halves * units), lambda j: (0, 0)),
-            pl.BlockSpec((halves, out_tile, units), lambda j: (0, j, 0)),
+            pl.BlockSpec((count, units), lambda j: (0, 0)),
+            pl.BlockSpec((count, units), lambda j: (0, 0)),
+            pl.BlockSpec((out_tile, units), lambda j: (j, 0)),
+            pl.BlockSpec((out_tile, units), lambda j: (j, 0)),
         ],
         out_specs=pl.BlockSpec((count, out_tile), lambda j: (0, j)),
         compiler_params=pltpu.CompilerParams(vmem_limit_bytes=48 * 1024 * 1024),
         cost_estimate=pl.CostEstimate(
-            flops=2 * count * width * halves * units,
+            flops=4 * count * width * units,
             transcendentals=0,
-            bytes_accessed=2 * (count * width + width * halves * units + count * halves * units),
+            bytes_accessed=2 * (count * width + 2 * width * units + 2 * count * units),
         ),
-    )(hidden, down_both)
+    )(h0, h1, d0, d1)
+
+
+def other_half(w):
+    return lax.ppermute(w, "role", [(0, 1), (1, 0)])
+
+
+def full_expert(rows, w_gate, w_up, w_down):
+    gate_own, up_own, down_own = w_gate[0], w_up[0], w_down[0]
+    gate_other, up_other, down_other = other_half(gate_own), other_half(up_own), other_half(down_own)
+    h0 = gate_up(rows, gate_own, up_own)
+    h1 = gate_up(rows, gate_other, up_other)
+    return down(h0, h1, down_own, down_other)
 
 
 score_scale = 192.0 ** (-0.5)
-
-
-def expert_block(chosen, gate_matrix, up_matrix, down_matrix):
-    gate_part = jnp.dot(chosen, gate_matrix, preferred_element_type=jnp.float32)
-    up_part = jnp.dot(chosen, up_matrix, preferred_element_type=jnp.float32)
-    hidden_units = (jax.nn.silu(gate_part) * up_part).astype(jnp.bfloat16)
-    return lax.dot_general(
-        hidden_units, down_matrix, (((1,), (1,)), ((), ())), preferred_element_type=jnp.float32
-    )
-
-
-def full_expert(rows, w_gate, w_up, w_down):
-    gate_both = lax.all_gather(w_gate[0], "role", axis=0)
-    up_both = lax.all_gather(w_up[0], "role", axis=0)
-    down_both = lax.all_gather(w_down[0], "role", axis=0)
-    return expert_ffn(rows, gate_both, up_both, down_both)
 
 
 def attend_row(query_lat, query_rope, cache_lat, cache_rope, length):

time: 162 us -> 151 us (0.932)
  blocking collectives: 58.3 us -> 0 us
  waiting for transfers between devices: 35.9 us -> 80.3 us
  between operations: 13.9 us -> 0.79 us
  starting transfers between devices: 8.58 us -> 20.8 us
  Pallas kernels: 19.2 us -> 22.6 us
  matrix products: 20.1 us -> 22.9 us
  local copies, waits for them, and re-layouts: 4.95 us -> 3.06 us
    all_to_all x1 -> x0, blocking collectives: 58.3 us -> none  [per_device(): lax.all_to_all(outgoing, 'dev', split_axis=0, concat_axis=0, tiled=True)]
    all_to_all x0 -> x1, waiting for transfers between devices: none -> 46.6 us  [per_device(): lax.all_to_all(outgoing, 'dev', split_axis=0, concat_axis=0, tiled=True)]
    all_to_all x0 -> x1, starting transfers between devices: none -> 11.7 us  [per_device(): lax.all_to_all(outgoing, 'dev', split_axis=0, concat_axis=0, tiled=True)]
    pallas_call x2 -> x3, Pallas kernels: 19.2 us -> 22.6 us  [the longest x2 14.7 us: gate_up(): pl.pallas_call(gate_up_kernel, out_shape=jax.ShapeDtypeStruct((count, uni...]
    dot_general x1, matrix products: 1.16 us -> 3.94 us  [per_device(): lax.dot_general(dispatch.astype(jnp.bfloat16), moe_rows, (((0,), (0,)), (...]
    unnamed x3 -> x0, waiting for transfers between devices: 2.06 us -> none
    unnamed x20 -> x14, local copies, waits for them, and re-layouts: 4.66 us -> 2.78 us
  transfers between devices with their start and end apart: 4 -> 5, of which waited for: 1 -> 2; matrix products, arithmetic and copies ran while one was open for 10% -> 10% of each run, Pallas kernels for 7% -> 10%
where the time goes in v6:
time: 151 us
  waiting for transfers between devices  80.3 us (53%)
  matrix products  22.9 us (15%)
  Pallas kernels  22.6 us (15%)
  starting transfers between devices  20.8 us (14%)
  local copies, waits for them, and re-layouts  3.06 us (2%)
    all_to_all x1, waiting for transfers between devices, per_device(): lax.all_to_all(outgoing, 'dev', split_axis=0, concat_axis=0, tiled=True)  46.6 us
    all_to_all x1, waiting for transfers between devices, per_device(): lax.all_to_all(finished, 'dev', split_axis=0, concat_axis=0, tiled=True)  33.7 us
    pallas_call x2, Pallas kernels, gate_up(): pl.pallas_call(gate_up_kernel, out_shape=jax.ShapeDtypeStruct((count, uni...  14.7 us
    all_to_all x1, starting transfers between devices, per_device(): lax.all_to_all(outgoing, 'dev', split_axis=0, concat_axis=0, tiled=True)  11.7 us
    all_to_all x1, starting transfers between devices, per_device(): lax.all_to_all(finished, 'dev', split_axis=0, concat_axis=0, tiled=True)  8.39 us
    pallas_call x1, Pallas kernels, down(): pl.pallas_call(down_kernel, out_shape=jax.ShapeDtypeStruct((count, width)...  7.92 us
    dot_general x1, matrix products, attend_row(): jnp.dot(probs, cache_lat, preferred_element_type=jnp.float32)  6.34 us
    dot_general x1, matrix products, attend_row(): lax.dot_general(query_lat, cache_lat, (((1,), (1,)), ((), ())), preferred...  6 us
  transfers between devices with their start and end apart: 5, of which 2 were waited for; matrix products, arithmetic and copies ran while one was open for 10% of the time, Pallas kernels for 10%

profile of v6, /device:TPU:0, one launch (start us, length us, event | category | flops | bytes accessed | tf_op | source)
XLA Modules:
  0.0 150.8 jit_solution(13004534752185596512)
XLA Ops:
  0.6 0.0 copy-start
  0.6 0.8 copy.19
  1.5 0.1 eq.51
  1.6 0.2 fusion.11
  1.8 0.1 convert_element_type.27
  1.9 0.2 fusion.15
  2.1 3.9 %fusion.1 = bf16[64,8,3584]{2,1,0:T(8,128)(2,1)} fusion(pred[32,512]{1,0:T(8,128)(4,1)S(1)} %fusion.15, bf16[32,3584]{1,0:T(8,128)(2,1)} %param.11), kind=kOutput, calls=%fused_computation.3 | convolution fusion | flops 119275520 | bytes 3915776 | tf_op jit(solution)/shard_map/dot_general | solution.py:135
  6.1 11.7 %all-to-all-start = ((bf16[64,8,3584]{2,1,0:T(8,128)(2,1)}), bf16[64,8,3584]{2,1,0:T(8,128)(2,1)}, u32[]{:S(2)}, u32[]{:S(2)}) async-start(bf16[64,8,3584]{2,1,0:T(8,128)(2,1)} %fusion.1), calls=%async_computation | async-start | bytes 7340032 | tf_op jit(solution)/shard_map/all_to_all | solution.py:139
  17.8 0.1 collective-permute-start
  17.9 0.5 collective-permute-start.1
  18.4 0.1 collective-permute-start.2
  18.5 46.6 %all-to-all-done = bf16[64,8,3584]{2,1,0:T(8,128)(2,1)} async-done(((bf16[64,8,3584]{2,1,0:T(8,128)(2,1)}), bf16[64,8,3584]{2,1,0:T(8,128)(2,1)}, u32[]{:S(2)}, u32[]{:S(2)}) %all-to-all-start) | async-done | bytes 3670048 | tf_op jit(solution)/shard_map/all_to_all | solution.py:139
  65.1 7.3 %shard_map.122.h0_ref = bf16[512,512]{1,0:T(8,128)(2,1)S(1)} custom-call(bf16[512,3584]{1,0:T(8,128)(2,1)} %bitcast.2.x_ref, bf16[3584,512]{1,0:T(8,128)(2,1)} %bitcast.26, bf16[3584,512]{1,0:T(8,128)(2,1)} %bitcast.28), custom_call_target="tpu_custom_call" | custom-call | flops 3758096384 | bytes 11534336 | tf_op jit(solution)/shard_map/pallas_call | solution.py:29
  72.4 0.0 collective-permute-done.g_ref
  72.5 0.0 collective-permute-done.1.u_ref
  72.5 7.4 %shard_map.123.h1_ref = bf16[512,512]{1,0:T(8,128)(2,1)S(1)} custom-call(bf16[512,3584]{1,0:T(8,128)(2,1)} %bitcast.2.x_ref, bf16[3584,512]{1,0:T(8,128)(2,1)} %collective-permute-done.g_ref, bf16[3584,512]{1,0:T(8,128)(2,1)} %collective-permute-done.1.u_ref), custom_call_target="tpu_custom_call" | custom-call | flops 3758096384 | bytes 11534336 | tf_op jit(solution)/shard_map/pallas_call | solution.py:29
  79.8 0.0 collective-permute-done.2.d1_ref
  79.9 7.9 %shard_map.124 = bf16[512,3584]{1,0:T(8,128)(2,1)S(1)} custom-call(bf16[512,512]{1,0:T(8,128)(2,1)S(1)} %shard_map.122.h0_ref, bf16[512,512]{1,0:T(8,128)(2,1)S(1)} %shard_map.123.h1_ref, bf16[3584,512]{1,0:T(8,128)(2,1)} %bitcast.30, bf16[3584,512]{1,0:T(8,128)(2,1)} %collective-permute-done.2.d1_ref), custom_call_target="tpu_custom_call" | custom-call | flops 3758096384 | bytes 12058624 | tf_op jit(solution)/shard_map/pallas_call | solution.py:51
  87.8 0.0 copy-start.1
  87.8 1.8 %copy-done.1 = bf16[512,3584]{1,0:T(8,128)(2,1)} copy-done((bf16[512,3584]{1,0:T(8,128)(2,1)}, bf16[512,3584]{1,0:T(8,128)(2,1)S(1)}, u32[]{:S(2)}) %copy-start.1) | copy-done | bytes 3670040
  89.6 0.0 copy-start.4
  89.6 0.0 copy-start.3
  89.6 0.0 copy-start.5
  89.6 0.0 copy-start.2
  89.6 8.4 %all-to-all-start.1 = ((bf16[64,8,3584]{2,1,0:T(8,128)(2,1)}), bf16[64,8,3584]{2,1,0:T(8,128)(2,1)}, u32[]{:S(2)}, u32[]{:S(2)}) async-start(bf16[64,8,3584]{2,1,0:T(8,128)(2,1)} %bitcast.24), calls=%async_computation.1 | async-start | bytes 7340032 | tf_op jit(solution)/shard_map/all_to_all | solution.py:143
  98.0 0.0 copy-done.4
  98.0 0.1 copy.21
  98.1 0.0 copy-done.3
  98.1 0.1 reshape.88
  98.2 0.0 copy-done.5
  98.3 0.1 iota_compare_fusion.6
  98.3 0.0 copy-done.2
  98.3 6.0 %fusion.19 = f32[4,64,2048]{2,1,0:T(8,128)S(1)} fusion(bf16[4,64,512]{2,1,0:T(8,128)(2,1)S(1)} %copy-done.2, bf16[4,2048,512]{2,1,0:T(8,128)(2,1)} %param.19), kind=kOutput, calls=%fused_computation.28 | convolution fusion | flops 536870912 | bytes 10747904 | tf_op jit(solution)/shard_map/vmap()/dot_general | solution.py:89
  104.3 0.0 copy-done
  104.4 2.4 %fusion.18 = (f32[4,64]{1,0:T(4,128)S(1)}, f32[4,64,2048]{2,1,0:T(8,128)}) fusion(pred[4,2048]{1,0:T(4,128)(4,1)S(1)} %iota_compare_fusion.6, f32[4,64,2048]{2,1,0:T(8,128)S(1)} %fusion.19, bf16[4,64,64]{2,1,0:T(8,128)(2,1)S(1)} %reshape.88, bf16[4,64,2048]{2,1,0:T(8,128)(2,1)S(1)} %copy-done), kind=kOutput, calls=%fused_computation.27 | convolution fusion | flops 70256640 | bytes 5284864 | tf_op jit(solution)/shard_map/vmap()/sub | solution.py:100
  106.7 6.3 %convolution_convert_fusion.1 = bf16[4,64,512]{2,1,0:T(8,128)(2,1)} fusion(bf16[4,2048,512]{2,1,0:T(8,128)(2,1)} %param.19, f32[4,64,2048]{2,1,0:T(8,128)} %get-tuple-element.3, f32[4,64]{1,0:T(4,128)S(1)} %get-tuple-element.2), kind=kOutput, calls=%fused_computation.13 | convolution fusion | flops 538050560 | bytes 10748928 | tf_op jit(solution)/shard_map/vmap()/dot_general | solution.py:102
  113.1 33.7 %all-to-all-done.1 = bf16[64,8,3584]{2,1,0:T(8,128)(2,1)} async-done(((bf16[64,8,3584]{2,1,0:T(8,128)(2,1)}), bf16[64,8,3584]{2,1,0:T(8,128)(2,1)}, u32[]{:S(2)}, u32[]{:S(2)}) %all-to-all-start.1) | async-done | bytes 3670048 | tf_op jit(solution)/shard_map/all_to_all | solution.py:143
  146.7 4.1 %fusion.8 = bf16[32,3584]{1,0:T(8,128)(2,1)} fusion(f32[32,8]{1,0:T(8,128)S(1)} %copy.21, bf16[64,8,3584]{2,1,0:T(8,128)(2,1)} %all-to-all-done.1, s32[32,8]{1,0:T(8,128)S(1)} %multiply_add_fusion), kind=kOutput, calls=%fused_computation.12 | convolution fusion | flops 941375488 | bytes 3901440 | tf_op jit(solution)/shard_map/dot_general | solution.py:145
  (2 shorter events, 0.0 us)
Async XLA Ops:
  0.6 103.7 %copy-start = (bf16[4,64,2048]{2,1,0:T(8,128)(2,1)S(1)}, bf16[4,64,2048]{2,1,0:T(8,128)(2,1)}, u32[]{:S(2)}) copy-start(bf16[4,64,2048]{2,1,0:T(8,128)(2,1)} %param.20) | copy-start | bytes 3145732
  6.1 59.0 %all-to-all-start = ((bf16[64,8,3584]{2,1,0:T(8,128)(2,1)}), bf16[64,8,3584]{2,1,0:T(8,128)(2,1)}, u32[]{:S(2)}, u32[]{:S(2)}) async-start(bf16[64,8,3584]{2,1,0:T(8,128)(2,1)} %fusion.1), calls=%async_computation | async-start | bytes 7340032 | tf_op jit(solution)/shard_map/all_to_all | solution.py:139
  17.8 54.6 %collective-permute-start = (bf16[3584,512]{1,0:T(8,128)(2,1)}, bf16[3584,512]{1,0:T(8,128)(2,1)}, u32[]{:S(2)}, u32[]{:S(2)}) collective-permute-start(bf16[3584,512]{1,0:T(8,128)(2,1)} %bitcast.25), channel_id=1, source_target_pairs={{0,64},{64,0},{1,65},{65,1},{2,66},{66,2},{3,67},{67,3},{4,68},{68... | collective-permute-start | bytes 11010056 | tf_op jit(solution)/shard_map/ppermute | solution.py:72
  17.9 54.5 %collective-permute-start.1 = (bf16[3584,512]{1,0:T(8,128)(2,1)}, bf16[3584,512]{1,0:T(8,128)(2,1)}, u32[]{:S(2)}, u32[]{:S(2)}) collective-permute-start(bf16[3584,512]{1,0:T(8,128)(2,1)} %bitcast.27), channel_id=1, source_target_pairs={{0,64},{64,0},{1,65},{65,1},{2,66},{66,2},{3,67},{67,3},{4,68},{68... | collective-permute-start | bytes 11010056 | tf_op jit(solution)/shard_map/ppermute | solution.py:72
  18.4 61.4 %collective-permute-start.2 = (bf16[3584,512]{1,0:T(8,128)(2,1)}, bf16[3584,512]{1,0:T(8,128)(2,1)}, u32[]{:S(2)}, u32[]{:S(2)}) collective-permute-start(bf16[3584,512]{1,0:T(8,128)(2,1)} %bitcast.29), channel_id=1, source_target_pairs={{0,64},{64,0},{1,65},{65,1},{2,66},{66,2},{3,67},{67,3},{4,68},{68... | collective-permute-start | bytes 11010056 | tf_op jit(solution)/shard_map/ppermute | solution.py:72
  87.8 1.8 %copy-start.1 = (bf16[512,3584]{1,0:T(8,128)(2,1)}, bf16[512,3584]{1,0:T(8,128)(2,1)S(1)}, u32[]{:S(2)}) copy-start(bf16[512,3584]{1,0:T(8,128)(2,1)S(1)} %shard_map.124) | copy-start | bytes 11010052
  89.6 8.4 %copy-start.4 = (f32[32,8]{0,1:T(8,128)S(1)}, f32[32,8]{0,1:T(8,128)}, u32[]{:S(2)}) copy-start(f32[32,8]{0,1:T(8,128)} %param.13) | copy-start | bytes 3076
  89.6 8.5 %copy-start.3 = (bf16[4,4096]{1,0:T(4,128)(2,1)S(1)}, bf16[4,4096]{1,0:T(4,128)(2,1)}, u32[]{:S(2)}) copy-start(bf16[4,4096]{1,0:T(4,128)(2,1)} %param.18) | copy-start | bytes 98308
  89.6 8.6 %copy-start.5 = (s32[4]{0:T(128)S(1)}, s32[4]{0:T(128)}, u32[]{:S(2)}) copy-start(s32[4]{0:T(128)} %param.21) | copy-start | bytes 52
  89.6 8.7 %copy-start.2 = (bf16[4,64,512]{2,1,0:T(8,128)(2,1)S(1)}, bf16[4,64,512]{2,1,0:T(8,128)(2,1)}, u32[]{:S(2)}) copy-start(bf16[4,64,512]{2,1,0:T(8,128)(2,1)} %param.17) | copy-start | bytes 786436
  89.6 57.1 %all-to-all-start.1 = ((bf16[64,8,3584]{2,1,0:T(8,128)(2,1)}), bf16[64,8,3584]{2,1,0:T(8,128)(2,1)}, u32[]{:S(2)}, u32[]{:S(2)}) async-start(bf16[64,8,3584]{2,1,0:T(8,128)(2,1)} %bitcast.24), calls=%async_computation.1 | async-start | bytes 7340032 | tf_op jit(solution)/shard_map/all_to_all | solution.py:143

commit v7 on v6

--- a/solution.py
+++ b/solution.py
@@ -72,12 +72,10 @@
     return lax.ppermute(w, "role", [(0, 1), (1, 0)])
 
 
-def full_expert(rows, w_gate, w_up, w_down):
-    gate_own, up_own, down_own = w_gate[0], w_up[0], w_down[0]
-    gate_other, up_other, down_other = other_half(gate_own), other_half(up_own), other_half(down_own)
-    h0 = gate_up(rows, gate_own, up_own)
-    h1 = gate_up(rows, gate_other, up_other)
-    return down(h0, h1, down_own, down_other)
+def full_expert(rows, own, other):
+    h0 = gate_up(rows, own[0], own[1])
+    h1 = gate_up(rows, other[0], other[1])
+    return down(h0, h1, own[2], other[2])
 
 
 score_scale = 192.0 ** (-0.5)
@@ -132,19 +130,31 @@
     slot_iota = jnp.arange(slot_count, dtype=jnp.int32)
     picks = destination[:, None] == slot_iota[None, :]
     dispatch = jnp.any(picks.reshape(tok_count, topk_count, slot_count), axis=1)
-    outgoing = lax.dot_general(
-        dispatch.astype(jnp.bfloat16), moe_rows, (((0,), (0,)), ((), ())),
-        preferred_element_type=jnp.float32,
-    ).astype(jnp.bfloat16).reshape(experts, capacity, width)
-    arrived = lax.all_to_all(outgoing, "dev", split_axis=0, concat_axis=0, tiled=True)
-    own_rows = arrived.reshape(experts * capacity, width)
-    expert_sum = full_expert(own_rows, w_gate, w_up, w_down)
-    finished = expert_sum.reshape(experts, capacity, width)
-    returned = lax.all_to_all(finished, "dev", split_axis=0, concat_axis=0, tiled=True)
-    flat_back = returned.reshape(slot_count, width)
-    picked = jnp.dot(
-        picks.astype(jnp.bfloat16), flat_back, preferred_element_type=jnp.float32
-    ).reshape(tok_count, topk_count, width)
+    dispatch = dispatch.astype(jnp.bfloat16).reshape(tok_count, experts, capacity)
+    pick_matrix = picks.astype(jnp.bfloat16).reshape(pair_count, experts, capacity)
+    own = (w_gate[0], w_up[0], w_down[0])
+    other = tuple(other_half(w) for w in own)
+    chunks = 2
+    per = capacity // chunks
+    picked = None
+    for chunk in range(chunks):
+        lo, hi = chunk * per, (chunk + 1) * per
+        outgoing = lax.dot_general(
+            dispatch[:, :, lo:hi].reshape(tok_count, experts * per), moe_rows,
+            (((0,), (0,)), ((), ())), preferred_element_type=jnp.float32,
+        ).astype(jnp.bfloat16).reshape(experts, per, width)
+        arrived = lax.all_to_all(outgoing, "dev", split_axis=0, concat_axis=0, tiled=True)
+        finished = full_expert(arrived.reshape(experts * per, width), own, other)
+        returned = lax.all_to_all(
+            finished.reshape(experts, per, width), "dev", split_axis=0, concat_axis=0, tiled=True
+        )
+        term = jnp.dot(
+            pick_matrix[:, :, lo:hi].reshape(pair_count, experts * per),
+            returned.reshape(experts * per, width),
+            preferred_element_type=jnp.float32,
+        )
+        picked = term if picked is None else picked + term
+    picked = picked.reshape(tok_count, topk_count, width)
     moe_out = jnp.sum(picked * gate_weights[:, :, None], axis=1).astype(jnp.bfloat16)
     attended = jax.vmap(attend_row)(q_latent, q_rope, latent_cache, rope_cache, lengths)
     return (moe_out, attended)

time: 151 us -> 156 us (1.033)
  waiting for transfers between devices: 80.3 us -> 40.3 us
  local copies, waits for them, and re-layouts: 3.06 us -> 21.1 us
  starting transfers between devices: 20.8 us -> 34.3 us
  Pallas kernels: 22.6 us -> 29.1 us
  matrix products: 22.9 us -> 28.7 us
    all_to_all x1 -> x2, waiting for transfers between devices: 33.7 us -> 12.5 us  [per_device(): lax.all_to_all(finished.reshape(experts, per, width), 'dev', split_axis=0...]
    all_to_all x1 -> x2, waiting for transfers between devices: 46.6 us -> 27.8 us  [per_device(): lax.all_to_all(outgoing, 'dev', split_axis=0, concat_axis=0, tiled=True)]
    reshape x0 -> x7, local copies, waits for them, and re-layouts: none -> 14.5 us  [the longest x2 5.88 us: per_device(): finished = full_expert(arrived.reshape(experts * per, width), own, other)]
    all_to_all x1 -> x2, starting transfers between devices: 8.39 us -> 16.3 us  [per_device(): lax.all_to_all(finished.reshape(experts, per, width), 'dev', split_axis=0...]
    all_to_all x1 -> x2, starting transfers between devices: 11.7 us -> 17.3 us  [per_device(): lax.all_to_all(outgoing, 'dev', split_axis=0, concat_axis=0, tiled=True)]
    dot_general x2 -> x4, matrix products: 8 us -> 12.5 us  [the longest x2 9.07 us: per_device(): jnp.dot(pick_matrix[:, :, lo:hi].reshape(pair_count, experts * per), retu...]
    pallas_call x1 -> x2, Pallas kernels: 7.92 us -> 12.3 us  [down(): pl.pallas_call(down_kernel, out_shape=jax.ShapeDtypeStruct((count, width)...]
    unnamed x14 -> x26, local copies, waits for them, and re-layouts: 2.78 us -> 6.19 us
  transfers between devices with their start and end apart: 5 -> 7, of which waited for: 2 -> 3; matrix products, arithmetic and copies ran while one was open for 10% -> 26% of each run, Pallas kernels for 10% -> 19%
where the time goes in v7:
time: 156 us; the launch traced here: 155 us
  waiting for transfers between devices  40.3 us (26%)
  starting transfers between devices  34.3 us (22%)
  Pallas kernels  29.1 us (19%)
  matrix products  28.7 us (18%)
  local copies, waits for them, and re-layouts  21.1 us (14%)
    all_to_all x2, waiting for transfers between devices, per_device(): lax.all_to_all(outgoing, 'dev', split_axis=0, concat_axis=0, tiled=True)  27.8 us
    all_to_all x2, starting transfers between devices, per_device(): lax.all_to_all(outgoing, 'dev', split_axis=0, concat_axis=0, tiled=True)  17.3 us
    pallas_call x4, Pallas kernels, gate_up(): pl.pallas_call(gate_up_kernel, out_shape=jax.ShapeDtypeStruct((count, uni...  16.8 us
    all_to_all x2, starting transfers between devices, per_device(): lax.all_to_all(finished.reshape(experts, per, width), 'dev', split_axis=0...  16.3 us
    all_to_all x2, waiting for transfers between devices, per_device(): lax.all_to_all(finished.reshape(experts, per, width), 'dev', split_axis=0...  12.5 us
    pallas_call x2, Pallas kernels, down(): pl.pallas_call(down_kernel, out_shape=jax.ShapeDtypeStruct((count, width)...  12.3 us
    dot_general x2, matrix products, per_device(): jnp.dot(pick_matrix[:, :, lo:hi].reshape(pair_count, experts * per), retu...  9.07 us
    dot_general x1, matrix products, attend_row(): lax.dot_general(query_lat, cache_lat, (((1,), (1,)), ((), ())), preferred...  7.4 us
  transfers between devices with their start and end apart: 7, of which 3 were waited for; matrix products, arithmetic and copies ran while one was open for 26% of the time, Pallas kernels for 19%

profile of v7, /device:TPU:0, one launch (start us, length us, event | category | flops | bytes accessed | tf_op | source)
XLA Modules:
  0.0 154.7 jit_solution(9345037508030559417)
XLA Ops:
  0.6 0.0 copy-start
  0.6 0.1 collective-permute-start
  0.7 0.5 collective-permute-start.1
  1.2 0.1 collective-permute-start.2
  1.3 0.8 copy.27
  2.1 0.1 reshape.100
  2.2 0.2 fusion.14
  2.4 0.1 convert_element_type.31
  2.5 0.2 fusion.18
  2.7 0.2 copy.29
  2.9 0.1 fusion.24
  3.0 1.5 convolution_convert_fusion
  4.5 1.5 reshape.107
  6.0 0.0 copy-start.7
  6.0 11.6 %all-to-all-start.2 = ((bf16[64,4,3584]{2,1,0:T(4,128)(2,1)}), bf16[64,4,3584]{2,1,0:T(4,128)(2,1)S(1)}, u32[]{:S(2)}, u32[]{:S(2)}) async-start(bf16[64,4,3584]{2,1,0:T(4,128)(2,1)} %reshape.107), calls=%async_computation.2 | async-start | bytes 3670016 | tf_op jit(solution)/shard_map/all_to_all | solution.py:146
  17.6 0.0 copy-done.7
  17.7 1.9 %convolution_convert_fusion.1 = bf16[256,3584]{1,0:T(8,128)(2,1)} fusion(pred[32,256]{0,1:T(8,128)(4,1)S(1)} %bitcast.43, bf16[32,3584]{1,0:T(8,128)(2,1)S(1)} %copy-done.7), kind=kOutput, calls=%fused_computation.7 | convolution fusion | flops 59637760 | bytes 2072576 | tf_op jit(solution)/shard_map/dot_general | solution.py:142
  19.5 4.1 %reshape.103 = bf16[64,4,3584]{2,1,0:T(4,128)(2,1)} reshape(bf16[256,3584]{1,0:T(8,128)(2,1)} %convolution_convert_fusion.1) | data formatting | bytes 3670016 | tf_op jit(solution)/shard_map/reshape | solution.py:145
  23.6 21.9 %all-to-all-done.2 = bf16[64,4,3584]{2,1,0:T(4,128)(2,1)S(1)} async-done(((bf16[64,4,3584]{2,1,0:T(4,128)(2,1)}), bf16[64,4,3584]{2,1,0:T(4,128)(2,1)S(1)}, u32[]{:S(2)}, u32[]{:S(2)}) %all-to-all-start.2) | async-done | bytes 1835040 | tf_op jit(solution)/shard_map/all_to_all | solution.py:146
  45.5 0.0 copy-start.5
  45.5 1.2 copy-done.5
  46.8 5.6 %all-to-all-start = ((bf16[64,4,3584]{2,1,0:T(4,128)(2,1)}), bf16[64,4,3584]{2,1,0:T(4,128)(2,1)}, u32[]{:S(2)}, u32[]{:S(2)}) async-start(bf16[64,4,3584]{2,1,0:T(4,128)(2,1)} %reshape.103), calls=%async_computation | async-start | bytes 3670016 | tf_op jit(solution)/shard_map/all_to_all | solution.py:146
  52.4 2.9 %reshape.108.x_ref = bf16[256,3584]{1,0:T(8,128)(2,1)S(1)} reshape(bf16[64,4,3584]{2,1,0:T(4,128)(2,1)} %copy-done.5) | data formatting | bytes 3670016 | tf_op jit(solution)/shard_map/reshape | solution.py:147
  55.4 0.0 copy-start.1
  55.4 2.0 %copy-done.1 = bf16[1,3584,512]{2,1,0:T(8,128)(2,1)S(1)} copy-done((bf16[1,3584,512]{2,1,0:T(8,128)(2,1)S(1)}, bf16[1,3584,512]{2,1,0:T(8,128)(2,1)}, u32[]{:S(2)}) %copy-start.1) | copy-done | bytes 3670040
  57.4 3.9 %shard_map.125.h0_ref = bf16[256,512]{1,0:T(8,128)(2,1)S(1)} custom-call(bf16[256,3584]{1,0:T(8,128)(2,1)S(1)} %reshape.108.x_ref, bf16[3584,512]{1,0:T(8,128)(2,1)S(1)} %bitcast.34, bf16[3584,512]{1,0:T(8,128)(2,1)} %bitcast.40), custom_call_target="tpu_custom_call" | custom-call | flops 1879048192 | bytes 9437184 | tf_op jit(solution)/shard_map/pallas_call | solution.py:29
  61.3 0.0 collective-permute-done.g_ref
  61.3 0.0 collective-permute-done.1.u_ref
  61.3 0.0 copy-start.3
  61.4 4.5 %shard_map.126.h1_ref = bf16[256,512]{1,0:T(8,128)(2,1)S(1)} custom-call(bf16[256,3584]{1,0:T(8,128)(2,1)S(1)} %reshape.108.x_ref, bf16[3584,512]{1,0:T(8,128)(2,1)} %collective-permute-done.g_ref, bf16[3584,512]{1,0:T(8,128)(2,1)} %collective-permute-done.1.u_ref), custom_call_target="tpu_custom_call" | custom-call | flops 1879048192 | bytes 9437184 | tf_op jit(solution)/shard_map/pallas_call | solution.py:29
  65.9 0.0 collective-permute-done.2.d1_ref
  65.9 0.0 copy-done.3
  65.9 6.1 %shard_map.127 = bf16[256,3584]{1,0:T(8,128)(2,1)S(1)} custom-call(bf16[256,512]{1,0:T(8,128)(2,1)S(1)} %shard_map.125.h0_ref, bf16[256,512]{1,0:T(8,128)(2,1)S(1)} %shard_map.126.h1_ref, bf16[3584,512]{1,0:T(8,128)(2,1)S(1)} %bitcast.37, bf16[3584,512]{1,0:T(8,128)(2,1)} %collective-permute-done.2.d1_ref), custom_call_target="tpu_custom_call" | custom-call | flops 1879048192 | bytes 9699328 | tf_op jit(solution)/shard_map/pallas_call | solution.py:51
  72.0 1.5 reshape.109
  73.5 0.0 copy-start.10
  73.5 0.0 copy-start.9
  73.5 5.9 %all-to-all-done = bf16[64,4,3584]{2,1,0:T(4,128)(2,1)} async-done(((bf16[64,4,3584]{2,1,0:T(4,128)(2,1)}), bf16[64,4,3584]{2,1,0:T(4,128)(2,1)}, u32[]{:S(2)}, u32[]{:S(2)}) %all-to-all-start) | async-done | bytes 1835040 | tf_op jit(solution)/shard_map/all_to_all | solution.py:146
  79.4 5.9 %all-to-all-start.3 = ((bf16[64,4,3584]{2,1,0:T(4,128)(2,1)}), bf16[64,4,3584]{2,1,0:T(4,128)(2,1)}, u32[]{:S(2)}, u32[]{:S(2)}) async-start(bf16[64,4,3584]{2,1,0:T(4,128)(2,1)} %reshape.109), calls=%async_computation.3 | async-start | bytes 3670016 | tf_op jit(solution)/shard_map/all_to_all | solution.py:148
  85.3 0.0 copy-done.10
  85.3 0.1 copy.32
  85.3 0.0 copy-done.9
  85.3 0.1 reshape.111
  85.5 0.0 copy-done.8
  85.5 7.4 %fusion.26 = f32[4,64,2048]{2,1,0:T(8,128)} fusion(bf16[4,64,512]{2,1,0:T(8,128)(2,1)S(1)} %copy-done.8, bf16[4,2048,512]{2,1,0:T(8,128)(2,1)} %param.19), kind=kOutput, calls=%fused_computation.39 | convolution fusion | flops 536870912 | bytes 10747904 | tf_op jit(solution)/shard_map/vmap()/dot_general | solution.py:87
  92.9 2.9 %reshape.104.x_ref = bf16[256,3584]{1,0:T(8,128)(2,1)S(1)} reshape(bf16[64,4,3584]{2,1,0:T(4,128)(2,1)} %all-to-all-done) | data formatting | bytes 3670016 | tf_op jit(solution)/shard_map/reshape | solution.py:147
  95.8 0.0 copy-start.2
  95.9 2.0 %copy-done.2 = bf16[1,3584,512]{2,1,0:T(8,128)(2,1)S(1)} copy-done((bf16[1,3584,512]{2,1,0:T(8,128)(2,1)S(1)}, bf16[1,3584,512]{2,1,0:T(8,128)(2,1)}, u32[]{:S(2)}) %copy-start.2) | copy-done | bytes 3670040
  97.9 3.9 %shard_map.122.h0_ref = bf16[256,512]{1,0:T(8,128)(2,1)S(1)} custom-call(bf16[256,3584]{1,0:T(8,128)(2,1)S(1)} %reshape.104.x_ref, bf16[3584,512]{1,0:T(8,128)(2,1)S(1)} %bitcast.35, bf16[3584,512]{1,0:T(8,128)(2,1)} %bitcast.41), custom_call_target="tpu_custom_call" | custom-call | flops 1879048192 | bytes 9437184 | tf_op jit(solution)/shard_map/pallas_call | solution.py:29
  101.8 0.0 copy-start.4
  101.8 4.5 %shard_map.123.h1_ref = bf16[256,512]{1,0:T(8,128)(2,1)S(1)} custom-call(bf16[256,3584]{1,0:T(8,128)(2,1)S(1)} %reshape.104.x_ref, bf16[3584,512]{1,0:T(8,128)(2,1)} %collective-permute-done.g_ref, bf16[3584,512]{1,0:T(8,128)(2,1)} %collective-permute-done.1.u_ref), custom_call_target="tpu_custom_call" | custom-call | flops 1879048192 | bytes 9437184 | tf_op jit(solution)/shard_map/pallas_call | solution.py:29
  106.3 0.0 copy-done.4
  106.3 6.1 %shard_map.124 = bf16[256,3584]{1,0:T(8,128)(2,1)S(1)} custom-call(bf16[256,512]{1,0:T(8,128)(2,1)S(1)} %shard_map.122.h0_ref, bf16[256,512]{1,0:T(8,128)(2,1)S(1)} %shard_map.123.h1_ref, bf16[3584,512]{1,0:T(8,128)(2,1)S(1)} %bitcast.38, bf16[3584,512]{1,0:T(8,128)(2,1)} %collective-permute-done.2.d1_ref), custom_call_target="tpu_custom_call" | custom-call | flops 1879048192 | bytes 9699328 | tf_op jit(solution)/shard_map/pallas_call | solution.py:51
  112.5 1.5 reshape.105
  114.0 0.0 all-to-all-done.3
  114.0 10.5 %all-to-all-start.1 = ((bf16[64,4,3584]{2,1,0:T(4,128)(2,1)}), bf16[64,4,3584]{2,1,0:T(4,128)(2,1)}, u32[]{:S(2)}, u32[]{:S(2)}) async-start(bf16[64,4,3584]{2,1,0:T(4,128)(2,1)} %reshape.105), calls=%async_computation.1 | async-start | bytes 3670016 | tf_op jit(solution)/shard_map/all_to_all | solution.py:148
  124.4 0.0 copy-done.11
  124.5 0.1 iota_compare_fusion.5
  124.5 0.0 copy-done
  124.6 0.0 copy-done.6
  124.6 2.3 %fusion.25 = (f32[4,64]{1,0:T(4,128)S(1)}, f32[4,64,2048]{2,1,0:T(8,128)}) fusion(pred[4,2048]{1,0:T(4,128)(4,1)S(1)} %iota_compare_fusion.5, f32[4,64,2048]{2,1,0:T(8,128)S(1)} %copy-done.6, bf16[4,64,64]{2,1,0:T(8,128)(2,1)S(1)} %reshape.111, bf16[4,64,2048]{2,1,0:T(8,128)(2,1)S(1)} %copy-done), kind=kOutput, calls=%fused_computation.38 | convolution fusion | flops 70256640 | bytes 5284864 | tf_op jit(solution)/shard_map/vmap()/sub | solution.py:98
  126.9 6.3 %convolution_convert_fusion.2 = bf16[4,64,512]{2,1,0:T(8,128)(2,1)} fusion(bf16[4,2048,512]{2,1,0:T(8,128)(2,1)} %param.19, f32[4,64,2048]{2,1,0:T(8,128)} %get-tuple-element.5, f32[4,64]{1,0:T(4,128)S(1)} %get-tuple-element.4), kind=kOutput, calls=%fused_computation.18 | convolution fusion | flops 538050560 | bytes 10748928 | tf_op jit(solution)/shard_map/vmap()/dot_general | solution.py:100
  133.2 4.1 %convolution_bitcast_fusion = f32[256,3584]{1,0:T(8,128)} fusion(bf16[64,4,3584]{2,1,0:T(4,128)(2,1)} %all-to-all-done.3, s32[64,8]{0,1:T(8,128)S(1)} %multiply_add_fusion.1, s32[256]{0:T(256)S(1)} %multiply_add_fusion.2), kind=kOutput, calls=%fused_computation.1 | convolution fusion | flops 469893120 | bytes 5508096 | tf_op jit(solution)/shard_map/dot_general | solution.py:151
  137.3 12.5 %all-to-all-done.1 = bf16[64,4,3584]{2,1,0:T(4,128)(2,1)} async-done(((bf16[64,4,3584]{2,1,0:T(4,128)(2,1)}), bf16[64,4,3584]{2,1,0:T(4,128)(2,1)}, u32[]{:S(2)}, u32[]{:S(2)}) %all-to-all-start.1) | async-done | bytes 1835040 | tf_op jit(solution)/shard_map/all_to_all | solution.py:148
  149.8 5.0 %fusion.11 = bf16[32,3584]{1,0:T(8,128)(2,1)} fusion(f32[32,8]{1,0:T(8,128)S(1)} %copy.32, f32[256,3584]{1,0:T(8,128)} %convolution_bitcast_fusion, bf16[64,4,3584]{2,1,0:T(4,128)(2,1)} %all-to-all-done.1, s32[64,8]{0,1:T(8,128)S(1)} %multiply_add_fusion.1, s32[256]{0:T(256)S(1)} %multiply_add_fusion.2), kind=kOutput, calls=%fused_computation.17 | convolution fusion | flops 472530944 | bytes 5738496 | tf_op jit(solution)/shard_map/dot_general | solution.py:151
  (7 shorter events, 0.0 us)
Async XLA Ops:
  0.6 123.9 %copy-start = (bf16[4,64,2048]{2,1,0:T(8,128)(2,1)S(1)}, bf16[4,64,2048]{2,1,0:T(8,128)(2,1)}, u32[]{:S(2)}) copy-start(bf16[4,64,2048]{2,1,0:T(8,128)(2,1)} %param.20) | copy-start | bytes 3145732
  0.6 60.7 %collective-permute-start = (bf16[3584,512]{1,0:T(8,128)(2,1)}, bf16[3584,512]{1,0:T(8,128)(2,1)}, u32[]{:S(2)}, u32[]{:S(2)}) collective-permute-start(bf16[3584,512]{1,0:T(8,128)(2,1)} %bitcast.33), channel_id=1, source_target_pairs={{0,64},{64,0},{1,65},{65,1},{2,66},{66,2},{3,67},{67,3},{4,68},{68... | collective-permute-start | bytes 11010056 | tf_op jit(solution)/shard_map/ppermute | solution.py:72
  0.7 60.6 %collective-permute-start.1 = (bf16[3584,512]{1,0:T(8,128)(2,1)}, bf16[3584,512]{1,0:T(8,128)(2,1)}, u32[]{:S(2)}, u32[]{:S(2)}) collective-permute-start(bf16[3584,512]{1,0:T(8,128)(2,1)} %bitcast.39), channel_id=1, source_target_pairs={{0,64},{64,0},{1,65},{65,1},{2,66},{66,2},{3,67},{67,3},{4,68},{68... | collective-permute-start | bytes 11010056 | tf_op jit(solution)/shard_map/ppermute | solution.py:72
  1.2 64.6 %collective-permute-start.2 = (bf16[3584,512]{1,0:T(8,128)(2,1)}, bf16[3584,512]{1,0:T(8,128)(2,1)}, u32[]{:S(2)}, u32[]{:S(2)}) collective-permute-start(bf16[3584,512]{1,0:T(8,128)(2,1)} %bitcast.36), channel_id=1, source_target_pairs={{0,64},{64,0},{1,65},{65,1},{2,66},{66,2},{3,67},{67,3},{4,68},{68... | collective-permute-start | bytes 11010056 | tf_op jit(solution)/shard_map/ppermute | solution.py:72
  6.0 11.6 %copy-start.7 = (bf16[32,3584]{1,0:T(8,128)(2,1)S(1)}, bf16[32,3584]{1,0:T(8,128)(2,1)}, u32[]{:S(2)}) copy-start(bf16[32,3584]{1,0:T(8,128)(2,1)} %param.11) | copy-start | bytes 688132
  6.0 39.5 %all-to-all-start.2 = ((bf16[64,4,3584]{2,1,0:T(4,128)(2,1)}), bf16[64,4,3584]{2,1,0:T(4,128)(2,1)S(1)}, u32[]{:S(2)}, u32[]{:S(2)}) async-start(bf16[64,4,3584]{2,1,0:T(4,128)(2,1)} %reshape.107), calls=%async_computation.2 | async-start | bytes 3670016 | tf_op jit(solution)/shard_map/all_to_all | solution.py:146
  45.5 1.2 copy-start.5
  46.8 32.6 %all-to-all-start = ((bf16[64,4,3584]{2,1,0:T(4,128)(2,1)}), bf16[64,4,3584]{2,1,0:T(4,128)(2,1)}, u32[]{:S(2)}, u32[]{:S(2)}) async-start(bf16[64,4,3584]{2,1,0:T(4,128)(2,1)} %reshape.103), calls=%async_computation | async-start | bytes 3670016 | tf_op jit(solution)/shard_map/all_to_all | solution.py:146
  55.4 2.0 %copy-start.1 = (bf16[1,3584,512]{2,1,0:T(8,128)(2,1)S(1)}, bf16[1,3584,512]{2,1,0:T(8,128)(2,1)}, u32[]{:S(2)}) copy-start(bf16[1,3584,512]{2,1,0:T(8,128)(2,1)} %param.14) | copy-start | bytes 11010052
  61.3 4.5 %copy-start.3 = (bf16[1,3584,512]{2,1,0:T(8,128)(2,1)S(1)}, bf16[1,3584,512]{2,1,0:T(8,128)(2,1)}, u32[]{:S(2)}) copy-start(bf16[1,3584,512]{2,1,0:T(8,128)(2,1)} %param.16) | copy-start | bytes 11010052
  73.5 11.8 %copy-start.10 = (f32[32,8]{0,1:T(8,128)S(1)}, f32[32,8]{0,1:T(8,128)}, u32[]{:S(2)}) copy-start(f32[32,8]{0,1:T(8,128)} %param.13) | copy-start | bytes 3076
  73.5 11.9 %copy-start.9 = (bf16[4,4096]{1,0:T(4,128)(2,1)S(1)}, bf16[4,4096]{1,0:T(4,128)(2,1)}, u32[]{:S(2)}) copy-start(bf16[4,4096]{1,0:T(4,128)(2,1)} %param.18) | copy-start | bytes 98308
  73.5 12.0 %copy-start.8 = (bf16[4,64,512]{2,1,0:T(8,128)(2,1)S(1)}, bf16[4,64,512]{2,1,0:T(8,128)(2,1)}, u32[]{:S(2)}) copy-start(bf16[4,64,512]{2,1,0:T(8,128)(2,1)} %param.17) | copy-start | bytes 786436
  79.4 34.6 %all-to-all-start.3 = ((bf16[64,4,3584]{2,1,0:T(4,128)(2,1)}), bf16[64,4,3584]{2,1,0:T(4,128)(2,1)}, u32[]{:S(2)}, u32[]{:S(2)}) async-start(bf16[64,4,3584]{2,1,0:T(4,128)(2,1)} %reshape.109), calls=%async_computation.3 | async-start | bytes 3670016 | tf_op jit(solution)/shard_map/all_to_all | solution.py:148
  95.8 2.0 %copy-start.2 = (bf16[1,3584,512]{2,1,0:T(8,128)(2,1)S(1)}, bf16[1,3584,512]{2,1,0:T(8,128)(2,1)}, u32[]{:S(2)}) copy-start(bf16[1,3584,512]{2,1,0:T(8,128)(2,1)} %param.14) | copy-start | bytes 11010052
  101.8 4.5 %copy-start.4 = (bf16[1,3584,512]{2,1,0:T(8,128)(2,1)S(1)}, bf16[1,3584,512]{2,1,0:T(8,128)(2,1)}, u32[]{:S(2)}) copy-start(bf16[1,3584,512]{2,1,0:T(8,128)(2,1)} %param.16) | copy-start | bytes 11010052
  114.0 10.5 %copy-start.11 = (s32[4]{0:T(128)S(1)}, s32[4]{0:T(128)}, u32[]{:S(2)}) copy-start(s32[4]{0:T(128)} %param.21) | copy-start | bytes 52
  114.0 10.6 %copy-start.6 = (f32[4,64,2048]{2,1,0:T(8,128)S(1)}, f32[4,64,2048]{2,1,0:T(8,128)}, u32[]{:S(2)}) copy-start(f32[4,64,2048]{2,1,0:T(8,128)} %fusion.26) | copy-start | bytes 6291460
  114.0 35.8 %all-to-all-start.1 = ((bf16[64,4,3584]{2,1,0:T(4,128)(2,1)}), bf16[64,4,3584]{2,1,0:T(4,128)(2,1)}, u32[]{:S(2)}, u32[]{:S(2)}) async-start(bf16[64,4,3584]{2,1,0:T(4,128)(2,1)} %reshape.105), calls=%async_computation.1 | async-start | bytes 3670016 | tf_op jit(solution)/shard_map/all_to_all | solution.py:148

commit v8 on v6

--- a/solution.py
+++ b/solution.py
@@ -6,10 +6,16 @@
 from jax.experimental.pallas import tpu as pltpu
 import functools
 
-def gate_up_kernel(x_ref, g_ref, u_ref, h_ref):
+def partial_kernel(x_ref, g_ref, u_ref, pg_ref, pu_ref):
     x = x_ref[...]
-    gate_part = jnp.dot(x, g_ref[...], preferred_element_type=jnp.float32)
-    up_part = jnp.dot(x, u_ref[...], preferred_element_type=jnp.float32)
+    pg_ref[...] = jnp.dot(x, g_ref[...], preferred_element_type=jnp.float32)
+    pu_ref[...] = jnp.dot(x, u_ref[...], preferred_element_type=jnp.float32)
+
+
+def finish_kernel(x_ref, g_ref, u_ref, pg_ref, pu_ref, h_ref):
+    x = x_ref[...]
+    gate_part = pg_ref[...] + jnp.dot(x, g_ref[...], preferred_element_type=jnp.float32)
+    up_part = pu_ref[...] + jnp.dot(x, u_ref[...], preferred_element_type=jnp.float32)
     h_ref[...] = (jax.nn.silu(gate_part) * up_part).astype(h_ref.dtype)
 
 
@@ -23,61 +29,79 @@
     o_ref[...] = total.astype(o_ref.dtype)
 
 
-def gate_up(rows, gate_matrix, up_matrix, unit_tile=256):
-    count, width = rows.shape
+def gate_up_partial(rows, gate_matrix, up_matrix, unit_tile=256):
+    count, depth = rows.shape
     units = gate_matrix.shape[1]
+    part = jax.ShapeDtypeStruct((count, units), jnp.float32)
     return pl.pallas_call(
-        gate_up_kernel,
+        partial_kernel,
+        out_shape=(part, part),
+        grid=(units // unit_tile,),
+        in_specs=[
+            pl.BlockSpec((count, depth), lambda j: (0, 0)),
+            pl.BlockSpec((depth, unit_tile), lambda j: (0, j)),
+            pl.BlockSpec((depth, unit_tile), lambda j: (0, j)),
+        ],
+        out_specs=[pl.BlockSpec((count, unit_tile), lambda j: (0, j))] * 2,
+        compiler_params=pltpu.CompilerParams(vmem_limit_bytes=48 * 1024 * 1024),
+        cost_estimate=pl.CostEstimate(
+            flops=4 * count * depth * units,
+            transcendentals=0,
+            bytes_accessed=2 * (count * depth + 2 * depth * units) + 8 * count * units,
+        ),
+    )(rows, gate_matrix, up_matrix)
+
+
+def gate_up_finish(rows, gate_matrix, up_matrix, partials, unit_tile=256):
+    count, depth = rows.shape
+    units = gate_matrix.shape[1]
+    tile = pl.BlockSpec((count, unit_tile), lambda j: (0, j))
+    return pl.pallas_call(
+        finish_kernel,
         out_shape=jax.ShapeDtypeStruct((count, units), jnp.bfloat16),
         grid=(units // unit_tile,),
         in_specs=[
-            pl.BlockSpec((count, width), lambda j: (0, 0)),
-            pl.BlockSpec((width, unit_tile), lambda j: (0, j)),
-            pl.BlockSpec((width, unit_tile), lambda j: (0, j)),
+            pl.BlockSpec((count, depth), lambda j: (0, 0)),
+            pl.BlockSpec((depth, unit_tile), lambda j: (1, j)),
+            pl.BlockSpec((depth, unit_tile), lambda j: (1, j)),
+            tile,
+            tile,
         ],
-        out_specs=pl.BlockSpec((count, unit_tile), lambda j: (0, j)),
+        out_specs=tile,
         compiler_params=pltpu.CompilerParams(vmem_limit_bytes=48 * 1024 * 1024),
         cost_estimate=pl.CostEstimate(
-            flops=4 * count * width * units,
+            flops=4 * count * depth * units,
             transcendentals=count * units,
-            bytes_accessed=2 * (count * width + 2 * width * units + count * units),
+            bytes_accessed=2 * (count * depth + 2 * depth * units + count * units) + 8 * count * units,
         ),
-    )(rows, gate_matrix, up_matrix)
-
-
-def down(h0, h1, d0, d1, out_tile=512):
+    )(rows, gate_matrix, up_matrix, *partials)
+
+
+def down_columns(h0, h1, d0, d1, first, count_out, out_tile=256):
     count, units = h0.shape
-    width = d0.shape[0]
+    offset = first // out_tile
     return pl.pallas_call(
         down_kernel,
-        out_shape=jax.ShapeDtypeStruct((count, width), jnp.bfloat16),
-        grid=(width // out_tile,),
+        out_shape=jax.ShapeDtypeStruct((count, count_out), jnp.bfloat16),
+        grid=(count_out // out_tile,),
         in_specs=[
             pl.BlockSpec((count, units), lambda j: (0, 0)),
             pl.BlockSpec((count, units), lambda j: (0, 0)),
-            pl.BlockSpec((out_tile, units), lambda j: (j, 0)),
-            pl.BlockSpec((out_tile, units), lambda j: (j, 0)),
+            pl.BlockSpec((out_tile, units), lambda j: (j + offset, 0)),
+            pl.BlockSpec((out_tile, units), lambda j: (j + offset, 0)),
         ],
         out_specs=pl.BlockSpec((count, out_tile), lambda j: (0, j)),
         compiler_params=pltpu.CompilerParams(vmem_limit_bytes=48 * 1024 * 1024),
         cost_estimate=pl.CostEstimate(
-            flops=4 * count * width * units,
+            flops=4 * count * count_out * units,
             transcendentals=0,
-            bytes_accessed=2 * (count * width + 2 * width * units + 2 * count * units),
+            bytes_accessed=2 * (count * count_out + 2 * count_out * units + 2 * count * units),
         ),
     )(h0, h1, d0, d1)
 
 
 def other_half(w):
     return lax.ppermute(w, "role", [(0, 1), (1, 0)])
-
-
-def full_expert(rows, w_gate, w_up, w_down):
-    gate_own, up_own, down_own = w_gate[0], w_up[0], w_down[0]
-    gate_other, up_other, down_other = other_half(gate_own), other_half(up_own), other_half(down_own)
-    h0 = gate_up(rows, gate_own, up_own)
-    h1 = gate_up(rows, gate_other, up_other)
-    return down(h0, h1, down_own, down_other)
 
 
 score_scale = 192.0 ** (-0.5)
@@ -131,20 +155,30 @@
     destination = flat_ids * capacity + slot_index
     slot_iota = jnp.arange(slot_count, dtype=jnp.int32)
     picks = destination[:, None] == slot_iota[None, :]
-    dispatch = jnp.any(picks.reshape(tok_count, topk_count, slot_count), axis=1)
-    outgoing = lax.dot_general(
-        dispatch.astype(jnp.bfloat16), moe_rows, (((0,), (0,)), ((), ())),
-        preferred_element_type=jnp.float32,
-    ).astype(jnp.bfloat16).reshape(experts, capacity, width)
-    arrived = lax.all_to_all(outgoing, "dev", split_axis=0, concat_axis=0, tiled=True)
-    own_rows = arrived.reshape(experts * capacity, width)
-    expert_sum = full_expert(own_rows, w_gate, w_up, w_down)
-    finished = expert_sum.reshape(experts, capacity, width)
-    returned = lax.all_to_all(finished, "dev", split_axis=0, concat_axis=0, tiled=True)
-    flat_back = returned.reshape(slot_count, width)
-    picked = jnp.dot(
-        picks.astype(jnp.bfloat16), flat_back, preferred_element_type=jnp.float32
-    ).reshape(tok_count, topk_count, width)
+    dispatch = jnp.any(picks.reshape(tok_count, topk_count, slot_count), axis=1).astype(jnp.bfloat16)
+    half = width // 2
+    arrived = []
+    for lo in (0, half):
+        outgoing = lax.dot_general(
+            dispatch, moe_rows[:, lo:lo + half], (((0,), (0,)), ((), ())),
+            preferred_element_type=jnp.float32,
+        ).astype(jnp.bfloat16).reshape(experts, capacity, half)
+        arrived.append(
+            lax.all_to_all(outgoing, "dev", split_axis=0, concat_axis=0, tiled=True).reshape(slot_count, half)
+        )
+    own = (w_gate[0], w_up[0], w_down[0])
+    other = tuple(other_half(w) for w in own)
+    partials = [gate_up_partial(arrived[0], w[0], w[1]) for w in (own, other)]
+    h0, h1 = [gate_up_finish(arrived[1], w[0], w[1], p) for w, p in zip((own, other), partials)]
+    pick_matrix = picks.astype(jnp.bfloat16)
+    picked = []
+    for lo in (0, half):
+        finished = down_columns(h0, h1, own[2], other[2], lo, half)
+        returned = lax.all_to_all(
+            finished.reshape(experts, capacity, half), "dev", split_axis=0, concat_axis=0, tiled=True
+        )
+        picked.append(jnp.dot(pick_matrix, returned.reshape(slot_count, half), preferred_element_type=jnp.float32))
+    picked = jnp.concatenate(picked, axis=1).reshape(tok_count, topk_count, width)
     moe_out = jnp.sum(picked * gate_weights[:, :, None], axis=1).astype(jnp.bfloat16)
     attended = jax.vmap(attend_row)(q_latent, q_rope, latent_cache, rope_cache, lengths)
     return (moe_out, attended)

time: 151 us -> 165 us (1.093)
  waiting for transfers between devices: 80.3 us -> 67.7 us
  starting transfers between devices: 20.8 us -> 29.3 us
  Pallas kernels: 22.6 us -> 30.8 us
  matrix products: 22.9 us -> 26.7 us
  local copies, waits for them, and re-layouts: 3.06 us -> 6.45 us
  other arithmetic: 0.33 us -> 2.18 us
    all_to_all x1 -> x2, waiting for transfers between devices: 33.7 us -> 22 us  [per_device(): lax.all_to_all(finished.reshape(experts, capacity, half), 'dev', split_ax...]
    pallas_call x3 -> x6, Pallas kernels: 22.6 us -> 30.8 us  [the longest x2 14.3 us: down_columns(): pl.pallas_call(down_kernel, out_shape=jax.ShapeDtypeStruct((count, count_...]
    all_to_all x1 -> x2, starting transfers between devices: 11.7 us -> 17.4 us  [per_device(): lax.all_to_all(outgoing, 'dev', split_axis=0, concat_axis=0, tiled=True)]
    unnamed x14 -> x24, local copies, waits for them, and re-layouts: 2.78 us -> 6.16 us
    all_to_all x1 -> x2, starting transfers between devices: 8.39 us -> 11.3 us  [per_device(): lax.all_to_all(finished.reshape(experts, capacity, half), 'dev', split_ax...]
    reduce_sum x0 -> x1, other arithmetic: none -> 1.85 us  [per_device(): jnp.sum(picked * gate_weights[:, :, None], axis=1).astype(jnp.bfloat16)]
    all_to_all x1 -> x2, waiting for transfers between devices: 46.6 us -> 45.6 us  [per_device(): lax.all_to_all(outgoing, 'dev', split_axis=0, concat_axis=0, tiled=True)]
    dot_general x2 -> x4, matrix products: 8 us -> 8.9 us  [the longest x2 4.78 us: per_device(): lax.dot_general(dispatch, moe_rows[:, lo:lo + half], (((0,), (0,)), ((),...]
  transfers between devices with their start and end apart: 5 -> 7, of which waited for: 2 -> 4; matrix products, arithmetic and copies ran while one was open for 10% -> 14% of each run, Pallas kernels for 10% -> 14%
where the time goes in v8:
time: 165 us; the launch traced here: 164 us
  waiting for transfers between devices  67.7 us (41%)
  Pallas kernels  30.8 us (19%)
  starting transfers between devices  29.3 us (18%)
  matrix products  26.7 us (16%)
  local copies, waits for them, and re-layouts  6.45 us (4%)
  other arithmetic  2.18 us (1%)
    all_to_all x2, waiting for transfers between devices, per_device(): lax.all_to_all(outgoing, 'dev', split_axis=0, concat_axis=0, tiled=True)  45.6 us
    all_to_all x2, waiting for transfers between devices, per_device(): lax.all_to_all(finished.reshape(experts, capacity, half), 'dev', split_ax...  22 us
    all_to_all x2, starting transfers between devices, per_device(): lax.all_to_all(outgoing, 'dev', split_axis=0, concat_axis=0, tiled=True)  17.4 us
    pallas_call x2, Pallas kernels, down_columns(): pl.pallas_call(down_kernel, out_shape=jax.ShapeDtypeStruct((count, count_...  14.3 us
    all_to_all x2, starting transfers between devices, per_device(): lax.all_to_all(finished.reshape(experts, capacity, half), 'dev', split_ax...  11.3 us
    pallas_call x2, Pallas kernels, gate_up_finish(): pl.pallas_call(finish_kernel, out_shape=jax.ShapeDtypeStruct((count, unit...  8.8 us
    pallas_call x2, Pallas kernels, gate_up_partial(): pl.pallas_call(partial_kernel, out_shape=(part, part), grid=(units // uni...  7.72 us
    dot_general x1, matrix products, attend_row(): lax.dot_general(query_lat, cache_lat, (((1,), (1,)), ((), ())), preferred...  7.34 us
  transfers between devices with their start and end apart: 7, of which 4 were waited for; matrix products, arithmetic and copies ran while one was open for 14% of the time, Pallas kernels for 14%

profile of v8, /device:TPU:0, one launch (start us, length us, event | category | flops | bytes accessed | tf_op | source)
XLA Modules:
  0.0 163.9 jit_solution(16868159088115215807)
XLA Ops:
  0.6 0.0 copy-start
  0.6 0.8 copy.18
  1.5 0.1 reshape.78
  1.6 0.2 fusion.14
  1.8 0.1 convert_element_type.31
  1.9 0.2 fusion.16
  2.1 2.8 %fusion.5 = bf16[64,8,1792]{2,1,0:T(8,128)(2,1)} fusion(pred[32,512]{1,0:T(8,128)(4,1)S(1)} %fusion.16, bf16[32,3584]{1,0:T(8,128)(2,1)} %param.11), kind=kOutput, calls=%fused_computation.8 | convolution fusion | flops 59637760 | bytes 1966080 | tf_op jit(solution)/shard_map/dot_general | solution.py:162
  5.0 0.0 copy-start.7
  5.0 11.6 %all-to-all-start.1 = ((bf16[64,8,1792]{2,1,0:T(8,128)(2,1)}), bf16[64,8,1792]{2,1,0:T(8,128)(2,1)S(1)}, u32[]{:S(2)}, u32[]{:S(2)}) async-start(bf16[64,8,1792]{2,1,0:T(8,128)(2,1)} %fusion.5), calls=%async_computation.1 | async-start | bytes 3670016 | tf_op jit(solution)/shard_map/all_to_all | solution.py:167
  16.6 0.1 collective-permute-start
  16.7 0.5 collective-permute-start.1
  17.2 0.1 collective-permute-start.2
  17.3 0.0 copy-done.7
  17.3 1.9 %fusion.4 = bf16[64,8,1792]{2,1,0:T(8,128)(2,1)} fusion(pred[32,512]{1,0:T(8,128)(4,1)S(1)} %fusion.16, bf16[32,3584]{1,0:T(8,128)(2,1)S(1)} %copy-done.7), kind=kOutput, calls=%fused_computation.7 | convolution fusion | flops 59637760 | bytes 1966080 | tf_op jit(solution)/shard_map/dot_general | solution.py:162
  19.3 24.6 %all-to-all-done.1 = bf16[64,8,1792]{2,1,0:T(8,128)(2,1)S(1)} async-done(((bf16[64,8,1792]{2,1,0:T(8,128)(2,1)}), bf16[64,8,1792]{2,1,0:T(8,128)(2,1)S(1)}, u32[]{:S(2)}, u32[]{:S(2)}) %all-to-all-start.1) | async-done | bytes 1835040 | tf_op jit(solution)/shard_map/all_to_all | solution.py:167
  43.8 5.8 %all-to-all-start = ((bf16[64,8,1792]{2,1,0:T(8,128)(2,1)}), bf16[64,8,1792]{2,1,0:T(8,128)(2,1)}, u32[]{:S(2)}, u32[]{:S(2)}) async-start(bf16[64,8,1792]{2,1,0:T(8,128)(2,1)} %fusion.4), calls=%async_computation | async-start | bytes 3670016 | tf_op jit(solution)/shard_map/all_to_all | solution.py:167
  49.6 3.8 %shard_map.122 = (f32[512,512]{1,0:T(8,128)S(1)}, f32[512,512]{1,0:T(8,128)S(1)}) custom-call(bf16[512,1792]{1,0:T(8,128)(2,1)S(1)} %bitcast.30, bf16[3584,512]{1,0:T(8,128)(2,1)} %bitcast.33, bf16[3584,512]{1,0:T(8,128)(2,1)} %bitcast.36), custom_call_target="tpu_custom_call" | custom-call | flops 1879048192 | bytes 7602176 | tf_op jit(solution)/shard_map/pallas_call | solution.py:36
  53.4 0.0 copy-start.1
  53.5 1.0 copy-done.1
  54.4 0.0 copy-start.3
  54.4 1.0 copy-done.3
  55.4 21.0 %all-to-all-done = bf16[64,8,1792]{2,1,0:T(8,128)(2,1)} async-done(((bf16[64,8,1792]{2,1,0:T(8,128)(2,1)}), bf16[64,8,1792]{2,1,0:T(8,128)(2,1)}, u32[]{:S(2)}, u32[]{:S(2)}) %all-to-all-start) | async-done | bytes 1835040 | tf_op jit(solution)/shard_map/all_to_all | solution.py:167
  76.4 0.0 copy-start.2
  76.4 1.2 copy-done.2
  77.7 0.0 copy-start.4
  77.7 1.2 copy-done.4
  78.9 4.4 %shard_map.123.h0_ref = bf16[512,512]{1,0:T(8,128)(2,1)S(1)} custom-call(bf16[512,1792]{1,0:T(8,128)(2,1)} %bitcast.1.x_ref, bf16[3584,512]{1,0:T(8,128)(2,1)} %bitcast.34, bf16[3584,512]{1,0:T(8,128)(2,1)} %bitcast.37, f32[512,512]{1,0:T(8,128)S(1)} %copy-done.2, f32[512,512]{1,0:T(8,128)S(1)} %copy-done.4), custom_call_target="tpu_custom_call" | custom-call | flops 1879048192 | bytes 8126464 | tf_op jit(solution)/shard_map/pallas_call | solution.py:59
  83.3 0.0 collective-permute-done.g_ref
  83.3 0.0 collective-permute-done.1.u_ref
  83.3 3.9 %shard_map.124 = (f32[512,512]{1,0:T(8,128)S(1)}, f32[512,512]{1,0:T(8,128)S(1)}) custom-call(bf16[512,1792]{1,0:T(8,128)(2,1)S(1)} %bitcast.31, bf16[3584,512]{1,0:T(8,128)(2,1)} %collective-permute-done.g_ref, bf16[3584,512]{1,0:T(8,128)(2,1)} %collective-permute-done.1.u_ref), custom_call_target="tpu_custom_call" | custom-call | flops 1879048192 | bytes 7602176 | tf_op jit(solution)/shard_map/pallas_call | solution.py:36
  87.2 4.4 %shard_map.125.h1_ref = bf16[512,512]{1,0:T(8,128)(2,1)S(1)} custom-call(bf16[512,1792]{1,0:T(8,128)(2,1)} %bitcast.1.x_ref, bf16[3584,512]{1,0:T(8,128)(2,1)} %collective-permute-done.g_ref, bf16[3584,512]{1,0:T(8,128)(2,1)} %collective-permute-done.1.u_ref, f32[512,512]{1,0:T(8,128)S(1)} %get-tuple-element.8.pg_ref, f32[512,512]{1,0:T(8,128)S(1)} %get-tuple-element.9.pu_ref), custom_call_target="tpu_custom_call" | custom-call | flops 1879048192 | bytes 8126464 | tf_op jit(solution)/shard_map/pallas_call | solution.py:59
  91.6 0.0 collective-permute-done.2.d1_ref
  91.6 7.2 %shard_map.127 = bf16[512,1792]{1,0:T(8,128)(2,1)} custom-call(bf16[512,512]{1,0:T(8,128)(2,1)S(1)} %shard_map.123.h0_ref, bf16[512,512]{1,0:T(8,128)(2,1)S(1)} %shard_map.125.h1_ref, bf16[3584,512]{1,0:T(8,128)(2,1)} %bitcast.39, bf16[3584,512]{1,0:T(8,128)(2,1)} %collective-permute-done.2.d1_ref), custom_call_target="tpu_custom_call" | custom-call | flops 1879048192 | bytes 6553600 | tf_op jit(solution)/shard_map/pallas_call | solution.py:83
  98.8 0.0 copy-start.9
  98.8 0.0 copy-start.8
  98.8 0.0 copy-start.6
  98.8 5.8 %all-to-all-start.3 = ((bf16[64,8,1792]{2,1,0:T(8,128)(2,1)}), bf16[64,8,1792]{2,1,0:T(8,128)(2,1)}, u32[]{:S(2)}, u32[]{:S(2)}) async-start(bf16[64,8,1792]{2,1,0:T(8,128)(2,1)} %bitcast.9), calls=%async_computation.3 | async-start | bytes 3670016 | tf_op jit(solution)/shard_map/all_to_all | solution.py:177
  104.6 0.0 copy-done.9
  104.6 0.1 copy.20
  104.7 0.0 copy-done.8
  104.7 0.1 reshape.88
  104.8 0.0 copy-done.6
  104.9 7.3 %fusion.23 = f32[4,64,2048]{2,1,0:T(8,128)} fusion(bf16[4,64,512]{2,1,0:T(8,128)(2,1)S(1)} %copy-done.6, bf16[4,2048,512]{2,1,0:T(8,128)(2,1)} %param.19), kind=kOutput, calls=%fused_computation.37 | convolution fusion | flops 536870912 | bytes 10747904 | tf_op jit(solution)/shard_map/vmap()/dot_general | solution.py:113
  112.2 7.1 %shard_map.126 = bf16[512,1792]{1,0:T(8,128)(2,1)} custom-call(bf16[512,512]{1,0:T(8,128)(2,1)S(1)} %shard_map.123.h0_ref, bf16[512,512]{1,0:T(8,128)(2,1)S(1)} %shard_map.125.h1_ref, bf16[3584,512]{1,0:T(8,128)(2,1)} %bitcast.40, bf16[3584,512]{1,0:T(8,128)(2,1)} %collective-permute-done.2.d1_ref), custom_call_target="tpu_custom_call" | custom-call | flops 1879048192 | bytes 6553600 | tf_op jit(solution)/shard_map/pallas_call | solution.py:83
  119.3 0.0 copy-start.10
  119.3 11.2 %all-to-all-done.3 = bf16[64,8,1792]{2,1,0:T(8,128)(2,1)} async-done(((bf16[64,8,1792]{2,1,0:T(8,128)(2,1)}), bf16[64,8,1792]{2,1,0:T(8,128)(2,1)}, u32[]{:S(2)}, u32[]{:S(2)}) %all-to-all-start.3) | async-done | bytes 1835040 | tf_op jit(solution)/shard_map/all_to_all | solution.py:177
  130.5 5.4 %all-to-all-start.2 = ((bf16[64,8,1792]{2,1,0:T(8,128)(2,1)}), bf16[64,8,1792]{2,1,0:T(8,128)(2,1)S(1)}, u32[]{:S(2)}, u32[]{:S(2)}) async-start(bf16[64,8,1792]{2,1,0:T(8,128)(2,1)} %bitcast.7), calls=%async_computation.2 | async-start | bytes 3670016 | tf_op jit(solution)/shard_map/all_to_all | solution.py:177
  135.9 0.0 copy-done.10
  135.9 0.1 iota_compare_fusion.8
  136.0 0.0 copy-done
  136.0 3.9 %fusion.22 = (f32[4,64]{1,0:T(4,128)S(1)}, f32[4,64,2048]{2,1,0:T(8,128)}) fusion(pred[4,2048]{1,0:T(4,128)(4,1)S(1)} %iota_compare_fusion.8, f32[4,64,2048]{2,1,0:T(8,128)} %fusion.23, bf16[4,64,64]{2,1,0:T(8,128)(2,1)S(1)} %reshape.88, bf16[4,64,2048]{2,1,0:T(8,128)(2,1)S(1)} %copy-done), kind=kOutput, calls=%fused_computation.36 | convolution fusion | flops 70256640 | bytes 5284864 | tf_op jit(solution)/shard_map/vmap()/sub | solution.py:124
  139.9 6.3 %convolution_convert_fusion.2 = bf16[4,64,512]{2,1,0:T(8,128)(2,1)} fusion(bf16[4,2048,512]{2,1,0:T(8,128)(2,1)} %param.19, f32[4,64,2048]{2,1,0:T(8,128)} %get-tuple-element.11, f32[4,64]{1,0:T(4,128)S(1)} %get-tuple-element.10), kind=kOutput, calls=%fused_computation.19 | convolution fusion | flops 538050560 | bytes 10748928 | tf_op jit(solution)/shard_map/vmap()/dot_general | solution.py:126
  146.2 3.4 %fusion.10 = f32[256,1792]{1,0:T(8,128)} fusion(bf16[64,8,1792]{2,1,0:T(8,128)(2,1)} %all-to-all-done.3, s32[256]{0:T(256)S(1)} %multiply_add_fusion.1), kind=kOutput, calls=%fused_computation.15 | convolution fusion | flops 469893120 | bytes 3671040 | tf_op jit(solution)/shard_map/dot_general | solution.py:180
  149.7 10.9 %all-to-all-done.2 = bf16[64,8,1792]{2,1,0:T(8,128)(2,1)S(1)} async-done(((bf16[64,8,1792]{2,1,0:T(8,128)(2,1)}), bf16[64,8,1792]{2,1,0:T(8,128)(2,1)S(1)}, u32[]{:S(2)}, u32[]{:S(2)}) %all-to-all-start.2) | async-done | bytes 1835040 | tf_op jit(solution)/shard_map/all_to_all | solution.py:177
  160.5 0.0 copy-start.5
  160.5 0.7 fusion.12
  161.2 0.8 copy-done.5
  162.0 1.8 %fusion.2 = bf16[32,3584]{1,0:T(8,128)(2,1)} fusion(f32[256,1792]{1,0:T(8,128)S(1)} %copy-done.5, f32[256,1792]{1,0:T(8,128)S(1)} %fusion.12, f32[32,8]{1,0:T(8,128)S(1)} %copy.20), kind=kLoop, calls=%fused_computation.3 | loop fusion | flops 2637824 | bytes 3900416 | tf_op jit(solution)/shard_map/reduce_sum | solution.py:182
  (3 shorter events, 0.0 us)
Async XLA Ops:
  0.6 135.4 %copy-start = (bf16[4,64,2048]{2,1,0:T(8,128)(2,1)S(1)}, bf16[4,64,2048]{2,1,0:T(8,128)(2,1)}, u32[]{:S(2)}) copy-start(bf16[4,64,2048]{2,1,0:T(8,128)(2,1)} %param.20) | copy-start | bytes 3145732
  5.0 12.3 %copy-start.7 = (bf16[32,3584]{1,0:T(8,128)(2,1)S(1)}, bf16[32,3584]{1,0:T(8,128)(2,1)}, u32[]{:S(2)}) copy-start(bf16[32,3584]{1,0:T(8,128)(2,1)} %param.11) | copy-start | bytes 688132
  5.0 38.8 %all-to-all-start.1 = ((bf16[64,8,1792]{2,1,0:T(8,128)(2,1)}), bf16[64,8,1792]{2,1,0:T(8,128)(2,1)S(1)}, u32[]{:S(2)}, u32[]{:S(2)}) async-start(bf16[64,8,1792]{2,1,0:T(8,128)(2,1)} %fusion.5), calls=%async_computation.1 | async-start | bytes 3670016 | tf_op jit(solution)/shard_map/all_to_all | solution.py:167
  16.6 66.7 %collective-permute-start = (bf16[3584,512]{1,0:T(8,128)(2,1)}, bf16[3584,512]{1,0:T(8,128)(2,1)}, u32[]{:S(2)}, u32[]{:S(2)}) collective-permute-start(bf16[3584,512]{1,0:T(8,128)(2,1)} %bitcast.32), channel_id=1, source_target_pairs={{0,64},{64,0},{1,65},{65,1},{2,66},{66,2},{3,67},{67,3},{4,68},{68... | collective-permute-start | bytes 11010056 | tf_op jit(solution)/shard_map/ppermute | solution.py:104
  16.7 66.6 %collective-permute-start.1 = (bf16[3584,512]{1,0:T(8,128)(2,1)}, bf16[3584,512]{1,0:T(8,128)(2,1)}, u32[]{:S(2)}, u32[]{:S(2)}) collective-permute-start(bf16[3584,512]{1,0:T(8,128)(2,1)} %bitcast.35), channel_id=1, source_target_pairs={{0,64},{64,0},{1,65},{65,1},{2,66},{66,2},{3,67},{67,3},{4,68},{68... | collective-permute-start | bytes 11010056 | tf_op jit(solution)/shard_map/ppermute | solution.py:104
  17.2 74.4 %collective-permute-start.2 = (bf16[3584,512]{1,0:T(8,128)(2,1)}, bf16[3584,512]{1,0:T(8,128)(2,1)}, u32[]{:S(2)}, u32[]{:S(2)}) collective-permute-start(bf16[3584,512]{1,0:T(8,128)(2,1)} %bitcast.38), channel_id=1, source_target_pairs={{0,64},{64,0},{1,65},{65,1},{2,66},{66,2},{3,67},{67,3},{4,68},{68... | collective-permute-start | bytes 11010056 | tf_op jit(solution)/shard_map/ppermute | solution.py:104
  43.8 32.6 %all-to-all-start = ((bf16[64,8,1792]{2,1,0:T(8,128)(2,1)}), bf16[64,8,1792]{2,1,0:T(8,128)(2,1)}, u32[]{:S(2)}, u32[]{:S(2)}) async-start(bf16[64,8,1792]{2,1,0:T(8,128)(2,1)} %fusion.4), calls=%async_computation | async-start | bytes 3670016 | tf_op jit(solution)/shard_map/all_to_all | solution.py:167
  53.4 1.0 copy-start.1
  54.4 1.0 copy-start.3
  76.4 1.2 copy-start.2
  77.7 1.2 copy-start.4
  98.8 5.8 %copy-start.9 = (f32[32,8]{0,1:T(8,128)S(1)}, f32[32,8]{0,1:T(8,128)}, u32[]{:S(2)}) copy-start(f32[32,8]{0,1:T(8,128)} %param.13) | copy-start | bytes 3076
  98.8 5.9 %copy-start.8 = (bf16[4,4096]{1,0:T(4,128)(2,1)S(1)}, bf16[4,4096]{1,0:T(4,128)(2,1)}, u32[]{:S(2)}) copy-start(bf16[4,4096]{1,0:T(4,128)(2,1)} %param.18) | copy-start | bytes 98308
  98.8 6.1 %copy-start.6 = (bf16[4,64,512]{2,1,0:T(8,128)(2,1)S(1)}, bf16[4,64,512]{2,1,0:T(8,128)(2,1)}, u32[]{:S(2)}) copy-start(bf16[4,64,512]{2,1,0:T(8,128)(2,1)} %param.17) | copy-start | bytes 786436
  98.8 31.7 %all-to-all-start.3 = ((bf16[64,8,1792]{2,1,0:T(8,128)(2,1)}), bf16[64,8,1792]{2,1,0:T(8,128)(2,1)}, u32[]{:S(2)}, u32[]{:S(2)}) async-start(bf16[64,8,1792]{2,1,0:T(8,128)(2,1)} %bitcast.9), calls=%async_computation.3 | async-start | bytes 3670016 | tf_op jit(solution)/shard_map/all_to_all | solution.py:177
  119.3 16.6 %copy-start.10 = (s32[4]{0:T(128)S(1)}, s32[4]{0:T(128)}, u32[]{:S(2)}) copy-start(s32[4]{0:T(128)} %param.21) | copy-start | bytes 52
  130.5 30.1 %all-to-all-start.2 = ((bf16[64,8,1792]{2,1,0:T(8,128)(2,1)}), bf16[64,8,1792]{2,1,0:T(8,128)(2,1)S(1)}, u32[]{:S(2)}, u32[]{:S(2)}) async-start(bf16[64,8,1792]{2,1,0:T(8,128)(2,1)} %bitcast.7), calls=%async_computation.2 | async-start | bytes 3670016 | tf_op jit(solution)/shard_map/all_to_all | solution.py:177
  160.5 1.5 copy-start.5

commit v9 on v6

--- a/solution.py
+++ b/solution.py
@@ -131,10 +131,11 @@
     destination = flat_ids * capacity + slot_index
     slot_iota = jnp.arange(slot_count, dtype=jnp.int32)
     picks = destination[:, None] == slot_iota[None, :]
-    dispatch = jnp.any(picks.reshape(tok_count, topk_count, slot_count), axis=1)
-    outgoing = lax.dot_general(
-        dispatch.astype(jnp.bfloat16), moe_rows, (((0,), (0,)), ((), ())),
-        preferred_element_type=jnp.float32,
+    dispatch = jnp.any(
+        destination.reshape(tok_count, topk_count)[None, :, :] == slot_iota[:, None, None], axis=2
+    )
+    outgoing = jnp.dot(
+        dispatch.astype(jnp.bfloat16), moe_rows, preferred_element_type=jnp.float32
     ).astype(jnp.bfloat16).reshape(experts, capacity, width)
     arrived = lax.all_to_all(outgoing, "dev", split_axis=0, concat_axis=0, tiled=True)
     own_rows = arrived.reshape(experts * capacity, width)
@@ -142,10 +143,14 @@
     finished = expert_sum.reshape(experts, capacity, width)
     returned = lax.all_to_all(finished, "dev", split_axis=0, concat_axis=0, tiled=True)
     flat_back = returned.reshape(slot_count, width)
-    picked = jnp.dot(
-        picks.astype(jnp.bfloat16), flat_back, preferred_element_type=jnp.float32
-    ).reshape(tok_count, topk_count, width)
-    moe_out = jnp.sum(picked * gate_weights[:, :, None], axis=1).astype(jnp.bfloat16)
+    weighted = jnp.sum(
+        jnp.where(picks, gate_weights.reshape(pair_count)[:, None], 0.0).reshape(tok_count, topk_count, slot_count),
+        axis=1,
+    )
+    moe_out = jnp.dot(
+        weighted, flat_back.astype(jnp.float32), precision=lax.Precision.HIGHEST,
+        preferred_element_type=jnp.float32,
+    ).astype(jnp.bfloat16)
     attended = jax.vmap(attend_row)(q_latent, q_rope, latent_cache, rope_cache, lengths)
     return (moe_out, attended)
 

time: 151 us -> 152 us (level)
  no operation moved by 1% of the time
where the time goes in v9:
time: 152 us; the launch traced here: 151 us
  waiting for transfers between devices  80 us (53%)
  matrix products  23.5 us (15%)
  Pallas kernels  22.6 us (15%)
  starting transfers between devices  20.8 us (14%)
  local copies, waits for them, and re-layouts  3.06 us (2%)
    all_to_all x1, waiting for transfers between devices, per_device(): lax.all_to_all(outgoing, 'dev', split_axis=0, concat_axis=0, tiled=True)  46.6 us
    all_to_all x1, waiting for transfers between devices, per_device(): lax.all_to_all(finished, 'dev', split_axis=0, concat_axis=0, tiled=True)  33.4 us
    pallas_call x2, Pallas kernels, gate_up(): pl.pallas_call(gate_up_kernel, out_shape=jax.ShapeDtypeStruct((count, uni...  14.7 us
    all_to_all x1, starting transfers between devices, per_device(): lax.all_to_all(outgoing, 'dev', split_axis=0, concat_axis=0, tiled=True)  11.7 us
    all_to_all x1, starting transfers between devices, per_device(): lax.all_to_all(finished, 'dev', split_axis=0, concat_axis=0, tiled=True)  8.39 us
    pallas_call x1, Pallas kernels, down(): pl.pallas_call(down_kernel, out_shape=jax.ShapeDtypeStruct((count, width)...  7.92 us
    dot_general x1, matrix products, attend_row(): jnp.dot(probs, cache_lat, preferred_element_type=jnp.float32)  6.34 us
    dot_general x1, matrix products, attend_row(): lax.dot_general(query_lat, cache_lat, (((1,), (1,)), ((), ())), preferred...  6 us
  transfers between devices with their start and end apart: 5, of which 2 were waited for; matrix products, arithmetic and copies ran while one was open for 10% of the time, Pallas kernels for 10%

profile of v9, /device:TPU:0, one launch (start us, length us, event | category | flops | bytes accessed | tf_op | source)
XLA Modules:
  0.0 151.3 jit_solution(11033047509819788419)
XLA Ops:
  0.6 0.0 copy-start
  0.6 0.8 copy.19
  1.5 0.1 eq.42
  1.6 0.2 fusion.8
  1.8 0.1 convert_element_type.29
  1.9 0.2 fusion.10
  2.1 3.9 %fusion.1 = bf16[64,8,3584]{2,1,0:T(8,128)(2,1)} fusion(pred[512,32]{0,1:T(8,128)(4,1)S(1)} %fusion.10, bf16[32,3584]{1,0:T(8,128)(2,1)} %param.11), kind=kOutput, calls=%fused_computation.2 | convolution fusion | flops 119275520 | bytes 3915776 | tf_op jit(solution)/shard_map/dot_general | solution.py:137
  6.1 11.7 %all-to-all-start = ((bf16[64,8,3584]{2,1,0:T(8,128)(2,1)}), bf16[64,8,3584]{2,1,0:T(8,128)(2,1)}, u32[]{:S(2)}, u32[]{:S(2)}) async-start(bf16[64,8,3584]{2,1,0:T(8,128)(2,1)} %fusion.1), calls=%async_computation | async-start | bytes 7340032 | tf_op jit(solution)/shard_map/all_to_all | solution.py:140
  17.8 0.1 collective-permute-start
  17.9 0.5 collective-permute-start.1
  18.4 0.1 collective-permute-start.2
  18.5 46.6 %all-to-all-done = bf16[64,8,3584]{2,1,0:T(8,128)(2,1)} async-done(((bf16[64,8,3584]{2,1,0:T(8,128)(2,1)}), bf16[64,8,3584]{2,1,0:T(8,128)(2,1)}, u32[]{:S(2)}, u32[]{:S(2)}) %all-to-all-start) | async-done | bytes 3670048 | tf_op jit(solution)/shard_map/all_to_all | solution.py:140
  65.1 7.3 %shard_map.122.h0_ref = bf16[512,512]{1,0:T(8,128)(2,1)S(1)} custom-call(bf16[512,3584]{1,0:T(8,128)(2,1)} %bitcast.1.x_ref, bf16[3584,512]{1,0:T(8,128)(2,1)} %bitcast.20, bf16[3584,512]{1,0:T(8,128)(2,1)} %bitcast.22), custom_call_target="tpu_custom_call" | custom-call | flops 3758096384 | bytes 11534336 | tf_op jit(solution)/shard_map/pallas_call | solution.py:29
  72.4 0.0 collective-permute-done.g_ref
  72.5 0.0 collective-permute-done.1.u_ref
  72.5 7.4 %shard_map.123.h1_ref = bf16[512,512]{1,0:T(8,128)(2,1)S(1)} custom-call(bf16[512,3584]{1,0:T(8,128)(2,1)} %bitcast.1.x_ref, bf16[3584,512]{1,0:T(8,128)(2,1)} %collective-permute-done.g_ref, bf16[3584,512]{1,0:T(8,128)(2,1)} %collective-permute-done.1.u_ref), custom_call_target="tpu_custom_call" | custom-call | flops 3758096384 | bytes 11534336 | tf_op jit(solution)/shard_map/pallas_call | solution.py:29
  79.8 0.0 collective-permute-done.2.d1_ref
  79.9 7.9 %shard_map.124 = bf16[512,3584]{1,0:T(8,128)(2,1)S(1)} custom-call(bf16[512,512]{1,0:T(8,128)(2,1)S(1)} %shard_map.122.h0_ref, bf16[512,512]{1,0:T(8,128)(2,1)S(1)} %shard_map.123.h1_ref, bf16[3584,512]{1,0:T(8,128)(2,1)} %bitcast.24, bf16[3584,512]{1,0:T(8,128)(2,1)} %collective-permute-done.2.d1_ref), custom_call_target="tpu_custom_call" | custom-call | flops 3758096384 | bytes 12058624 | tf_op jit(solution)/shard_map/pallas_call | solution.py:51
  87.8 0.0 copy-start.1
  87.8 1.8 %copy-done.1 = bf16[512,3584]{1,0:T(8,128)(2,1)} copy-done((bf16[512,3584]{1,0:T(8,128)(2,1)}, bf16[512,3584]{1,0:T(8,128)(2,1)S(1)}, u32[]{:S(2)}) %copy-start.1) | copy-done | bytes 3670040
  89.6 0.0 copy-start.4
  89.6 0.0 copy-start.3
  89.6 0.0 copy-start.5
  89.6 0.0 copy-start.2
  89.6 8.4 %all-to-all-start.1 = ((bf16[64,8,3584]{2,1,0:T(8,128)(2,1)}), bf16[64,8,3584]{2,1,0:T(8,128)(2,1)}, u32[]{:S(2)}, u32[]{:S(2)}) async-start(bf16[64,8,3584]{2,1,0:T(8,128)(2,1)} %bitcast.18), calls=%async_computation.1 | async-start | bytes 7340032 | tf_op jit(solution)/shard_map/all_to_all | solution.py:144
  98.0 0.0 copy-done.4
  98.0 0.1 copy.21
  98.1 0.0 copy-done.3
  98.1 0.1 reshape.76
  98.2 0.2 select_reduce_fusion
  98.5 0.0 copy-done.5
  98.5 0.1 iota_compare_fusion.6
  98.6 0.0 copy-done.2
  98.6 6.0 %fusion.13 = f32[4,64,2048]{2,1,0:T(8,128)S(1)} fusion(bf16[4,64,512]{2,1,0:T(8,128)(2,1)S(1)} %copy-done.2, bf16[4,2048,512]{2,1,0:T(8,128)(2,1)} %param.19), kind=kOutput, calls=%fused_computation.26 | convolution fusion | flops 536870912 | bytes 10747904 | tf_op jit(solution)/shard_map/vmap()/dot_general | solution.py:89
  104.6 0.0 copy-done
  104.6 2.4 %fusion.12 = (f32[4,64]{1,0:T(4,128)S(1)}, f32[4,64,2048]{2,1,0:T(8,128)}) fusion(pred[4,2048]{1,0:T(4,128)(4,1)S(1)} %iota_compare_fusion.6, f32[4,64,2048]{2,1,0:T(8,128)S(1)} %fusion.13, bf16[4,64,64]{2,1,0:T(8,128)(2,1)S(1)} %reshape.76, bf16[4,64,2048]{2,1,0:T(8,128)(2,1)S(1)} %copy-done), kind=kOutput, calls=%fused_computation.25 | convolution fusion | flops 70256640 | bytes 5284864 | tf_op jit(solution)/shard_map/vmap()/sub | solution.py:100
  106.9 6.3 %convolution_convert_fusion.2 = bf16[4,64,512]{2,1,0:T(8,128)(2,1)} fusion(bf16[4,2048,512]{2,1,0:T(8,128)(2,1)} %param.19, f32[4,64,2048]{2,1,0:T(8,128)} %get-tuple-element.3, f32[4,64]{1,0:T(4,128)S(1)} %get-tuple-element.2), kind=kOutput, calls=%fused_computation.12 | convolution fusion | flops 538050560 | bytes 10748928 | tf_op jit(solution)/shard_map/vmap()/dot_general | solution.py:102
  113.3 33.4 %all-to-all-done.1 = bf16[64,8,3584]{2,1,0:T(8,128)(2,1)} async-done(((bf16[64,8,3584]{2,1,0:T(8,128)(2,1)}), bf16[64,8,3584]{2,1,0:T(8,128)(2,1)}, u32[]{:S(2)}, u32[]{:S(2)}) %all-to-all-start.1) | async-done | bytes 3670048 | tf_op jit(solution)/shard_map/all_to_all | solution.py:144
  146.7 4.6 %convolution_convert_fusion.1 = bf16[32,3584]{1,0:T(8,128)(2,1)} fusion(f32[32,512]{1,0:T(8,128)S(1)} %select_reduce_fusion, bf16[64,8,3584]{2,1,0:T(8,128)(2,1)} %all-to-all-done.1), kind=kOutput, calls=%fused_computation.3 | convolution fusion | flops 704757760 | bytes 3964928 | tf_op jit(solution)/shard_map/dot_general | solution.py:150
  (2 shorter events, 0.0 us)
Async XLA Ops:
  0.6 104.0 %copy-start = (bf16[4,64,2048]{2,1,0:T(8,128)(2,1)S(1)}, bf16[4,64,2048]{2,1,0:T(8,128)(2,1)}, u32[]{:S(2)}) copy-start(bf16[4,64,2048]{2,1,0:T(8,128)(2,1)} %param.20) | copy-start | bytes 3145732
  6.1 59.0 %all-to-all-start = ((bf16[64,8,3584]{2,1,0:T(8,128)(2,1)}), bf16[64,8,3584]{2,1,0:T(8,128)(2,1)}, u32[]{:S(2)}, u32[]{:S(2)}) async-start(bf16[64,8,3584]{2,1,0:T(8,128)(2,1)} %fusion.1), calls=%async_computation | async-start | bytes 7340032 | tf_op jit(solution)/shard_map/all_to_all | solution.py:140
  17.8 54.6 %collective-permute-start = (bf16[3584,512]{1,0:T(8,128)(2,1)}, bf16[3584,512]{1,0:T(8,128)(2,1)}, u32[]{:S(2)}, u32[]{:S(2)}) collective-permute-start(bf16[3584,512]{1,0:T(8,128)(2,1)} %bitcast.19), channel_id=1, source_target_pairs={{0,64},{64,0},{1,65},{65,1},{2,66},{66,2},{3,67},{67,3},{4,68},{68... | collective-permute-start | bytes 11010056 | tf_op jit(solution)/shard_map/ppermute | solution.py:72
  17.9 54.5 %collective-permute-start.1 = (bf16[3584,512]{1,0:T(8,128)(2,1)}, bf16[3584,512]{1,0:T(8,128)(2,1)}, u32[]{:S(2)}, u32[]{:S(2)}) collective-permute-start(bf16[3584,512]{1,0:T(8,128)(2,1)} %bitcast.21), channel_id=1, source_target_pairs={{0,64},{64,0},{1,65},{65,1},{2,66},{66,2},{3,67},{67,3},{4,68},{68... | collective-permute-start | bytes 11010056 | tf_op jit(solution)/shard_map/ppermute | solution.py:72
  18.4 61.4 %collective-permute-start.2 = (bf16[3584,512]{1,0:T(8,128)(2,1)}, bf16[3584,512]{1,0:T(8,128)(2,1)}, u32[]{:S(2)}, u32[]{:S(2)}) collective-permute-start(bf16[3584,512]{1,0:T(8,128)(2,1)} %bitcast.23), channel_id=1, source_target_pairs={{0,64},{64,0},{1,65},{65,1},{2,66},{66,2},{3,67},{67,3},{4,68},{68... | collective-permute-start | bytes 11010056 | tf_op jit(solution)/shard_map/ppermute | solution.py:72
  87.8 1.8 %copy-start.1 = (bf16[512,3584]{1,0:T(8,128)(2,1)}, bf16[512,3584]{1,0:T(8,128)(2,1)S(1)}, u32[]{:S(2)}) copy-start(bf16[512,3584]{1,0:T(8,128)(2,1)S(1)} %shard_map.124) | copy-start | bytes 11010052
  89.6 8.4 %copy-start.4 = (f32[32,8]{0,1:T(8,128)S(1)}, f32[32,8]{0,1:T(8,128)}, u32[]{:S(2)}) copy-start(f32[32,8]{0,1:T(8,128)} %param.13) | copy-start | bytes 3076
  89.6 8.5 %copy-start.3 = (bf16[4,4096]{1,0:T(4,128)(2,1)S(1)}, bf16[4,4096]{1,0:T(4,128)(2,1)}, u32[]{:S(2)}) copy-start(bf16[4,4096]{1,0:T(4,128)(2,1)} %param.18) | copy-start | bytes 98308
  89.6 8.9 %copy-start.5 = (s32[4]{0:T(128)S(1)}, s32[4]{0:T(128)}, u32[]{:S(2)}) copy-start(s32[4]{0:T(128)} %param.21) | copy-start | bytes 52
  89.6 8.9 %copy-start.2 = (bf16[4,64,512]{2,1,0:T(8,128)(2,1)S(1)}, bf16[4,64,512]{2,1,0:T(8,128)(2,1)}, u32[]{:S(2)}) copy-start(bf16[4,64,512]{2,1,0:T(8,128)(2,1)} %param.17) | copy-start | bytes 786436
  89.6 57.1 %all-to-all-start.1 = ((bf16[64,8,3584]{2,1,0:T(8,128)(2,1)}), bf16[64,8,3584]{2,1,0:T(8,128)(2,1)}, u32[]{:S(2)}, u32[]{:S(2)}) async-start(bf16[64,8,3584]{2,1,0:T(8,128)(2,1)} %bitcast.18), calls=%async_computation.1 | async-start | bytes 7340032 | tf_op jit(solution)/shard_map/all_to_all | solution.py:144

commit v10 on v9

--- a/solution.py
+++ b/solution.py
@@ -72,12 +72,78 @@
     return lax.ppermute(w, "role", [(0, 1), (1, 0)])
 
 
-def full_expert(rows, w_gate, w_up, w_down):
-    gate_own, up_own, down_own = w_gate[0], w_up[0], w_down[0]
-    gate_other, up_other, down_other = other_half(gate_own), other_half(up_own), other_half(down_own)
-    h0 = gate_up(rows, gate_own, up_own)
-    h1 = gate_up(rows, gate_other, up_other)
-    return down(h0, h1, down_own, down_other)
+def ffn_kernel(steps, x_ref, go_ref, uo_ref, gt_ref, ut_ref, do_ref, dt_ref, o_ref, h_ref):
+    i = pl.program_id(0)
+    tile = go_ref.shape[1]
+    units = h_ref.shape[1] // 2
+
+    def hidden(g_ref, u_ref, column):
+        x = x_ref[...]
+        gate_part = jnp.dot(x, g_ref[...], preferred_element_type=jnp.float32)
+        up_part = jnp.dot(x, u_ref[...], preferred_element_type=jnp.float32)
+        h_ref[:, pl.ds(pl.multiple_of(column, tile), tile)] = (
+            jax.nn.silu(gate_part) * up_part
+        ).astype(h_ref.dtype)
+
+    @pl.when(i < steps)
+    def _():
+        hidden(go_ref, uo_ref, i * tile)
+
+    @pl.when((i >= steps) & (i < 2 * steps))
+    def _():
+        hidden(gt_ref, ut_ref, units + (i - steps) * tile)
+
+    @pl.when(i >= 2 * steps)
+    def _():
+        total = lax.dot_general(
+            h_ref[:, :units], do_ref[...], (((1,), (1,)), ((), ())), preferred_element_type=jnp.float32
+        )
+        total = total + lax.dot_general(
+            h_ref[:, units:], dt_ref[...], (((1,), (1,)), ((), ())), preferred_element_type=jnp.float32
+        )
+        o_ref[...] = total.astype(o_ref.dtype)
+
+
+def full_expert(rows, w_gate, w_up, w_down, unit_tile=256, out_tile=896):
+    count, width = rows.shape
+    own = (w_gate[0], w_up[0], w_down[0])
+    other = tuple(other_half(w) for w in own)
+    units = own[0].shape[1]
+    steps = units // unit_tile
+    outs = width // out_tile
+
+    def own_map(i):
+        return (0, jnp.minimum(i, steps - 1))
+
+    def other_map(i):
+        return (0, jnp.clip(i - steps, 0, steps - 1))
+
+    def down_map(i):
+        return (jnp.clip(i - 2 * steps, 0, outs - 1), 0)
+
+    unit_block = (width, unit_tile)
+    return pl.pallas_call(
+        functools.partial(ffn_kernel, steps),
+        out_shape=jax.ShapeDtypeStruct((count, width), jnp.bfloat16),
+        grid=(2 * steps + outs,),
+        in_specs=[
+            pl.BlockSpec((count, width), lambda i: (0, 0)),
+            pl.BlockSpec(unit_block, own_map),
+            pl.BlockSpec(unit_block, own_map),
+            pl.BlockSpec(unit_block, other_map),
+            pl.BlockSpec(unit_block, other_map),
+            pl.BlockSpec((out_tile, units), down_map),
+            pl.BlockSpec((out_tile, units), down_map),
+        ],
+        out_specs=pl.BlockSpec((count, out_tile), lambda i: (0, jnp.clip(i - 2 * steps, 0, outs - 1))),
+        scratch_shapes=[pltpu.VMEM((count, 2 * units), jnp.bfloat16)],
+        compiler_params=pltpu.CompilerParams(vmem_limit_bytes=56 * 1024 * 1024),
+        cost_estimate=pl.CostEstimate(
+            flops=12 * count * width * units,
+            transcendentals=2 * count * units,
+            bytes_accessed=2 * (2 * count * width + 6 * width * units),
+        ),
+    )(rows, own[0], own[1], other[0], other[1], own[2], other[2])
 
 
 score_scale = 192.0 ** (-0.5)

time: 152 us -> 143 us (0.941)
  blocking collectives: 0 us -> 58.9 us
  waiting for transfers between devices: 80 us -> 31.6 us
  starting transfers between devices: 20.8 us -> 6.61 us
  local copies, waits for them, and re-layouts: 3.06 us -> 1.15 us
  matrix products: 23.5 us -> 21.6 us
    all_to_all x0 -> x1, blocking collectives: none -> 58.9 us  [per_device(): lax.all_to_all(outgoing, 'dev', split_axis=0, concat_axis=0, tiled=True)]
    all_to_all x1 -> x0, waiting for transfers between devices: 46.6 us -> none  [per_device(): lax.all_to_all(outgoing, 'dev', split_axis=0, concat_axis=0, tiled=True)]
    all_to_all x1 -> x0, starting transfers between devices: 11.7 us -> none  [per_device(): lax.all_to_all(outgoing, 'dev', split_axis=0, concat_axis=0, tiled=True)]
    all_to_all x1, starting transfers between devices: 8.39 us -> 5.93 us  [per_device(): lax.all_to_all(finished, 'dev', split_axis=0, concat_axis=0, tiled=True)]
    unnamed x14 -> x12, local copies, waits for them, and re-layouts: 2.78 us -> 0.87 us
    dot_general x1, matrix products: 3.94 us -> 2.1 us  [per_device(): jnp.dot(dispatch.astype(jnp.bfloat16), moe_rows, preferred_element_type=j...]
    all_to_all x1, waiting for transfers between devices: 33.4 us -> 31.6 us  [per_device(): lax.all_to_all(finished, 'dev', split_axis=0, concat_axis=0, tiled=True)]
    pallas_call x3 -> x1, Pallas kernels: 22.6 us -> 21.3 us  [full_expert(): pl.pallas_call(functools.partial(ffn_kernel, steps), out_shape=jax.ShapeD...]
  transfers between devices with their start and end apart: 5 -> 4, of which waited for: 2 -> 1; matrix products, arithmetic and copies ran while one was open for 10% -> 13% of each run, Pallas kernels for 10% -> 0%
where the time goes in v10:
time: 143 us
  blocking collectives  58.9 us (41%)
  waiting for transfers between devices  31.6 us (22%)
  matrix products  21.6 us (15%)
  Pallas kernels  21.3 us (15%)
  starting transfers between devices  6.61 us (5%)
    all_to_all x1, blocking collectives, per_device(): lax.all_to_all(outgoing, 'dev', split_axis=0, concat_axis=0, tiled=True)  58.9 us
    all_to_all x1, waiting for transfers between devices, per_device(): lax.all_to_all(finished, 'dev', split_axis=0, concat_axis=0, tiled=True)  31.6 us
    pallas_call x1, Pallas kernels, full_expert(): pl.pallas_call(functools.partial(ffn_kernel, steps), out_shape=jax.ShapeD...  21.3 us
    dot_general x1, matrix products, attend_row(): jnp.dot(probs, cache_lat, preferred_element_type=jnp.float32)  6.34 us
    dot_general x1, matrix products, attend_row(): lax.dot_general(query_lat, cache_lat, (((1,), (1,)), ((), ())), preferred...  6 us
    all_to_all x1, starting transfers between devices, per_device(): lax.all_to_all(finished, 'dev', split_axis=0, concat_axis=0, tiled=True)  5.93 us
    dot_general x1, matrix products, per_device(): jnp.dot(weighted, flat_back.astype(jnp.float32), precision=lax.Precision....  4.61 us
  transfers between devices with their start and end apart: 4, of which 1 were waited for; matrix products, arithmetic and copies ran while one was open for 13% of the time, Pallas kernels for 0%

profile of v10, /device:TPU:0, one launch (start us, length us, event | category | flops | bytes accessed | tf_op | source)
XLA Modules:
  0.0 142.5 jit_solution(2347637835392159219)
XLA Ops:
  0.6 0.0 copy-start
  0.6 0.1 collective-permute-start
  0.7 0.5 collective-permute-start.1
  1.2 0.1 collective-permute-start.2
  1.3 0.8 copy.19
  2.1 0.1 eq.42
  2.2 0.2 fusion.8
  2.4 0.1 convert_element_type.29
  2.5 0.2 fusion.10
  2.7 2.1 %fusion.1 = bf16[64,8,3584]{2,1,0:T(8,128)(2,1)S(1)} fusion(pred[512,32]{0,1:T(8,128)(4,1)S(1)} %fusion.10, bf16[32,3584]{1,0:T(8,128)(2,1)} %param.11), kind=kOutput, calls=%fused_computation.2 | convolution fusion | flops 119275520 | bytes 3915776 | tf_op jit(solution)/shard_map/dot_general | solution.py:203
  4.9 58.9 %all_to_all.10 = bf16[64,8,3584]{2,1,0:T(8,128)(2,1)} all-to-all(bf16[64,8,3584]{2,1,0:T(8,128)(2,1)S(1)} %fusion.1), channel_id=1, replica_groups=mesh['role'=2,'dev'=64] {'dev'}, dimensions={0} | all-to-all | bytes 7340032 | tf_op jit(solution)/shard_map/all_to_all | solution.py:206
  63.7 0.0 collective-permute-done.gt_ref
  63.7 0.0 collective-permute-done.1.ut_ref
  63.7 0.0 collective-permute-done.2.dt_ref
  63.8 21.3 %shard_map.122 = bf16[512,3584]{1,0:T(8,128)(2,1)} custom-call(bf16[512,3584]{1,0:T(8,128)(2,1)} %bitcast.19, bf16[3584,512]{1,0:T(8,128)(2,1)} %bitcast.21, bf16[3584,512]{1,0:T(8,128)(2,1)} %bitcast.23, bf16[3584,512]{1,0:T(8,128)(2,1)} %collective-permute-done.gt_ref, bf16[3584,512]{1,0:T(8,128)(2,1)} %collective-permute-done.1.ut_ref, ...), custom_call_target="tpu_custom_call" | custom-call | flops 11274289152 | bytes 29360128 | tf_op jit(solution)/shard_map/pallas_call | solution.py:125
  85.1 0.0 copy-start.3
  85.1 0.0 copy-start.2
  85.1 0.0 copy-start.4
  85.1 0.0 copy-start.1
  85.1 5.9 %all-to-all-start.1 = ((bf16[64,8,3584]{2,1,0:T(8,128)(2,1)}), bf16[64,8,3584]{2,1,0:T(8,128)(2,1)}, u32[]{:S(2)}, u32[]{:S(2)}) async-start(bf16[64,8,3584]{2,1,0:T(8,128)(2,1)} %bitcast.18), calls=%async_computation.1 | async-start | bytes 7340032 | tf_op jit(solution)/shard_map/all_to_all | solution.py:210
  91.0 0.0 copy-done.3
  91.1 0.1 copy.21
  91.1 0.0 copy-done.2
  91.1 0.1 reshape.76
  91.3 0.2 select_reduce_fusion
  91.5 0.0 copy-done.4
  91.5 0.1 iota_compare_fusion.6
  91.6 0.0 copy-done.1
  91.6 6.0 %fusion.13 = f32[4,64,2048]{2,1,0:T(8,128)S(1)} fusion(bf16[4,64,512]{2,1,0:T(8,128)(2,1)S(1)} %copy-done.1, bf16[4,2048,512]{2,1,0:T(8,128)(2,1)} %param.19), kind=kOutput, calls=%fused_computation.26 | convolution fusion | flops 536870912 | bytes 10747904 | tf_op jit(solution)/shard_map/vmap()/dot_general | solution.py:155
  97.6 0.0 copy-done
  97.6 2.3 %fusion.12 = (f32[4,64]{1,0:T(4,128)S(1)}, f32[4,64,2048]{2,1,0:T(8,128)}) fusion(pred[4,2048]{1,0:T(4,128)(4,1)S(1)} %iota_compare_fusion.6, f32[4,64,2048]{2,1,0:T(8,128)S(1)} %fusion.13, bf16[4,64,64]{2,1,0:T(8,128)(2,1)S(1)} %reshape.76, bf16[4,64,2048]{2,1,0:T(8,128)(2,1)S(1)} %copy-done), kind=kOutput, calls=%fused_computation.25 | convolution fusion | flops 70256640 | bytes 5284864 | tf_op jit(solution)/shard_map/vmap()/sub | solution.py:166
  99.9 6.3 %convolution_convert_fusion.2 = bf16[4,64,512]{2,1,0:T(8,128)(2,1)} fusion(bf16[4,2048,512]{2,1,0:T(8,128)(2,1)} %param.19, f32[4,64,2048]{2,1,0:T(8,128)} %get-tuple-element.3, f32[4,64]{1,0:T(4,128)S(1)} %get-tuple-element.2), kind=kOutput, calls=%fused_computation.12 | convolution fusion | flops 538050560 | bytes 10748928 | tf_op jit(solution)/shard_map/vmap()/dot_general | solution.py:168
  106.3 31.6 %all-to-all-done.1 = bf16[64,8,3584]{2,1,0:T(8,128)(2,1)} async-done(((bf16[64,8,3584]{2,1,0:T(8,128)(2,1)}), bf16[64,8,3584]{2,1,0:T(8,128)(2,1)}, u32[]{:S(2)}, u32[]{:S(2)}) %all-to-all-start.1) | async-done | bytes 3670048 | tf_op jit(solution)/shard_map/all_to_all | solution.py:210
  137.9 4.6 %convolution_convert_fusion.1 = bf16[32,3584]{1,0:T(8,128)(2,1)} fusion(f32[32,512]{1,0:T(8,128)S(1)} %select_reduce_fusion, bf16[64,8,3584]{2,1,0:T(8,128)(2,1)} %all-to-all-done.1), kind=kOutput, calls=%fused_computation.3 | convolution fusion | flops 704757760 | bytes 3964928 | tf_op jit(solution)/shard_map/dot_general | solution.py:216
  (2 shorter events, 0.0 us)
Async XLA Ops:
  0.6 97.0 %copy-start = (bf16[4,64,2048]{2,1,0:T(8,128)(2,1)S(1)}, bf16[4,64,2048]{2,1,0:T(8,128)(2,1)}, u32[]{:S(2)}) copy-start(bf16[4,64,2048]{2,1,0:T(8,128)(2,1)} %param.20) | copy-start | bytes 3145732
  0.6 63.1 %collective-permute-start = (bf16[3584,512]{1,0:T(8,128)(2,1)}, bf16[3584,512]{1,0:T(8,128)(2,1)}, u32[]{:S(2)}, u32[]{:S(2)}) collective-permute-start(bf16[3584,512]{1,0:T(8,128)(2,1)} %bitcast.20), channel_id=1, source_target_pairs={{0,64},{64,0},{1,65},{65,1},{2,66},{66,2},{3,67},{67,3},{4,68},{68... | collective-permute-start | bytes 11010056 | tf_op jit(solution)/shard_map/ppermute | solution.py:72
  0.7 63.0 %collective-permute-start.1 = (bf16[3584,512]{1,0:T(8,128)(2,1)}, bf16[3584,512]{1,0:T(8,128)(2,1)}, u32[]{:S(2)}, u32[]{:S(2)}) collective-permute-start(bf16[3584,512]{1,0:T(8,128)(2,1)} %bitcast.22), channel_id=1, source_target_pairs={{0,64},{64,0},{1,65},{65,1},{2,66},{66,2},{3,67},{67,3},{4,68},{68... | collective-permute-start | bytes 11010056 | tf_op jit(solution)/shard_map/ppermute | solution.py:72
  1.2 62.5 %collective-permute-start.2 = (bf16[3584,512]{1,0:T(8,128)(2,1)}, bf16[3584,512]{1,0:T(8,128)(2,1)}, u32[]{:S(2)}, u32[]{:S(2)}) collective-permute-start(bf16[3584,512]{1,0:T(8,128)(2,1)} %bitcast.24), channel_id=1, source_target_pairs={{0,64},{64,0},{1,65},{65,1},{2,66},{66,2},{3,67},{67,3},{4,68},{68... | collective-permute-start | bytes 11010056 | tf_op jit(solution)/shard_map/ppermute | solution.py:72
  85.1 6.0 %copy-start.3 = (f32[32,8]{0,1:T(8,128)S(1)}, f32[32,8]{0,1:T(8,128)}, u32[]{:S(2)}) copy-start(f32[32,8]{0,1:T(8,128)} %param.13) | copy-start | bytes 3076
  85.1 6.1 %copy-start.2 = (bf16[4,4096]{1,0:T(4,128)(2,1)S(1)}, bf16[4,4096]{1,0:T(4,128)(2,1)}, u32[]{:S(2)}) copy-start(bf16[4,4096]{1,0:T(4,128)(2,1)} %param.18) | copy-start | bytes 98308
  85.1 6.4 %copy-start.4 = (s32[4]{0:T(128)S(1)}, s32[4]{0:T(128)}, u32[]{:S(2)}) copy-start(s32[4]{0:T(128)} %param.21) | copy-start | bytes 52
  85.1 6.5 %copy-start.1 = (bf16[4,64,512]{2,1,0:T(8,128)(2,1)S(1)}, bf16[4,64,512]{2,1,0:T(8,128)(2,1)}, u32[]{:S(2)}) copy-start(bf16[4,64,512]{2,1,0:T(8,128)(2,1)} %param.17) | copy-start | bytes 786436
  85.1 52.8 %all-to-all-start.1 = ((bf16[64,8,3584]{2,1,0:T(8,128)(2,1)}), bf16[64,8,3584]{2,1,0:T(8,128)(2,1)}, u32[]{:S(2)}, u32[]{:S(2)}) async-start(bf16[64,8,3584]{2,1,0:T(8,128)(2,1)} %bitcast.18), calls=%async_computation.1 | async-start | bytes 7340032 | tf_op jit(solution)/shard_map/all_to_all | solution.py:210

commit v11 on v10

--- a/solution.py
+++ b/solution.py
@@ -213,10 +213,14 @@
         jnp.where(picks, gate_weights.reshape(pair_count)[:, None], 0.0).reshape(tok_count, topk_count, slot_count),
         axis=1,
     )
-    moe_out = jnp.dot(
-        weighted, flat_back.astype(jnp.float32), precision=lax.Precision.HIGHEST,
-        preferred_element_type=jnp.float32,
-    ).astype(jnp.bfloat16)
+    first = weighted.astype(jnp.bfloat16)
+    rest = weighted - first.astype(jnp.float32)
+    second = rest.astype(jnp.bfloat16)
+    third = (rest - second.astype(jnp.float32)).astype(jnp.bfloat16)
+    parts = jnp.dot(
+        jnp.concatenate([first, second, third], axis=0), flat_back, preferred_element_type=jnp.float32
+    )
+    moe_out = (parts[:tok_count] + parts[tok_count:2 * tok_count] + parts[2 * tok_count:]).astype(jnp.bfloat16)
     attended = jax.vmap(attend_row)(q_latent, q_rope, latent_cache, rope_cache, lengths)
     return (moe_out, attended)
 

time: 143 us -> 142 us (level)
    dot_general x1, matrix products: 4.61 us -> 2.76 us  [per_device(): jnp.dot(jnp.concatenate([first, second, third], axis=0), flat_back, prefe...]
  transfers between devices with their start and end apart: 4 -> 4, of which waited for: 1 -> 1; matrix products, arithmetic and copies ran while one was open for 13% -> 14% of each run, Pallas kernels for 0% -> 0%
where the time goes in v11:
time: 142 us; the launch traced here: 141 us
  blocking collectives  58.9 us (41%)
  waiting for transfers between devices  30.3 us (21%)
  Pallas kernels  21.3 us (15%)
  matrix products  20.6 us (15%)
  starting transfers between devices  6.42 us (5%)
  local copies, waits for them, and re-layouts  1.79 us (1%)
    all_to_all x1, blocking collectives, per_device(): lax.all_to_all(outgoing, 'dev', split_axis=0, concat_axis=0, tiled=True)  58.9 us
    all_to_all x1, waiting for transfers between devices, per_device(): lax.all_to_all(finished, 'dev', split_axis=0, concat_axis=0, tiled=True)  30.3 us
    pallas_call x1, Pallas kernels, full_expert(): pl.pallas_call(functools.partial(ffn_kernel, steps), out_shape=jax.ShapeD...  21.3 us
    dot_general x1, matrix products, attend_row(): jnp.dot(probs, cache_lat, preferred_element_type=jnp.float32)  6.34 us
    dot_general x1, matrix products, attend_row(): lax.dot_general(query_lat, cache_lat, (((1,), (1,)), ((), ())), preferred...  6 us
    all_to_all x1, starting transfers between devices, per_device(): lax.all_to_all(finished, 'dev', split_axis=0, concat_axis=0, tiled=True)  5.75 us
    sub x1, matrix products, attend_row(): weights = jnp.where(valid, jnp.exp(scores - highest), jnp.float32(0.0))  3.2 us
  transfers between devices with their start and end apart: 4, of which 1 were waited for; matrix products, arithmetic and copies ran while one was open for 14% of the time, Pallas kernels for 0%

profile of v11, /device:TPU:0, one launch (start us, length us, event | category | flops | bytes accessed | tf_op | source)
XLA Modules:
  0.0 141.4 jit_solution(8488821136901415115)
XLA Ops:
  0.6 0.0 copy-start
  0.6 0.1 collective-permute-start
  0.7 0.5 collective-permute-start.1
  1.2 0.1 collective-permute-start.2
  1.3 0.8 copy.19
  2.1 0.1 eq.42
  2.2 0.2 fusion.9
  2.4 0.1 convert_element_type.43
  2.5 0.2 fusion.11
  2.7 2.1 %fusion.1 = bf16[64,8,3584]{2,1,0:T(8,128)(2,1)S(1)} fusion(pred[512,32]{0,1:T(8,128)(4,1)S(1)} %fusion.11, bf16[32,3584]{1,0:T(8,128)(2,1)} %param.11), kind=kOutput, calls=%fused_computation.2 | convolution fusion | flops 119275520 | bytes 3915776 | tf_op jit(solution)/shard_map/dot_general | solution.py:203
  4.8 58.9 %all_to_all.10 = bf16[64,8,3584]{2,1,0:T(8,128)(2,1)} all-to-all(bf16[64,8,3584]{2,1,0:T(8,128)(2,1)S(1)} %fusion.1), channel_id=1, replica_groups=mesh['role'=2,'dev'=64] {'dev'}, dimensions={0} | all-to-all | bytes 7340032 | tf_op jit(solution)/shard_map/all_to_all | solution.py:206
  63.7 0.0 collective-permute-done.gt_ref
  63.7 0.0 collective-permute-done.1.ut_ref
  63.7 0.0 collective-permute-done.2.dt_ref
  63.8 21.3 %shard_map.122 = bf16[512,3584]{1,0:T(8,128)(2,1)} custom-call(bf16[512,3584]{1,0:T(8,128)(2,1)} %bitcast.18, bf16[3584,512]{1,0:T(8,128)(2,1)} %bitcast.20, bf16[3584,512]{1,0:T(8,128)(2,1)} %bitcast.22, bf16[3584,512]{1,0:T(8,128)(2,1)} %collective-permute-done.gt_ref, bf16[3584,512]{1,0:T(8,128)(2,1)} %collective-permute-done.1.ut_ref, ...), custom_call_target="tpu_custom_call" | custom-call | flops 11274289152 | bytes 29360128 | tf_op jit(solution)/shard_map/pallas_call | solution.py:125
  85.1 0.0 copy-start.3
  85.1 0.0 copy-start.2
  85.1 0.0 copy-start.4
  85.1 0.0 copy-start.1
  85.1 5.7 %all-to-all-start.1 = ((bf16[64,8,3584]{2,1,0:T(8,128)(2,1)}), bf16[64,8,3584]{2,1,0:T(8,128)(2,1)}, u32[]{:S(2)}, u32[]{:S(2)}) async-start(bf16[64,8,3584]{2,1,0:T(8,128)(2,1)} %bitcast.17), calls=%async_computation.1 | async-start | bytes 7340032 | tf_op jit(solution)/shard_map/all_to_all | solution.py:210
  90.9 0.0 copy-done.3
  90.9 0.1 copy.21
  91.0 0.0 copy-done.2
  91.0 0.8 reshape.76
  91.7 0.2 select_reduce_fusion
  92.0 0.0 copy-done.4
  92.0 0.1 iota_compare_fusion.6
  92.1 0.0 copy-done.1
  92.1 6.0 %fusion.23 = f32[4,64,2048]{2,1,0:T(8,128)S(1)} fusion(bf16[4,64,512]{2,1,0:T(8,128)(2,1)S(1)} %copy-done.1, bf16[4,2048,512]{2,1,0:T(8,128)(2,1)} %param.19), kind=kOutput, calls=%fused_computation.39 | convolution fusion | flops 536870912 | bytes 10747904 | tf_op jit(solution)/shard_map/vmap()/dot_general | solution.py:155
  98.1 0.0 copy-done
  98.1 3.2 %fusion.22 = (f32[4,64]{1,0:T(4,128)S(1)}, f32[4,64,2048]{2,1,0:T(8,128)}) fusion(pred[4,2048]{1,0:T(4,128)(4,1)S(1)} %iota_compare_fusion.6, f32[4,64,2048]{2,1,0:T(8,128)S(1)} %fusion.23, bf16[4,64,64]{2,1,0:T(8,128)(2,1)} %reshape.76, bf16[4,64,2048]{2,1,0:T(8,128)(2,1)S(1)} %copy-done), kind=kOutput, calls=%fused_computation.38 | convolution fusion | flops 70256640 | bytes 5284864 | tf_op jit(solution)/shard_map/vmap()/sub | solution.py:166
  101.3 6.3 %convolution_convert_fusion.1 = bf16[4,64,512]{2,1,0:T(8,128)(2,1)} fusion(bf16[4,2048,512]{2,1,0:T(8,128)(2,1)} %param.19, f32[4,64,2048]{2,1,0:T(8,128)} %get-tuple-element.6, f32[4,64]{1,0:T(4,128)S(1)} %get-tuple-element.5), kind=kOutput, calls=%fused_computation.12 | convolution fusion | flops 538050560 | bytes 10748928 | tf_op jit(solution)/shard_map/vmap()/dot_general | solution.py:168
  107.6 30.3 %all-to-all-done.1 = bf16[64,8,3584]{2,1,0:T(8,128)(2,1)} async-done(((bf16[64,8,3584]{2,1,0:T(8,128)(2,1)}), bf16[64,8,3584]{2,1,0:T(8,128)(2,1)}, u32[]{:S(2)}, u32[]{:S(2)}) %all-to-all-start.1) | async-done | bytes 3670048 | tf_op jit(solution)/shard_map/all_to_all | solution.py:210
  137.9 2.8 %fusion.2 = f32[96,3584]{1,0:T(8,128)S(1)} fusion(bf16[64,8,3584]{2,1,0:T(8,128)(2,1)} %all-to-all-done.1, bf16[32,512]{1,0:T(8,128)(2,1)S(1)} %get-tuple-element.3, bf16[32,512]{1,0:T(8,128)(2,1)S(1)} %get-tuple-element.4, bf16[32,512]{1,0:T(8,128)(2,1)S(1)} %get-tuple-element.2), kind=kOutput, calls=%fused_computation.3 | convolution fusion | flops 352616448 | bytes 5144576 | tf_op jit(solution)/shard_map/dot_general | solution.py:220
  140.7 0.8 fusion.12
  (3 shorter events, 0.0 us)
Async XLA Ops:
  0.6 97.4 %copy-start = (bf16[4,64,2048]{2,1,0:T(8,128)(2,1)S(1)}, bf16[4,64,2048]{2,1,0:T(8,128)(2,1)}, u32[]{:S(2)}) copy-start(bf16[4,64,2048]{2,1,0:T(8,128)(2,1)} %param.20) | copy-start | bytes 3145732
  0.6 63.1 %collective-permute-start = (bf16[3584,512]{1,0:T(8,128)(2,1)}, bf16[3584,512]{1,0:T(8,128)(2,1)}, u32[]{:S(2)}, u32[]{:S(2)}) collective-permute-start(bf16[3584,512]{1,0:T(8,128)(2,1)} %bitcast.19), channel_id=1, source_target_pairs={{0,64},{64,0},{1,65},{65,1},{2,66},{66,2},{3,67},{67,3},{4,68},{68... | collective-permute-start | bytes 11010056 | tf_op jit(solution)/shard_map/ppermute | solution.py:72
  0.7 63.0 %collective-permute-start.1 = (bf16[3584,512]{1,0:T(8,128)(2,1)}, bf16[3584,512]{1,0:T(8,128)(2,1)}, u32[]{:S(2)}, u32[]{:S(2)}) collective-permute-start(bf16[3584,512]{1,0:T(8,128)(2,1)} %bitcast.21), channel_id=1, source_target_pairs={{0,64},{64,0},{1,65},{65,1},{2,66},{66,2},{3,67},{67,3},{4,68},{68... | collective-permute-start | bytes 11010056 | tf_op jit(solution)/shard_map/ppermute | solution.py:72
  1.2 62.5 %collective-permute-start.2 = (bf16[3584,512]{1,0:T(8,128)(2,1)}, bf16[3584,512]{1,0:T(8,128)(2,1)}, u32[]{:S(2)}, u32[]{:S(2)}) collective-permute-start(bf16[3584,512]{1,0:T(8,128)(2,1)} %bitcast.23), channel_id=1, source_target_pairs={{0,64},{64,0},{1,65},{65,1},{2,66},{66,2},{3,67},{67,3},{4,68},{68... | collective-permute-start | bytes 11010056 | tf_op jit(solution)/shard_map/ppermute | solution.py:72
  85.1 5.8 %copy-start.3 = (f32[32,8]{0,1:T(8,128)S(1)}, f32[32,8]{0,1:T(8,128)}, u32[]{:S(2)}) copy-start(f32[32,8]{0,1:T(8,128)} %param.13) | copy-start | bytes 3076
  85.1 5.9 %copy-start.2 = (bf16[4,4096]{1,0:T(4,128)(2,1)S(1)}, bf16[4,4096]{1,0:T(4,128)(2,1)}, u32[]{:S(2)}) copy-start(bf16[4,4096]{1,0:T(4,128)(2,1)} %param.18) | copy-start | bytes 98308
  85.1 6.9 %copy-start.4 = (s32[4]{0:T(128)S(1)}, s32[4]{0:T(128)}, u32[]{:S(2)}) copy-start(s32[4]{0:T(128)} %param.21) | copy-start | bytes 52
  85.1 7.0 %copy-start.1 = (bf16[4,64,512]{2,1,0:T(8,128)(2,1)S(1)}, bf16[4,64,512]{2,1,0:T(8,128)(2,1)}, u32[]{:S(2)}) copy-start(bf16[4,64,512]{2,1,0:T(8,128)(2,1)} %param.17) | copy-start | bytes 786436
  85.1 52.8 %all-to-all-start.1 = ((bf16[64,8,3584]{2,1,0:T(8,128)(2,1)}), bf16[64,8,3584]{2,1,0:T(8,128)(2,1)}, u32[]{:S(2)}, u32[]{:S(2)}) async-start(bf16[64,8,3584]{2,1,0:T(8,128)(2,1)} %bitcast.17), calls=%async_computation.1 | async-start | bytes 7340032 | tf_op jit(solution)/shard_map/all_to_all | solution.py:210

commit v12 on v10

--- a/solution.py
+++ b/solution.py
@@ -66,6 +66,61 @@
             bytes_accessed=2 * (count * width + 2 * width * units + 2 * count * units),
         ),
     )(h0, h1, d0, d1)
+
+
+MESH = pl.DeviceIdType.MESH
+
+def a2a_kernel(n, x_ref, o_ref, send_sems, recv_sems, local_sem):
+    me = lax.axis_index("dev")
+    core = lax.axis_index("role")
+    local = pltpu.make_async_copy(x_ref.at[me], o_ref.at[me], local_sem)
+    local.start()
+
+    def offset_of(k):
+        return lax.rem((k - 1) * 2 + me, n - 1) + 1
+
+    def describe(offset):
+        peer = lax.rem(me + offset, n)
+        return pltpu.make_async_remote_copy(
+            src_ref=x_ref.at[peer],
+            dst_ref=o_ref.at[me],
+            send_sem=send_sems.at[offset],
+            recv_sem=recv_sems.at[offset],
+            device_id=(core, peer),
+            device_id_type=MESH,
+        )
+
+    def issue(k, carry):
+        describe(offset_of(k)).start()
+        return carry
+
+    lax.fori_loop(1, n, issue, 0)
+
+    def finish(offset, carry):
+        describe(offset).wait()
+        return carry
+
+    lax.fori_loop(1, n, finish, 0)
+    local.wait()
+
+
+def all_to_all_dev(x):
+    n = lax.axis_size("dev")
+    return pl.pallas_call(
+        functools.partial(a2a_kernel, n),
+        out_shape=jax.ShapeDtypeStruct(x.shape, x.dtype),
+        in_specs=[pl.BlockSpec(memory_space=pltpu.VMEM)],
+        out_specs=pl.BlockSpec(memory_space=pltpu.VMEM),
+        scratch_shapes=[
+            pltpu.SemaphoreType.DMA((n,)),
+            pltpu.SemaphoreType.DMA((n,)),
+            pltpu.SemaphoreType.DMA(()),
+        ],
+        compiler_params=pltpu.CompilerParams(has_side_effects=True, vmem_limit_bytes=32 * 1024 * 1024),
+    )(x)
+
+
+score_scale = 192.0 ** (-0.5)
 
 
 def other_half(w):
@@ -203,7 +258,7 @@
     outgoing = jnp.dot(
         dispatch.astype(jnp.bfloat16), moe_rows, preferred_element_type=jnp.float32
     ).astype(jnp.bfloat16).reshape(experts, capacity, width)
-    arrived = lax.all_to_all(outgoing, "dev", split_axis=0, concat_axis=0, tiled=True)
+    arrived = all_to_all_dev(outgoing)
     own_rows = arrived.reshape(experts * capacity, width)
     expert_sum = full_expert(own_rows, w_gate, w_up, w_down)
     finished = expert_sum.reshape(experts, capacity, width)

time: 143 us -> 170 us (1.19)
  Pallas kernels: 21.3 us -> 89.7 us
  blocking collectives: 58.9 us -> 0 us
  starting transfers between devices: 6.61 us -> 22.9 us
  local copies, waits for them, and re-layouts: 1.15 us -> 2.98 us
    pallas_call x0 -> x1, Pallas kernels: none -> 68.4 us  [all_to_all_dev(): pl.pallas_call(functools.partial(a2a_kernel, n), out_shape=jax.ShapeDtype...]
    all_to_all x1 -> x0, blocking collectives: 58.9 us -> none  [per_device(): lax.all_to_all(outgoing, 'dev', split_axis=0, concat_axis=0, tiled=True)]
    all_to_all x1, starting transfers between devices: 5.93 us -> 22.2 us  [per_device(): lax.all_to_all(finished, 'dev', split_axis=0, concat_axis=0, tiled=True)]
    unnamed x12 -> x14, local copies, waits for them, and re-layouts: 0.87 us -> 2.69 us
  transfers between devices with their start and end apart: 4 -> 4, of which waited for: 1 -> 1; matrix products, arithmetic and copies ran while one was open for 13% -> 11% of each run, Pallas kernels for 0% -> 40%
where the time goes in v12:
time: 170 us
  Pallas kernels  89.7 us (53%)
  waiting for transfers between devices  31.6 us (19%)
  starting transfers between devices  22.9 us (13%)
  matrix products  21.6 us (13%)
  local copies, waits for them, and re-layouts  2.98 us (2%)
    pallas_call x1, Pallas kernels, all_to_all_dev(): pl.pallas_call(functools.partial(a2a_kernel, n), out_shape=jax.ShapeDtype...  68.4 us
    all_to_all x1, waiting for transfers between devices, per_device(): lax.all_to_all(finished, 'dev', split_axis=0, concat_axis=0, tiled=True)  31.6 us
    all_to_all x1, starting transfers between devices, per_device(): lax.all_to_all(finished, 'dev', split_axis=0, concat_axis=0, tiled=True)  22.2 us
    pallas_call x1, Pallas kernels, full_expert(): pl.pallas_call(functools.partial(ffn_kernel, steps), out_shape=jax.ShapeD...  21.3 us
    dot_general x1, matrix products, attend_row(): jnp.dot(probs, cache_lat, preferred_element_type=jnp.float32)  6.34 us
    dot_general x1, matrix products, attend_row(): lax.dot_general(query_lat, cache_lat, (((1,), (1,)), ((), ())), preferred...  6 us
    dot_general x1, matrix products, per_device(): jnp.dot(weighted, flat_back.astype(jnp.float32), precision=lax.Precision....  4.61 us
  transfers between devices with their start and end apart: 4, of which 1 were waited for; matrix products, arithmetic and copies ran while one was open for 11% of the time, Pallas kernels for 40%

profile of v12, /device:TPU:0, one launch (start us, length us, event | category | flops | bytes accessed | tf_op | source)
XLA Modules:
  0.0 170.0 jit_solution(14706175900863860800)
XLA Ops:
  0.6 0.0 copy-start
  0.6 0.1 collective-permute-start
  0.7 0.5 collective-permute-start.1
  1.2 0.1 collective-permute-start.2
  1.3 0.8 copy.19
  2.1 0.1 eq.42
  2.2 0.2 fusion.8
  2.4 0.1 convert_element_type.29
  2.5 0.2 fusion.10
  2.7 2.1 %fusion.1.x_ref = bf16[64,8,3584]{2,1,0:T(8,128)(2,1)S(1)} fusion(pred[512,32]{0,1:T(8,128)(4,1)S(1)} %fusion.10, bf16[32,3584]{1,0:T(8,128)(2,1)} %param.11), kind=kOutput, calls=%fused_computation.2 | convolution fusion | flops 119275520 | bytes 3915776 | tf_op jit(solution)/shard_map/dot_general | solution.py:258
  4.8 68.4 %shard_map.122 = bf16[64,8,3584]{2,1,0:T(8,128)(2,1)S(1)} custom-call(bf16[64,8,3584]{2,1,0:T(8,128)(2,1)S(1)} %fusion.1.x_ref), custom_call_target="tpu_custom_call" | custom-call | tf_op jit(solution)/shard_map/pallas_call | solution.py:109
  73.2 0.0 copy-start.1
  73.2 1.8 %copy-done.1 = bf16[64,8,3584]{2,1,0:T(8,128)(2,1)} copy-done((bf16[64,8,3584]{2,1,0:T(8,128)(2,1)}, bf16[64,8,3584]{2,1,0:T(8,128)(2,1)S(1)}, u32[]{:S(2)}) %copy-start.1) | copy-done | bytes 3670040
  75.1 0.0 collective-permute-done.gt_ref
  75.1 0.0 collective-permute-done.1.ut_ref
  75.1 0.0 collective-permute-done.2.dt_ref
  75.1 21.3 %shard_map.123 = bf16[512,3584]{1,0:T(8,128)(2,1)} custom-call(bf16[512,3584]{1,0:T(8,128)(2,1)} %bitcast.18, bf16[3584,512]{1,0:T(8,128)(2,1)} %bitcast.21, bf16[3584,512]{1,0:T(8,128)(2,1)} %bitcast.23, bf16[3584,512]{1,0:T(8,128)(2,1)} %collective-permute-done.gt_ref, bf16[3584,512]{1,0:T(8,128)(2,1)} %collective-permute-done.1.ut_ref, ...), custom_call_target="tpu_custom_call" | custom-call | flops 11274289152 | bytes 29360128 | tf_op jit(solution)/shard_map/pallas_call | solution.py:180
  96.4 0.0 copy-start.4
  96.4 0.0 copy-start.3
  96.4 0.0 copy-start.5
  96.4 0.0 copy-start.2
  96.4 22.2 %all-to-all-start = ((bf16[64,8,3584]{2,1,0:T(8,128)(2,1)}), bf16[64,8,3584]{2,1,0:T(8,128)(2,1)}, u32[]{:S(2)}, u32[]{:S(2)}) async-start(bf16[64,8,3584]{2,1,0:T(8,128)(2,1)} %bitcast.19), calls=%async_computation | async-start | bytes 7340032 | tf_op jit(solution)/shard_map/all_to_all | solution.py:265
  118.6 0.0 copy-done.4
  118.6 0.1 copy.21
  118.7 0.0 copy-done.3
  118.7 0.1 reshape.76
  118.8 0.2 select_reduce_fusion
  119.0 0.0 copy-done.5
  119.1 0.1 iota_compare_fusion.6
  119.1 0.0 copy-done.2
  119.2 6.0 %fusion.13 = f32[4,64,2048]{2,1,0:T(8,128)S(1)} fusion(bf16[4,64,512]{2,1,0:T(8,128)(2,1)S(1)} %copy-done.2, bf16[4,2048,512]{2,1,0:T(8,128)(2,1)} %param.19), kind=kOutput, calls=%fused_computation.26 | convolution fusion | flops 536870912 | bytes 10747904 | tf_op jit(solution)/shard_map/vmap()/dot_general | solution.py:210
  125.2 0.0 copy-done
  125.2 2.3 %fusion.12 = (f32[4,64]{1,0:T(4,128)S(1)}, f32[4,64,2048]{2,1,0:T(8,128)}) fusion(pred[4,2048]{1,0:T(4,128)(4,1)S(1)} %iota_compare_fusion.6, f32[4,64,2048]{2,1,0:T(8,128)S(1)} %fusion.13, bf16[4,64,64]{2,1,0:T(8,128)(2,1)S(1)} %reshape.76, bf16[4,64,2048]{2,1,0:T(8,128)(2,1)S(1)} %copy-done), kind=kOutput, calls=%fused_computation.25 | convolution fusion | flops 70256640 | bytes 5284864 | tf_op jit(solution)/shard_map/vmap()/sub | solution.py:221
  127.5 6.3 %convolution_convert_fusion.2 = bf16[4,64,512]{2,1,0:T(8,128)(2,1)} fusion(bf16[4,2048,512]{2,1,0:T(8,128)(2,1)} %param.19, f32[4,64,2048]{2,1,0:T(8,128)} %get-tuple-element.3, f32[4,64]{1,0:T(4,128)S(1)} %get-tuple-element.2), kind=kOutput, calls=%fused_computation.12 | convolution fusion | flops 538050560 | bytes 10748928 | tf_op jit(solution)/shard_map/vmap()/dot_general | solution.py:223
  133.9 31.6 %all-to-all-done = bf16[64,8,3584]{2,1,0:T(8,128)(2,1)} async-done(((bf16[64,8,3584]{2,1,0:T(8,128)(2,1)}), bf16[64,8,3584]{2,1,0:T(8,128)(2,1)}, u32[]{:S(2)}, u32[]{:S(2)}) %all-to-all-start) | async-done | bytes 3670048 | tf_op jit(solution)/shard_map/all_to_all | solution.py:265
  165.4 4.6 %convolution_convert_fusion.1 = bf16[32,3584]{1,0:T(8,128)(2,1)} fusion(f32[32,512]{1,0:T(8,128)S(1)} %select_reduce_fusion, bf16[64,8,3584]{2,1,0:T(8,128)(2,1)} %all-to-all-done), kind=kOutput, calls=%fused_computation.3 | convolution fusion | flops 704757760 | bytes 3964928 | tf_op jit(solution)/shard_map/dot_general | solution.py:271
  (2 shorter events, 0.0 us)
Async XLA Ops:
  0.6 124.5 %copy-start = (bf16[4,64,2048]{2,1,0:T(8,128)(2,1)S(1)}, bf16[4,64,2048]{2,1,0:T(8,128)(2,1)}, u32[]{:S(2)}) copy-start(bf16[4,64,2048]{2,1,0:T(8,128)(2,1)} %param.20) | copy-start | bytes 3145732
  0.6 74.4 %collective-permute-start = (bf16[3584,512]{1,0:T(8,128)(2,1)}, bf16[3584,512]{1,0:T(8,128)(2,1)}, u32[]{:S(2)}, u32[]{:S(2)}) collective-permute-start(bf16[3584,512]{1,0:T(8,128)(2,1)} %bitcast.20), channel_id=1, source_target_pairs={{0,64},{64,0},{1,65},{65,1},{2,66},{66,2},{3,67},{67,3},{4,68},{68... | collective-permute-start | bytes 11010056 | tf_op jit(solution)/shard_map/ppermute | solution.py:127
  0.7 74.3 %collective-permute-start.1 = (bf16[3584,512]{1,0:T(8,128)(2,1)}, bf16[3584,512]{1,0:T(8,128)(2,1)}, u32[]{:S(2)}, u32[]{:S(2)}) collective-permute-start(bf16[3584,512]{1,0:T(8,128)(2,1)} %bitcast.22), channel_id=1, source_target_pairs={{0,64},{64,0},{1,65},{65,1},{2,66},{66,2},{3,67},{67,3},{4,68},{68... | collective-permute-start | bytes 11010056 | tf_op jit(solution)/shard_map/ppermute | solution.py:127
  1.2 73.8 %collective-permute-start.2 = (bf16[3584,512]{1,0:T(8,128)(2,1)}, bf16[3584,512]{1,0:T(8,128)(2,1)}, u32[]{:S(2)}, u32[]{:S(2)}) collective-permute-start(bf16[3584,512]{1,0:T(8,128)(2,1)} %bitcast.24), channel_id=1, source_target_pairs={{0,64},{64,0},{1,65},{65,1},{2,66},{66,2},{3,67},{67,3},{4,68},{68... | collective-permute-start | bytes 11010056 | tf_op jit(solution)/shard_map/ppermute | solution.py:127
  73.2 1.8 %copy-start.1 = (bf16[64,8,3584]{2,1,0:T(8,128)(2,1)}, bf16[64,8,3584]{2,1,0:T(8,128)(2,1)S(1)}, u32[]{:S(2)}) copy-start(bf16[64,8,3584]{2,1,0:T(8,128)(2,1)S(1)} %shard_map.122) | copy-start | bytes 11010052
  96.4 22.2 %copy-start.4 = (f32[32,8]{0,1:T(8,128)S(1)}, f32[32,8]{0,1:T(8,128)}, u32[]{:S(2)}) copy-start(f32[32,8]{0,1:T(8,128)} %param.13) | copy-start | bytes 3076
  96.4 22.3 %copy-start.3 = (bf16[4,4096]{1,0:T(4,128)(2,1)S(1)}, bf16[4,4096]{1,0:T(4,128)(2,1)}, u32[]{:S(2)}) copy-start(bf16[4,4096]{1,0:T(4,128)(2,1)} %param.18) | copy-start | bytes 98308
  96.4 22.7 %copy-start.5 = (s32[4]{0:T(128)S(1)}, s32[4]{0:T(128)}, u32[]{:S(2)}) copy-start(s32[4]{0:T(128)} %param.21) | copy-start | bytes 52
  96.4 22.7 %copy-start.2 = (bf16[4,64,512]{2,1,0:T(8,128)(2,1)S(1)}, bf16[4,64,512]{2,1,0:T(8,128)(2,1)}, u32[]{:S(2)}) copy-start(bf16[4,64,512]{2,1,0:T(8,128)(2,1)} %param.17) | copy-start | bytes 786436
  96.4 69.0 %all-to-all-start = ((bf16[64,8,3584]{2,1,0:T(8,128)(2,1)}), bf16[64,8,3584]{2,1,0:T(8,128)(2,1)}, u32[]{:S(2)}, u32[]{:S(2)}) async-start(bf16[64,8,3584]{2,1,0:T(8,128)(2,1)} %bitcast.19), calls=%async_computation | async-start | bytes 7340032 | tf_op jit(solution)/shard_map/all_to_all | solution.py:265

commit v13 on v10

--- a/solution.py
+++ b/solution.py
@@ -213,10 +213,13 @@
         jnp.where(picks, gate_weights.reshape(pair_count)[:, None], 0.0).reshape(tok_count, topk_count, slot_count),
         axis=1,
     )
-    moe_out = jnp.dot(
-        weighted, flat_back.astype(jnp.float32), precision=lax.Precision.HIGHEST,
-        preferred_element_type=jnp.float32,
-    ).astype(jnp.bfloat16)
+    first = lax.reduce_precision(weighted, exponent_bits=8, mantissa_bits=7)
+    rest = weighted - first
+    second = lax.reduce_precision(rest, exponent_bits=8, mantissa_bits=7)
+    parts = [first, second, rest - second]
+    split = jnp.concatenate([part.astype(jnp.bfloat16) for part in parts], axis=0)
+    sums = jnp.dot(split, flat_back, preferred_element_type=jnp.float32)
+    moe_out = (sums[:tok_count] + sums[tok_count:2 * tok_count] + sums[2 * tok_count:]).astype(jnp.bfloat16)
     attended = jax.vmap(attend_row)(q_latent, q_rope, latent_cache, rope_cache, lengths)
     return (moe_out, attended)
 

time: 143 us -> 142 us (level)
    dot_general x1, matrix products: 4.61 us -> 2.76 us  [per_device(): sums = jnp.dot(split, flat_back, preferred_element_type=jnp.float32)]
  transfers between devices with their start and end apart: 4 -> 4, of which waited for: 1 -> 1; matrix products, arithmetic and copies ran while one was open for 13% -> 14% of each run, Pallas kernels for 0% -> 0%
where the time goes in v13:
time: 142 us; the launch traced here: 141 us
  blocking collectives  58.9 us (41%)
  waiting for transfers between devices  30.3 us (21%)
  Pallas kernels  21.3 us (15%)
  matrix products  20.6 us (15%)
  starting transfers between devices  6.42 us (5%)
  local copies, waits for them, and re-layouts  1.79 us (1%)
    all_to_all x1, blocking collectives, per_device(): lax.all_to_all(outgoing, 'dev', split_axis=0, concat_axis=0, tiled=True)  58.9 us
    all_to_all x1, waiting for transfers between devices, per_device(): lax.all_to_all(finished, 'dev', split_axis=0, concat_axis=0, tiled=True)  30.3 us
    pallas_call x1, Pallas kernels, full_expert(): pl.pallas_call(functools.partial(ffn_kernel, steps), out_shape=jax.ShapeD...  21.3 us
    dot_general x1, matrix products, attend_row(): jnp.dot(probs, cache_lat, preferred_element_type=jnp.float32)  6.34 us
    dot_general x1, matrix products, attend_row(): lax.dot_general(query_lat, cache_lat, (((1,), (1,)), ((), ())), preferred...  6 us
    all_to_all x1, starting transfers between devices, per_device(): lax.all_to_all(finished, 'dev', split_axis=0, concat_axis=0, tiled=True)  5.75 us
    sub x1, matrix products, attend_row(): weights = jnp.where(valid, jnp.exp(scores - highest), jnp.float32(0.0))  3.2 us
  transfers between devices with their start and end apart: 4, of which 1 were waited for; matrix products, arithmetic and copies ran while one was open for 14% of the time, Pallas kernels for 0%

profile of v13, /device:TPU:0, one launch (start us, length us, event | category | flops | bytes accessed | tf_op | source)
XLA Modules:
  0.0 141.4 jit_solution(6743563314639147606)
XLA Ops:
  0.6 0.0 copy-start
  0.6 0.1 collective-permute-start
  0.7 0.5 collective-permute-start.1
  1.2 0.1 collective-permute-start.2
  1.3 0.8 copy.19
  2.1 0.1 eq.42
  2.2 0.2 fusion.9
  2.4 0.1 convert_element_type.37
  2.5 0.2 fusion.11
  2.7 2.1 %fusion.1 = bf16[64,8,3584]{2,1,0:T(8,128)(2,1)S(1)} fusion(pred[512,32]{0,1:T(8,128)(4,1)S(1)} %fusion.11, bf16[32,3584]{1,0:T(8,128)(2,1)} %param.11), kind=kOutput, calls=%fused_computation.2 | convolution fusion | flops 119275520 | bytes 3915776 | tf_op jit(solution)/shard_map/dot_general | solution.py:203
  4.8 58.9 %all_to_all.10 = bf16[64,8,3584]{2,1,0:T(8,128)(2,1)} all-to-all(bf16[64,8,3584]{2,1,0:T(8,128)(2,1)S(1)} %fusion.1), channel_id=1, replica_groups=mesh['role'=2,'dev'=64] {'dev'}, dimensions={0} | all-to-all | bytes 7340032 | tf_op jit(solution)/shard_map/all_to_all | solution.py:206
  63.7 0.0 collective-permute-done.gt_ref
  63.7 0.0 collective-permute-done.1.ut_ref
  63.7 0.0 collective-permute-done.2.dt_ref
  63.8 21.3 %shard_map.122 = bf16[512,3584]{1,0:T(8,128)(2,1)} custom-call(bf16[512,3584]{1,0:T(8,128)(2,1)} %bitcast.18, bf16[3584,512]{1,0:T(8,128)(2,1)} %bitcast.20, bf16[3584,512]{1,0:T(8,128)(2,1)} %bitcast.22, bf16[3584,512]{1,0:T(8,128)(2,1)} %collective-permute-done.gt_ref, bf16[3584,512]{1,0:T(8,128)(2,1)} %collective-permute-done.1.ut_ref, ...), custom_call_target="tpu_custom_call" | custom-call | flops 11274289152 | bytes 29360128 | tf_op jit(solution)/shard_map/pallas_call | solution.py:125
  85.1 0.0 copy-start.3
  85.1 0.0 copy-start.2
  85.1 0.0 copy-start.4
  85.1 0.0 copy-start.1
  85.1 5.7 %all-to-all-start.1 = ((bf16[64,8,3584]{2,1,0:T(8,128)(2,1)}), bf16[64,8,3584]{2,1,0:T(8,128)(2,1)}, u32[]{:S(2)}, u32[]{:S(2)}) async-start(bf16[64,8,3584]{2,1,0:T(8,128)(2,1)} %bitcast.17), calls=%async_computation.1 | async-start | bytes 7340032 | tf_op jit(solution)/shard_map/all_to_all | solution.py:210
  90.9 0.0 copy-done.3
  90.9 0.1 copy.21
  91.0 0.0 copy-done.2
  91.0 0.8 reshape.76
  91.7 0.2 select_reduce_fusion
  92.0 0.0 copy-done.4
  92.0 0.1 iota_compare_fusion.6
  92.1 0.0 copy-done.1
  92.1 6.0 %fusion.22 = f32[4,64,2048]{2,1,0:T(8,128)S(1)} fusion(bf16[4,64,512]{2,1,0:T(8,128)(2,1)S(1)} %copy-done.1, bf16[4,2048,512]{2,1,0:T(8,128)(2,1)} %param.19), kind=kOutput, calls=%fused_computation.40 | convolution fusion | flops 536870912 | bytes 10747904 | tf_op jit(solution)/shard_map/vmap()/dot_general | solution.py:155
  98.1 0.0 copy-done
  98.1 3.2 %fusion.21 = (f32[4,64]{1,0:T(4,128)S(1)}, f32[4,64,2048]{2,1,0:T(8,128)}) fusion(pred[4,2048]{1,0:T(4,128)(4,1)S(1)} %iota_compare_fusion.6, f32[4,64,2048]{2,1,0:T(8,128)S(1)} %fusion.22, bf16[4,64,64]{2,1,0:T(8,128)(2,1)} %reshape.76, bf16[4,64,2048]{2,1,0:T(8,128)(2,1)S(1)} %copy-done), kind=kOutput, calls=%fused_computation.39 | convolution fusion | flops 70256640 | bytes 5284864 | tf_op jit(solution)/shard_map/vmap()/sub | solution.py:166
  101.3 6.3 %convolution_convert_fusion.1 = bf16[4,64,512]{2,1,0:T(8,128)(2,1)} fusion(bf16[4,2048,512]{2,1,0:T(8,128)(2,1)} %param.19, f32[4,64,2048]{2,1,0:T(8,128)} %get-tuple-element.6, f32[4,64]{1,0:T(4,128)S(1)} %get-tuple-element.5), kind=kOutput, calls=%fused_computation.12 | convolution fusion | flops 538050560 | bytes 10748928 | tf_op jit(solution)/shard_map/vmap()/dot_general | solution.py:168
  107.6 30.3 %all-to-all-done.1 = bf16[64,8,3584]{2,1,0:T(8,128)(2,1)} async-done(((bf16[64,8,3584]{2,1,0:T(8,128)(2,1)}), bf16[64,8,3584]{2,1,0:T(8,128)(2,1)}, u32[]{:S(2)}, u32[]{:S(2)}) %all-to-all-start.1) | async-done | bytes 3670048 | tf_op jit(solution)/shard_map/all_to_all | solution.py:210
  137.9 2.8 %fusion.2 = f32[96,3584]{1,0:T(8,128)S(1)} fusion(bf16[64,8,3584]{2,1,0:T(8,128)(2,1)} %all-to-all-done.1, bf16[32,512]{1,0:T(8,128)(2,1)S(1)} %get-tuple-element.3, bf16[32,512]{1,0:T(8,128)(2,1)S(1)} %get-tuple-element.4, bf16[32,512]{1,0:T(8,128)(2,1)S(1)} %get-tuple-element.2), kind=kOutput, calls=%fused_computation.3 | convolution fusion | flops 352616448 | bytes 5144576 | tf_op jit(solution)/shard_map/dot_general | solution.py:221
  140.7 0.8 fusion.12
  (3 shorter events, 0.0 us)
Async XLA Ops:
  0.6 97.4 %copy-start = (bf16[4,64,2048]{2,1,0:T(8,128)(2,1)S(1)}, bf16[4,64,2048]{2,1,0:T(8,128)(2,1)}, u32[]{:S(2)}) copy-start(bf16[4,64,2048]{2,1,0:T(8,128)(2,1)} %param.20) | copy-start | bytes 3145732
  0.6 63.1 %collective-permute-start = (bf16[3584,512]{1,0:T(8,128)(2,1)}, bf16[3584,512]{1,0:T(8,128)(2,1)}, u32[]{:S(2)}, u32[]{:S(2)}) collective-permute-start(bf16[3584,512]{1,0:T(8,128)(2,1)} %bitcast.19), channel_id=1, source_target_pairs={{0,64},{64,0},{1,65},{65,1},{2,66},{66,2},{3,67},{67,3},{4,68},{68... | collective-permute-start | bytes 11010056 | tf_op jit(solution)/shard_map/ppermute | solution.py:72
  0.7 63.0 %collective-permute-start.1 = (bf16[3584,512]{1,0:T(8,128)(2,1)}, bf16[3584,512]{1,0:T(8,128)(2,1)}, u32[]{:S(2)}, u32[]{:S(2)}) collective-permute-start(bf16[3584,512]{1,0:T(8,128)(2,1)} %bitcast.21), channel_id=1, source_target_pairs={{0,64},{64,0},{1,65},{65,1},{2,66},{66,2},{3,67},{67,3},{4,68},{68... | collective-permute-start | bytes 11010056 | tf_op jit(solution)/shard_map/ppermute | solution.py:72
  1.2 62.5 %collective-permute-start.2 = (bf16[3584,512]{1,0:T(8,128)(2,1)}, bf16[3584,512]{1,0:T(8,128)(2,1)}, u32[]{:S(2)}, u32[]{:S(2)}) collective-permute-start(bf16[3584,512]{1,0:T(8,128)(2,1)} %bitcast.23), channel_id=1, source_target_pairs={{0,64},{64,0},{1,65},{65,1},{2,66},{66,2},{3,67},{67,3},{4,68},{68... | collective-permute-start | bytes 11010056 | tf_op jit(solution)/shard_map/ppermute | solution.py:72
  85.1 5.8 %copy-start.3 = (f32[32,8]{0,1:T(8,128)S(1)}, f32[32,8]{0,1:T(8,128)}, u32[]{:S(2)}) copy-start(f32[32,8]{0,1:T(8,128)} %param.13) | copy-start | bytes 3076
  85.1 5.9 %copy-start.2 = (bf16[4,4096]{1,0:T(4,128)(2,1)S(1)}, bf16[4,4096]{1,0:T(4,128)(2,1)}, u32[]{:S(2)}) copy-start(bf16[4,4096]{1,0:T(4,128)(2,1)} %param.18) | copy-start | bytes 98308
  85.1 6.9 %copy-start.4 = (s32[4]{0:T(128)S(1)}, s32[4]{0:T(128)}, u32[]{:S(2)}) copy-start(s32[4]{0:T(128)} %param.21) | copy-start | bytes 52
  85.1 7.0 %copy-start.1 = (bf16[4,64,512]{2,1,0:T(8,128)(2,1)S(1)}, bf16[4,64,512]{2,1,0:T(8,128)(2,1)}, u32[]{:S(2)}) copy-start(bf16[4,64,512]{2,1,0:T(8,128)(2,1)} %param.17) | copy-start | bytes 786436
  85.1 52.8 %all-to-all-start.1 = ((bf16[64,8,3584]{2,1,0:T(8,128)(2,1)}), bf16[64,8,3584]{2,1,0:T(8,128)(2,1)}, u32[]{:S(2)}, u32[]{:S(2)}) async-start(bf16[64,8,3584]{2,1,0:T(8,128)(2,1)} %bitcast.17), calls=%async_computation.1 | async-start | bytes 7340032 | tf_op jit(solution)/shard_map/all_to_all | solution.py:210

commit v14 on v13

--- a/solution.py
+++ b/solution.py
@@ -104,7 +104,7 @@
         o_ref[...] = total.astype(o_ref.dtype)
 
 
-def full_expert(rows, w_gate, w_up, w_down, unit_tile=256, out_tile=896):
+def full_expert(rows, w_gate, w_up, w_down, unit_tile=256, out_tile=1792):
     count, width = rows.shape
     own = (w_gate[0], w_up[0], w_down[0])
     other = tuple(other_half(w) for w in own)

time: 142 us -> 141 us (level)
  no operation moved by 1% of the time
where the time goes in v14:
time: 141 us
  blocking collectives  58.9 us (42%)
  waiting for transfers between devices  30.1 us (21%)
  matrix products  20.6 us (15%)
  Pallas kernels  20.6 us (15%)
  starting transfers between devices  6.61 us (5%)
  local copies, waits for them, and re-layouts  1.79 us (1%)
    all_to_all x1, blocking collectives, per_device(): lax.all_to_all(outgoing, 'dev', split_axis=0, concat_axis=0, tiled=True)  58.9 us
    all_to_all x1, waiting for transfers between devices, per_device(): lax.all_to_all(finished, 'dev', split_axis=0, concat_axis=0, tiled=True)  30.1 us
    pallas_call x1, Pallas kernels, full_expert(): pl.pallas_call(functools.partial(ffn_kernel, steps), out_shape=jax.ShapeD...  20.6 us
    dot_general x1, matrix products, attend_row(): jnp.dot(probs, cache_lat, preferred_element_type=jnp.float32)  6.34 us
    dot_general x1, matrix products, attend_row(): lax.dot_general(query_lat, cache_lat, (((1,), (1,)), ((), ())), preferred...  6 us
    all_to_all x1, starting transfers between devices, per_device(): lax.all_to_all(finished, 'dev', split_axis=0, concat_axis=0, tiled=True)  5.93 us
    sub x1, matrix products, attend_row(): weights = jnp.where(valid, jnp.exp(scores - highest), jnp.float32(0.0))  3.2 us
  transfers between devices with their start and end apart: 4, of which 1 were waited for; matrix products, arithmetic and copies ran while one was open for 14% of the time, Pallas kernels for 0%

profile of v14, /device:TPU:0, one launch (start us, length us, event | category | flops | bytes accessed | tf_op | source)
XLA Modules:
  0.0 140.7 jit_solution(6112186859968307378)
XLA Ops:
  0.6 0.0 copy-start
  0.6 0.1 collective-permute-start
  0.7 0.5 collective-permute-start.1
  1.2 0.1 collective-permute-start.2
  1.3 0.8 copy.19
  2.1 0.1 eq.42
  2.2 0.2 fusion.9
  2.4 0.1 convert_element_type.37
  2.5 0.2 fusion.11
  2.7 2.1 %fusion.1 = bf16[64,8,3584]{2,1,0:T(8,128)(2,1)S(1)} fusion(pred[512,32]{0,1:T(8,128)(4,1)S(1)} %fusion.11, bf16[32,3584]{1,0:T(8,128)(2,1)} %param.11), kind=kOutput, calls=%fused_computation.2 | convolution fusion | flops 119275520 | bytes 3915776 | tf_op jit(solution)/shard_map/dot_general | solution.py:203
  4.9 58.9 %all_to_all.10 = bf16[64,8,3584]{2,1,0:T(8,128)(2,1)} all-to-all(bf16[64,8,3584]{2,1,0:T(8,128)(2,1)S(1)} %fusion.1), channel_id=1, replica_groups=mesh['role'=2,'dev'=64] {'dev'}, dimensions={0} | all-to-all | bytes 7340032 | tf_op jit(solution)/shard_map/all_to_all | solution.py:206
  63.7 0.0 collective-permute-done.gt_ref
  63.7 0.0 collective-permute-done.1.ut_ref
  63.7 0.0 collective-permute-done.2.dt_ref
  63.8 20.6 %shard_map.122 = bf16[512,3584]{1,0:T(8,128)(2,1)} custom-call(bf16[512,3584]{1,0:T(8,128)(2,1)} %bitcast.18, bf16[3584,512]{1,0:T(8,128)(2,1)} %bitcast.20, bf16[3584,512]{1,0:T(8,128)(2,1)} %bitcast.22, bf16[3584,512]{1,0:T(8,128)(2,1)} %collective-permute-done.gt_ref, bf16[3584,512]{1,0:T(8,128)(2,1)} %collective-permute-done.1.ut_ref, ...), custom_call_target="tpu_custom_call" | custom-call | flops 11274289152 | bytes 29360128 | tf_op jit(solution)/shard_map/pallas_call | solution.py:125
  84.3 0.0 copy-start.3
  84.3 0.0 copy-start.2
  84.3 0.0 copy-start.4
  84.4 0.0 copy-start.1
  84.4 5.9 %all-to-all-start.1 = ((bf16[64,8,3584]{2,1,0:T(8,128)(2,1)}), bf16[64,8,3584]{2,1,0:T(8,128)(2,1)}, u32[]{:S(2)}, u32[]{:S(2)}) async-start(bf16[64,8,3584]{2,1,0:T(8,128)(2,1)} %bitcast.17), calls=%async_computation.1 | async-start | bytes 7340032 | tf_op jit(solution)/shard_map/all_to_all | solution.py:210
  90.3 0.0 copy-done.3
  90.3 0.1 copy.21
  90.4 0.0 copy-done.2
  90.4 0.8 reshape.76
  91.1 0.2 select_reduce_fusion
  91.4 0.0 copy-done.4
  91.4 0.1 iota_compare_fusion.6
  91.5 0.0 copy-done.1
  91.5 6.0 %fusion.22 = f32[4,64,2048]{2,1,0:T(8,128)S(1)} fusion(bf16[4,64,512]{2,1,0:T(8,128)(2,1)S(1)} %copy-done.1, bf16[4,2048,512]{2,1,0:T(8,128)(2,1)} %param.19), kind=kOutput, calls=%fused_computation.40 | convolution fusion | flops 536870912 | bytes 10747904 | tf_op jit(solution)/shard_map/vmap()/dot_general | solution.py:155
  97.5 0.0 copy-done
  97.5 3.2 %fusion.21 = (f32[4,64]{1,0:T(4,128)S(1)}, f32[4,64,2048]{2,1,0:T(8,128)}) fusion(pred[4,2048]{1,0:T(4,128)(4,1)S(1)} %iota_compare_fusion.6, f32[4,64,2048]{2,1,0:T(8,128)S(1)} %fusion.22, bf16[4,64,64]{2,1,0:T(8,128)(2,1)} %reshape.76, bf16[4,64,2048]{2,1,0:T(8,128)(2,1)S(1)} %copy-done), kind=kOutput, calls=%fused_computation.39 | convolution fusion | flops 70256640 | bytes 5284864 | tf_op jit(solution)/shard_map/vmap()/sub | solution.py:166
  100.7 6.3 %convolution_convert_fusion.1 = bf16[4,64,512]{2,1,0:T(8,128)(2,1)} fusion(bf16[4,2048,512]{2,1,0:T(8,128)(2,1)} %param.19, f32[4,64,2048]{2,1,0:T(8,128)} %get-tuple-element.6, f32[4,64]{1,0:T(4,128)S(1)} %get-tuple-element.5), kind=kOutput, calls=%fused_computation.12 | convolution fusion | flops 538050560 | bytes 10748928 | tf_op jit(solution)/shard_map/vmap()/dot_general | solution.py:168
  107.1 30.1 %all-to-all-done.1 = bf16[64,8,3584]{2,1,0:T(8,128)(2,1)} async-done(((bf16[64,8,3584]{2,1,0:T(8,128)(2,1)}), bf16[64,8,3584]{2,1,0:T(8,128)(2,1)}, u32[]{:S(2)}, u32[]{:S(2)}) %all-to-all-start.1) | async-done | bytes 3670048 | tf_op jit(solution)/shard_map/all_to_all | solution.py:210
  137.2 2.8 %fusion.2 = f32[96,3584]{1,0:T(8,128)S(1)} fusion(bf16[64,8,3584]{2,1,0:T(8,128)(2,1)} %all-to-all-done.1, bf16[32,512]{1,0:T(8,128)(2,1)S(1)} %get-tuple-element.3, bf16[32,512]{1,0:T(8,128)(2,1)S(1)} %get-tuple-element.4, bf16[32,512]{1,0:T(8,128)(2,1)S(1)} %get-tuple-element.2), kind=kOutput, calls=%fused_computation.3 | convolution fusion | flops 352616448 | bytes 5144576 | tf_op jit(solution)/shard_map/dot_general | solution.py:221
  139.9 0.8 fusion.12
  (3 shorter events, 0.0 us)
Async XLA Ops:
  0.6 96.9 %copy-start = (bf16[4,64,2048]{2,1,0:T(8,128)(2,1)S(1)}, bf16[4,64,2048]{2,1,0:T(8,128)(2,1)}, u32[]{:S(2)}) copy-start(bf16[4,64,2048]{2,1,0:T(8,128)(2,1)} %param.20) | copy-start | bytes 3145732
  0.6 63.1 %collective-permute-start = (bf16[3584,512]{1,0:T(8,128)(2,1)}, bf16[3584,512]{1,0:T(8,128)(2,1)}, u32[]{:S(2)}, u32[]{:S(2)}) collective-permute-start(bf16[3584,512]{1,0:T(8,128)(2,1)} %bitcast.19), channel_id=1, source_target_pairs={{0,64},{64,0},{1,65},{65,1},{2,66},{66,2},{3,67},{67,3},{4,68},{68... | collective-permute-start | bytes 11010056 | tf_op jit(solution)/shard_map/ppermute | solution.py:72
  0.7 63.0 %collective-permute-start.1 = (bf16[3584,512]{1,0:T(8,128)(2,1)}, bf16[3584,512]{1,0:T(8,128)(2,1)}, u32[]{:S(2)}, u32[]{:S(2)}) collective-permute-start(bf16[3584,512]{1,0:T(8,128)(2,1)} %bitcast.21), channel_id=1, source_target_pairs={{0,64},{64,0},{1,65},{65,1},{2,66},{66,2},{3,67},{67,3},{4,68},{68... | collective-permute-start | bytes 11010056 | tf_op jit(solution)/shard_map/ppermute | solution.py:72
  1.2 62.5 %collective-permute-start.2 = (bf16[3584,512]{1,0:T(8,128)(2,1)}, bf16[3584,512]{1,0:T(8,128)(2,1)}, u32[]{:S(2)}, u32[]{:S(2)}) collective-permute-start(bf16[3584,512]{1,0:T(8,128)(2,1)} %bitcast.23), channel_id=1, source_target_pairs={{0,64},{64,0},{1,65},{65,1},{2,66},{66,2},{3,67},{67,3},{4,68},{68... | collective-permute-start | bytes 11010056 | tf_op jit(solution)/shard_map/ppermute | solution.py:72
  84.3 6.0 %copy-start.3 = (f32[32,8]{0,1:T(8,128)S(1)}, f32[32,8]{0,1:T(8,128)}, u32[]{:S(2)}) copy-start(f32[32,8]{0,1:T(8,128)} %param.13) | copy-start | bytes 3076
  84.3 6.1 %copy-start.2 = (bf16[4,4096]{1,0:T(4,128)(2,1)S(1)}, bf16[4,4096]{1,0:T(4,128)(2,1)}, u32[]{:S(2)}) copy-start(bf16[4,4096]{1,0:T(4,128)(2,1)} %param.18) | copy-start | bytes 98308
  84.3 7.1 %copy-start.4 = (s32[4]{0:T(128)S(1)}, s32[4]{0:T(128)}, u32[]{:S(2)}) copy-start(s32[4]{0:T(128)} %param.21) | copy-start | bytes 52
  84.4 7.1 %copy-start.1 = (bf16[4,64,512]{2,1,0:T(8,128)(2,1)S(1)}, bf16[4,64,512]{2,1,0:T(8,128)(2,1)}, u32[]{:S(2)}) copy-start(bf16[4,64,512]{2,1,0:T(8,128)(2,1)} %param.17) | copy-start | bytes 786436
  84.4 52.8 %all-to-all-start.1 = ((bf16[64,8,3584]{2,1,0:T(8,128)(2,1)}), bf16[64,8,3584]{2,1,0:T(8,128)(2,1)}, u32[]{:S(2)}, u32[]{:S(2)}) async-start(bf16[64,8,3584]{2,1,0:T(8,128)(2,1)} %bitcast.17), calls=%async_computation.1 | async-start | bytes 7340032 | tf_op jit(solution)/shard_map/all_to_all | solution.py:210

commit v15 on v14

--- a/solution.py
+++ b/solution.py
@@ -186,19 +186,18 @@
     topk_count = expert_ids.shape[1]
     experts = lax.axis_size("dev")
     capacity = min(tok_count, 2 * tok_count * topk_count // experts)
-    flat_ids = expert_ids.reshape(-1)
-    pair_count = flat_ids.shape[0]
     slot_count = experts * capacity
-    one_hot = flat_ids[:, None] == jnp.arange(experts, dtype=jnp.int32)[None, :]
-    pair_iota = jnp.arange(pair_count, dtype=jnp.int32)
-    lower = (pair_iota[:, None] > pair_iota[None, :]).astype(jnp.bfloat16)
-    earlier = jnp.dot(lower, one_hot.astype(jnp.bfloat16), preferred_element_type=jnp.float32)
-    slot_index = jnp.sum(jnp.where(one_hot, earlier, 0.0), axis=1).astype(jnp.int32)
-    destination = flat_ids * capacity + slot_index
+    expert_iota = jnp.arange(experts, dtype=jnp.int32)
+    named = expert_ids[:, :, None] == expert_iota[None, None, :]
+    row_iota = jnp.arange(tok_count, dtype=jnp.int32)
+    lower = (row_iota[:, None] > row_iota[None, :]).astype(jnp.bfloat16)
+    earlier = jnp.dot(lower, jnp.any(named, axis=1).astype(jnp.bfloat16), preferred_element_type=jnp.float32)
+    slot_index = jnp.sum(jnp.where(named, earlier[:, None, :], 0.0), axis=2).astype(jnp.int32)
+    destination = expert_ids * capacity + slot_index
     slot_iota = jnp.arange(slot_count, dtype=jnp.int32)
-    picks = destination[:, None] == slot_iota[None, :]
+    picks = destination[:, :, None] == slot_iota[None, None, :]
     dispatch = jnp.any(
-        destination.reshape(tok_count, topk_count)[None, :, :] == slot_iota[:, None, None], axis=2
+        destination[None, :, :] == slot_iota[:, None, None], axis=2
     )
     outgoing = jnp.dot(
         dispatch.astype(jnp.bfloat16), moe_rows, preferred_element_type=jnp.float32
@@ -209,10 +208,7 @@
     finished = expert_sum.reshape(experts, capacity, width)
     returned = lax.all_to_all(finished, "dev", split_axis=0, concat_axis=0, tiled=True)
     flat_back = returned.reshape(slot_count, width)
-    weighted = jnp.sum(
-        jnp.where(picks, gate_weights.reshape(pair_count)[:, None], 0.0).reshape(tok_count, topk_count, slot_count),
-        axis=1,
-    )
+    weighted = jnp.sum(jnp.where(picks, gate_weights[:, :, None], 0.0), axis=1)
     first = lax.reduce_precision(weighted, exponent_bits=8, mantissa_bits=7)
     rest = weighted - first
     second = lax.reduce_precision(rest, exponent_bits=8, mantissa_bits=7)

time: 141 us -> 141 us (level)
  no operation moved by 1% of the time
where the time goes in v15:
time: 141 us
  blocking collectives  58.9 us (42%)
  waiting for transfers between devices  30.1 us (21%)
  Pallas kernels  20.6 us (15%)
  matrix products  20.5 us (15%)
  starting transfers between devices  6.61 us (5%)
  local copies, waits for them, and re-layouts  1.62 us (1%)
  other arithmetic  1.62 us (1%)
    all_to_all x1, blocking collectives, per_device(): lax.all_to_all(outgoing, 'dev', split_axis=0, concat_axis=0, tiled=True)  58.9 us
    all_to_all x1, waiting for transfers between devices, per_device(): lax.all_to_all(finished, 'dev', split_axis=0, concat_axis=0, tiled=True)  30.1 us
    pallas_call x1, Pallas kernels, full_expert(): pl.pallas_call(functools.partial(ffn_kernel, steps), out_shape=jax.ShapeD...  20.6 us
    dot_general x1, matrix products, attend_row(): jnp.dot(probs, cache_lat, preferred_element_type=jnp.float32)  6.34 us
    dot_general x1, matrix products, attend_row(): lax.dot_general(query_lat, cache_lat, (((1,), (1,)), ((), ())), preferred...  6 us
    all_to_all x1, starting transfers between devices, per_device(): lax.all_to_all(finished, 'dev', split_axis=0, concat_axis=0, tiled=True)  5.93 us
    sub x1, matrix products, attend_row(): weights = jnp.where(valid, jnp.exp(scores - highest), jnp.float32(0.0))  3.2 us
  transfers between devices with their start and end apart: 4, of which 1 were waited for; matrix products, arithmetic and copies ran while one was open for 14% of the time, Pallas kernels for 0%

profile of v15, /device:TPU:0, one launch (start us, length us, event | category | flops | bytes accessed | tf_op | source)
XLA Modules:
  0.0 140.7 jit_solution(4013976389154737978)
XLA Ops:
  0.6 0.0 copy-start
  0.6 0.1 collective-permute-start
  0.7 0.5 collective-permute-start.1
  1.2 0.1 collective-permute-start.2
  1.3 0.8 copy.17
  2.1 0.1 fusion.12
  2.2 0.1 fusion.19
  2.3 0.2 select_reduce_fusion.1
  2.5 0.2 fusion.10
  2.8 2.1 %fusion.1 = bf16[64,8,3584]{2,1,0:T(8,128)(2,1)S(1)} fusion(pred[512,32]{0,1:T(8,128)(4,1)S(1)} %fusion.10, bf16[32,3584]{1,0:T(8,128)(2,1)} %param.11), kind=kOutput, calls=%fused_computation.2 | convolution fusion | flops 119275520 | bytes 3915776 | tf_op jit(solution)/shard_map/dot_general | solution.py:202
  4.9 58.9 %all_to_all.10 = bf16[64,8,3584]{2,1,0:T(8,128)(2,1)} all-to-all(bf16[64,8,3584]{2,1,0:T(8,128)(2,1)S(1)} %fusion.1), channel_id=1, replica_groups=mesh['role'=2,'dev'=64] {'dev'}, dimensions={0} | all-to-all | bytes 7340032 | tf_op jit(solution)/shard_map/all_to_all | solution.py:205
  63.8 0.0 collective-permute-done.gt_ref
  63.8 0.0 collective-permute-done.1.ut_ref
  63.8 0.0 collective-permute-done.2.dt_ref
  63.8 20.6 %shard_map.122 = bf16[512,3584]{1,0:T(8,128)(2,1)} custom-call(bf16[512,3584]{1,0:T(8,128)(2,1)} %bitcast.19, bf16[3584,512]{1,0:T(8,128)(2,1)} %bitcast.21, bf16[3584,512]{1,0:T(8,128)(2,1)} %bitcast.23, bf16[3584,512]{1,0:T(8,128)(2,1)} %collective-permute-done.gt_ref, bf16[3584,512]{1,0:T(8,128)(2,1)} %collective-permute-done.1.ut_ref, ...), custom_call_target="tpu_custom_call" | custom-call | flops 11274289152 | bytes 29360128 | tf_op jit(solution)/shard_map/pallas_call | solution.py:125
  84.4 0.0 copy-start.3
  84.4 0.0 copy-start.2
  84.4 0.0 copy-start.4
  84.4 0.0 copy-start.1
  84.4 5.9 %all-to-all-start.1 = ((bf16[64,8,3584]{2,1,0:T(8,128)(2,1)}), bf16[64,8,3584]{2,1,0:T(8,128)(2,1)}, u32[]{:S(2)}, u32[]{:S(2)}) async-start(bf16[64,8,3584]{2,1,0:T(8,128)(2,1)} %bitcast.18), calls=%async_computation.1 | async-start | bytes 7340032 | tf_op jit(solution)/shard_map/all_to_all | solution.py:209
  90.3 0.0 copy-done.3
  90.3 0.1 copy.19
  90.4 0.0 copy-done.2
  90.4 0.8 reshape.47
  91.2 0.2 select_reduce_fusion
  91.4 0.0 copy-done.4
  91.4 0.1 iota_compare_fusion.3
  91.5 0.0 copy-done.1
  91.5 6.0 %fusion.22 = f32[4,64,2048]{2,1,0:T(8,128)S(1)} fusion(bf16[4,64,512]{2,1,0:T(8,128)(2,1)S(1)} %copy-done.1, bf16[4,2048,512]{2,1,0:T(8,128)(2,1)} %param.19), kind=kOutput, calls=%fused_computation.40 | convolution fusion | flops 536870912 | bytes 10747904 | tf_op jit(solution)/shard_map/vmap()/dot_general | solution.py:155
  97.5 0.0 copy-done
  97.6 3.2 %fusion.21 = (f32[4,64]{1,0:T(4,128)S(1)}, f32[4,64,2048]{2,1,0:T(8,128)}) fusion(pred[4,2048]{1,0:T(4,128)(4,1)S(1)} %iota_compare_fusion.3, f32[4,64,2048]{2,1,0:T(8,128)S(1)} %fusion.22, bf16[4,64,64]{2,1,0:T(8,128)(2,1)} %reshape.47, bf16[4,64,2048]{2,1,0:T(8,128)(2,1)S(1)} %copy-done), kind=kOutput, calls=%fused_computation.39 | convolution fusion | flops 70256640 | bytes 5284864 | tf_op jit(solution)/shard_map/vmap()/sub | solution.py:166
  100.8 6.3 %convolution_convert_fusion.1 = bf16[4,64,512]{2,1,0:T(8,128)(2,1)} fusion(bf16[4,2048,512]{2,1,0:T(8,128)(2,1)} %param.19, f32[4,64,2048]{2,1,0:T(8,128)} %get-tuple-element.6, f32[4,64]{1,0:T(4,128)S(1)} %get-tuple-element.5), kind=kOutput, calls=%fused_computation.12 | convolution fusion | flops 538050560 | bytes 10748928 | tf_op jit(solution)/shard_map/vmap()/dot_general | solution.py:168
  107.1 30.1 %all-to-all-done.1 = bf16[64,8,3584]{2,1,0:T(8,128)(2,1)} async-done(((bf16[64,8,3584]{2,1,0:T(8,128)(2,1)}), bf16[64,8,3584]{2,1,0:T(8,128)(2,1)}, u32[]{:S(2)}, u32[]{:S(2)}) %all-to-all-start.1) | async-done | bytes 3670048 | tf_op jit(solution)/shard_map/all_to_all | solution.py:209
  137.2 2.8 %fusion.2 = f32[96,3584]{1,0:T(8,128)S(1)} fusion(bf16[64,8,3584]{2,1,0:T(8,128)(2,1)} %all-to-all-done.1, bf16[32,512]{1,0:T(8,128)(2,1)S(1)} %get-tuple-element.3, bf16[32,512]{1,0:T(8,128)(2,1)S(1)} %get-tuple-element.4, bf16[32,512]{1,0:T(8,128)(2,1)S(1)} %get-tuple-element.2), kind=kOutput, calls=%fused_computation.3 | convolution fusion | flops 352616448 | bytes 5144576 | tf_op jit(solution)/shard_map/dot_general | solution.py:217
  139.9 0.8 fusion.11
  (2 shorter events, 0.0 us)
Async XLA Ops:
  0.6 96.9 %copy-start = (bf16[4,64,2048]{2,1,0:T(8,128)(2,1)S(1)}, bf16[4,64,2048]{2,1,0:T(8,128)(2,1)}, u32[]{:S(2)}) copy-start(bf16[4,64,2048]{2,1,0:T(8,128)(2,1)} %param.20) | copy-start | bytes 3145732
  0.6 63.1 %collective-permute-start = (bf16[3584,512]{1,0:T(8,128)(2,1)}, bf16[3584,512]{1,0:T(8,128)(2,1)}, u32[]{:S(2)}, u32[]{:S(2)}) collective-permute-start(bf16[3584,512]{1,0:T(8,128)(2,1)} %bitcast.20), channel_id=1, source_target_pairs={{0,64},{64,0},{1,65},{65,1},{2,66},{66,2},{3,67},{67,3},{4,68},{68... | collective-permute-start | bytes 11010056 | tf_op jit(solution)/shard_map/ppermute | solution.py:72
  0.7 63.0 %collective-permute-start.1 = (bf16[3584,512]{1,0:T(8,128)(2,1)}, bf16[3584,512]{1,0:T(8,128)(2,1)}, u32[]{:S(2)}, u32[]{:S(2)}) collective-permute-start(bf16[3584,512]{1,0:T(8,128)(2,1)} %bitcast.22), channel_id=1, source_target_pairs={{0,64},{64,0},{1,65},{65,1},{2,66},{66,2},{3,67},{67,3},{4,68},{68... | collective-permute-start | bytes 11010056 | tf_op jit(solution)/shard_map/ppermute | solution.py:72
  1.2 62.5 %collective-permute-start.2 = (bf16[3584,512]{1,0:T(8,128)(2,1)}, bf16[3584,512]{1,0:T(8,128)(2,1)}, u32[]{:S(2)}, u32[]{:S(2)}) collective-permute-start(bf16[3584,512]{1,0:T(8,128)(2,1)} %bitcast.24), channel_id=1, source_target_pairs={{0,64},{64,0},{1,65},{65,1},{2,66},{66,2},{3,67},{67,3},{4,68},{68... | collective-permute-start | bytes 11010056 | tf_op jit(solution)/shard_map/ppermute | solution.py:72
  84.4 6.0 %copy-start.3 = (f32[32,8]{0,1:T(8,128)S(1)}, f32[32,8]{0,1:T(8,128)}, u32[]{:S(2)}) copy-start(f32[32,8]{0,1:T(8,128)} %param.13) | copy-start | bytes 3076
  84.4 6.1 %copy-start.2 = (bf16[4,4096]{1,0:T(4,128)(2,1)S(1)}, bf16[4,4096]{1,0:T(4,128)(2,1)}, u32[]{:S(2)}) copy-start(bf16[4,4096]{1,0:T(4,128)(2,1)} %param.18) | copy-start | bytes 98308
  84.4 7.1 %copy-start.4 = (s32[4]{0:T(128)S(1)}, s32[4]{0:T(128)}, u32[]{:S(2)}) copy-start(s32[4]{0:T(128)} %param.21) | copy-start | bytes 52
  84.4 7.1 %copy-start.1 = (bf16[4,64,512]{2,1,0:T(8,128)(2,1)S(1)}, bf16[4,64,512]{2,1,0:T(8,128)(2,1)}, u32[]{:S(2)}) copy-start(bf16[4,64,512]{2,1,0:T(8,128)(2,1)} %param.17) | copy-start | bytes 786436
  84.4 52.8 %all-to-all-start.1 = ((bf16[64,8,3584]{2,1,0:T(8,128)(2,1)}), bf16[64,8,3584]{2,1,0:T(8,128)(2,1)}, u32[]{:S(2)}, u32[]{:S(2)}) async-start(bf16[64,8,3584]{2,1,0:T(8,128)(2,1)} %bitcast.18), calls=%async_computation.1 | async-start | bytes 7340032 | tf_op jit(solution)/shard_map/all_to_all | solution.py:209

commit v16 on v15

--- a/solution.py
+++ b/solution.py
@@ -188,17 +188,16 @@
     capacity = min(tok_count, 2 * tok_count * topk_count // experts)
     slot_count = experts * capacity
     expert_iota = jnp.arange(experts, dtype=jnp.int32)
-    named = expert_ids[:, :, None] == expert_iota[None, None, :]
+    ids_t = expert_ids.T
+    named = ids_t[:, :, None] == expert_iota[None, None, :]
     row_iota = jnp.arange(tok_count, dtype=jnp.int32)
     lower = (row_iota[:, None] > row_iota[None, :]).astype(jnp.bfloat16)
-    earlier = jnp.dot(lower, jnp.any(named, axis=1).astype(jnp.bfloat16), preferred_element_type=jnp.float32)
-    slot_index = jnp.sum(jnp.where(named, earlier[:, None, :], 0.0), axis=2).astype(jnp.int32)
-    destination = expert_ids * capacity + slot_index
+    earlier = jnp.dot(lower, jnp.any(named, axis=0).astype(jnp.bfloat16), preferred_element_type=jnp.float32)
+    slot_index = jnp.sum(jnp.where(named, earlier[None, :, :], 0.0), axis=2).astype(jnp.int32)
+    destination = ids_t * capacity + slot_index
     slot_iota = jnp.arange(slot_count, dtype=jnp.int32)
     picks = destination[:, :, None] == slot_iota[None, None, :]
-    dispatch = jnp.any(
-        destination[None, :, :] == slot_iota[:, None, None], axis=2
-    )
+    dispatch = jnp.any(destination[None, :, :] == slot_iota[:, None, None], axis=1)
     outgoing = jnp.dot(
         dispatch.astype(jnp.bfloat16), moe_rows, preferred_element_type=jnp.float32
     ).astype(jnp.bfloat16).reshape(experts, capacity, width)
@@ -208,7 +207,7 @@
     finished = expert_sum.reshape(experts, capacity, width)
     returned = lax.all_to_all(finished, "dev", split_axis=0, concat_axis=0, tiled=True)
     flat_back = returned.reshape(slot_count, width)
-    weighted = jnp.sum(jnp.where(picks, gate_weights[:, :, None], 0.0), axis=1)
+    weighted = jnp.sum(jnp.where(picks, gate_weights.T[:, :, None], 0.0), axis=0)
     first = lax.reduce_precision(weighted, exponent_bits=8, mantissa_bits=7)
     rest = weighted - first
     second = lax.reduce_precision(rest, exponent_bits=8, mantissa_bits=7)

time: 141 us -> 144 us (1.021)
  other arithmetic: 1.62 us -> 3.47 us
  transfers between devices with their start and end apart: 4 -> 4, of which waited for: 1 -> 1; matrix products, arithmetic and copies ran while one was open for 14% -> 15% of each run, Pallas kernels for 0% -> 0%
where the time goes in v16:
time: 144 us
  blocking collectives  58.9 us (41%)
  waiting for transfers between devices  30.3 us (21%)
  Pallas kernels  20.6 us (14%)
  matrix products  20.5 us (14%)
  starting transfers between devices  6.61 us (5%)
  other arithmetic  3.47 us (2%)
  local copies, waits for them, and re-layouts  2.67 us (2%)
    all_to_all x1, blocking collectives, per_device(): lax.all_to_all(outgoing, 'dev', split_axis=0, concat_axis=0, tiled=True)  58.9 us
    all_to_all x1, waiting for transfers between devices, per_device(): lax.all_to_all(finished, 'dev', split_axis=0, concat_axis=0, tiled=True)  30.3 us
    pallas_call x1, Pallas kernels, full_expert(): pl.pallas_call(functools.partial(ffn_kernel, steps), out_shape=jax.ShapeD...  20.6 us
    dot_general x1, matrix products, attend_row(): jnp.dot(probs, cache_lat, preferred_element_type=jnp.float32)  6.34 us
    dot_general x1, matrix products, attend_row(): lax.dot_general(query_lat, cache_lat, (((1,), (1,)), ((), ())), preferred...  6 us
    all_to_all x1, starting transfers between devices, per_device(): lax.all_to_all(finished, 'dev', split_axis=0, concat_axis=0, tiled=True)  5.93 us
    sub x1, matrix products, attend_row(): weights = jnp.where(valid, jnp.exp(scores - highest), jnp.float32(0.0))  3.2 us
  transfers between devices with their start and end apart: 4, of which 1 were waited for; matrix products, arithmetic and copies ran while one was open for 15% of the time, Pallas kernels for 0%

profile of v16, /device:TPU:0, one launch (start us, length us, event | category | flops | bytes accessed | tf_op | source)
XLA Modules:
  0.0 143.8 jit_solution(14996027955392676342)
XLA Ops:
  0.6 0.0 copy-start
  0.6 0.1 collective-permute-start
  0.7 0.5 collective-permute-start.1
  1.2 0.1 collective-permute-start.2
  1.3 0.8 fusion.12
  2.1 0.1 fusion.19
  2.2 0.9 select_reduce_fusion.1
  3.1 0.7 convert_add_fusion
  3.8 0.1 fusion.10
  4.0 2.1 %fusion.1 = bf16[64,8,3584]{2,1,0:T(8,128)(2,1)S(1)} fusion(pred[512,32]{0,1:T(8,128)(4,1)S(1)} %fusion.10, bf16[32,3584]{1,0:T(8,128)(2,1)} %param.11), kind=kOutput, calls=%fused_computation.2 | convolution fusion | flops 119275520 | bytes 3915776 | tf_op jit(solution)/shard_map/dot_general | solution.py:201
  6.1 58.9 %all_to_all.10 = bf16[64,8,3584]{2,1,0:T(8,128)(2,1)} all-to-all(bf16[64,8,3584]{2,1,0:T(8,128)(2,1)S(1)} %fusion.1), channel_id=1, replica_groups=mesh['role'=2,'dev'=64] {'dev'}, dimensions={0} | all-to-all | bytes 7340032 | tf_op jit(solution)/shard_map/all_to_all | solution.py:204
  65.0 0.0 collective-permute-done.gt_ref
  65.0 0.0 copy-start.5
  65.0 0.0 collective-permute-done.1.ut_ref
  65.0 0.0 collective-permute-done.2.dt_ref
  65.0 1.9 %copy-done.5 = bf16[3584,512]{1,0:T(8,128)(2,1)} copy-done((bf16[3584,512]{1,0:T(8,128)(2,1)}, bf16[3584,512]{1,0:T(8,128)(2,1)S(1)}, u32[]{:S(2)}) %copy-start.5) | copy-done | bytes 3670040
  66.9 20.6 %shard_map.122 = bf16[512,3584]{1,0:T(8,128)(2,1)} custom-call(bf16[512,3584]{1,0:T(8,128)(2,1)} %bitcast.22, bf16[3584,512]{1,0:T(8,128)(2,1)} %bitcast.27, bf16[3584,512]{1,0:T(8,128)(2,1)} %bitcast.29, bf16[3584,512]{1,0:T(8,128)(2,1)} %copy-done.5, bf16[3584,512]{1,0:T(8,128)(2,1)} %collective-permute-done.1.ut_ref, bf16[3584,512]{1,0:T(8,128)(2,1)} %bitcast.31, ...), custom_call_target="tpu_custom_call" | custom-call | flops 11274289152 | bytes 29360128 | tf_op jit(solution)/shard_map/pallas_call | solution.py:125
  87.4 0.0 copy-start.2
  87.4 0.0 copy-start.3
  87.4 0.0 copy-start.4
  87.4 0.0 copy-start.1
  87.5 5.9 %all-to-all-start.1 = ((bf16[64,8,3584]{2,1,0:T(8,128)(2,1)}), bf16[64,8,3584]{2,1,0:T(8,128)(2,1)}, u32[]{:S(2)}, u32[]{:S(2)}) async-start(bf16[64,8,3584]{2,1,0:T(8,128)(2,1)} %bitcast.21), calls=%async_computation.1 | async-start | bytes 7340032 | tf_op jit(solution)/shard_map/all_to_all | solution.py:208
  93.4 0.0 copy-done.2
  93.4 0.8 reshape.47
  94.2 0.0 copy-done.3
  94.2 0.1 select_reduce_fusion
  94.3 0.0 copy-done.4
  94.3 0.1 iota_compare_fusion.3
  94.4 0.0 copy-done.1
  94.4 6.0 %fusion.22 = f32[4,64,2048]{2,1,0:T(8,128)S(1)} fusion(bf16[4,64,512]{2,1,0:T(8,128)(2,1)S(1)} %copy-done.1, bf16[4,2048,512]{2,1,0:T(8,128)(2,1)} %param.19), kind=kOutput, calls=%fused_computation.40 | convolution fusion | flops 536870912 | bytes 10747904 | tf_op jit(solution)/shard_map/vmap()/dot_general | solution.py:155
  100.4 0.0 copy-done
  100.4 3.2 %fusion.21 = (f32[4,64]{1,0:T(4,128)S(1)}, f32[4,64,2048]{2,1,0:T(8,128)}) fusion(pred[4,2048]{1,0:T(4,128)(4,1)S(1)} %iota_compare_fusion.3, f32[4,64,2048]{2,1,0:T(8,128)S(1)} %fusion.22, bf16[4,64,64]{2,1,0:T(8,128)(2,1)} %reshape.47, bf16[4,64,2048]{2,1,0:T(8,128)(2,1)S(1)} %copy-done), kind=kOutput, calls=%fused_computation.39 | convolution fusion | flops 70256640 | bytes 5284864 | tf_op jit(solution)/shard_map/vmap()/sub | solution.py:166
  103.6 6.3 %convolution_convert_fusion.1 = bf16[4,64,512]{2,1,0:T(8,128)(2,1)} fusion(bf16[4,2048,512]{2,1,0:T(8,128)(2,1)} %param.19, f32[4,64,2048]{2,1,0:T(8,128)} %get-tuple-element.6, f32[4,64]{1,0:T(4,128)S(1)} %get-tuple-element.5), kind=kOutput, calls=%fused_computation.12 | convolution fusion | flops 538050560 | bytes 10748928 | tf_op jit(solution)/shard_map/vmap()/dot_general | solution.py:168
  110.0 30.3 %all-to-all-done.1 = bf16[64,8,3584]{2,1,0:T(8,128)(2,1)} async-done(((bf16[64,8,3584]{2,1,0:T(8,128)(2,1)}), bf16[64,8,3584]{2,1,0:T(8,128)(2,1)}, u32[]{:S(2)}, u32[]{:S(2)}) %all-to-all-start.1) | async-done | bytes 3670048 | tf_op jit(solution)/shard_map/all_to_all | solution.py:208
  140.2 2.8 %fusion.2 = f32[96,3584]{1,0:T(8,128)S(1)} fusion(bf16[64,8,3584]{2,1,0:T(8,128)(2,1)} %all-to-all-done.1, bf16[32,512]{1,0:T(8,128)(2,1)S(1)} %get-tuple-element.3, bf16[32,512]{1,0:T(8,128)(2,1)S(1)} %get-tuple-element.4, bf16[32,512]{1,0:T(8,128)(2,1)S(1)} %get-tuple-element.2), kind=kOutput, calls=%fused_computation.3 | convolution fusion | flops 352616448 | bytes 5144576 | tf_op jit(solution)/shard_map/dot_general | solution.py:216
  143.0 0.8 fusion.11
  (1 shorter events, 0.0 us)
Async XLA Ops:
  0.6 99.8 %copy-start = (bf16[4,64,2048]{2,1,0:T(8,128)(2,1)S(1)}, bf16[4,64,2048]{2,1,0:T(8,128)(2,1)}, u32[]{:S(2)}) copy-start(bf16[4,64,2048]{2,1,0:T(8,128)(2,1)} %param.20) | copy-start | bytes 3145732
  0.6 64.3 %collective-permute-start = (bf16[3584,512]{1,0:T(8,128)(2,1)}, bf16[3584,512]{1,0:T(8,128)(2,1)S(1)}, u32[]{:S(2)}, u32[]{:S(2)}) collective-permute-start(bf16[3584,512]{1,0:T(8,128)(2,1)} %bitcast.26), channel_id=1, source_target_pairs={{0,64},{64,0},{1,65},{65,1},{2,66},{66,2},{3,67},{67,3},{4,68},{68... | collective-permute-start | bytes 11010056 | tf_op jit(solution)/shard_map/ppermute | solution.py:72
  0.7 64.2 %collective-permute-start.1 = (bf16[3584,512]{1,0:T(8,128)(2,1)}, bf16[3584,512]{1,0:T(8,128)(2,1)}, u32[]{:S(2)}, u32[]{:S(2)}) collective-permute-start(bf16[3584,512]{1,0:T(8,128)(2,1)} %bitcast.28), channel_id=1, source_target_pairs={{0,64},{64,0},{1,65},{65,1},{2,66},{66,2},{3,67},{67,3},{4,68},{68... | collective-permute-start | bytes 11010056 | tf_op jit(solution)/shard_map/ppermute | solution.py:72
  1.2 63.7 %collective-permute-start.2 = (bf16[3584,512]{1,0:T(8,128)(2,1)}, bf16[3584,512]{1,0:T(8,128)(2,1)}, u32[]{:S(2)}, u32[]{:S(2)}) collective-permute-start(bf16[3584,512]{1,0:T(8,128)(2,1)} %bitcast.30), channel_id=1, source_target_pairs={{0,64},{64,0},{1,65},{65,1},{2,66},{66,2},{3,67},{67,3},{4,68},{68... | collective-permute-start | bytes 11010056 | tf_op jit(solution)/shard_map/ppermute | solution.py:72
  65.0 1.9 %copy-start.5 = (bf16[3584,512]{1,0:T(8,128)(2,1)}, bf16[3584,512]{1,0:T(8,128)(2,1)S(1)}, u32[]{:S(2)}) copy-start(bf16[3584,512]{1,0:T(8,128)(2,1)S(1)} %collective-permute-done.gt_ref) | copy-start | bytes 11010052
  87.4 6.0 %copy-start.2 = (bf16[4,4096]{1,0:T(4,128)(2,1)S(1)}, bf16[4,4096]{1,0:T(4,128)(2,1)}, u32[]{:S(2)}) copy-start(bf16[4,4096]{1,0:T(4,128)(2,1)} %param.18) | copy-start | bytes 98308
  87.4 6.7 %copy-start.3 = (f32[32,8]{0,1:T(8,128)S(1)}, f32[32,8]{0,1:T(8,128)}, u32[]{:S(2)}) copy-start(f32[32,8]{0,1:T(8,128)} %param.13) | copy-start | bytes 3076
  87.4 6.9 %copy-start.4 = (s32[4]{0:T(128)S(1)}, s32[4]{0:T(128)}, u32[]{:S(2)}) copy-start(s32[4]{0:T(128)} %param.21) | copy-start | bytes 52
  87.4 7.0 %copy-start.1 = (bf16[4,64,512]{2,1,0:T(8,128)(2,1)S(1)}, bf16[4,64,512]{2,1,0:T(8,128)(2,1)}, u32[]{:S(2)}) copy-start(bf16[4,64,512]{2,1,0:T(8,128)(2,1)} %param.17) | copy-start | bytes 786436
  87.5 52.8 %all-to-all-start.1 = ((bf16[64,8,3584]{2,1,0:T(8,128)(2,1)}), bf16[64,8,3584]{2,1,0:T(8,128)(2,1)}, u32[]{:S(2)}, u32[]{:S(2)}) async-start(bf16[64,8,3584]{2,1,0:T(8,128)(2,1)} %bitcast.21), calls=%async_computation.1 | async-start | bytes 7340032 | tf_op jit(solution)/shard_map/all_to_all | solution.py:208

commit v17 on v15

--- a/solution.py
+++ b/solution.py
@@ -137,7 +137,7 @@
         ],
         out_specs=pl.BlockSpec((count, out_tile), lambda i: (0, jnp.clip(i - 2 * steps, 0, outs - 1))),
         scratch_shapes=[pltpu.VMEM((count, 2 * units), jnp.bfloat16)],
-        compiler_params=pltpu.CompilerParams(vmem_limit_bytes=56 * 1024 * 1024),
+        compiler_params=pltpu.CompilerParams(vmem_limit_bytes=40 * 1024 * 1024),
         cost_estimate=pl.CostEstimate(
             flops=12 * count * width * units,
             transcendentals=2 * count * units,

time: 141 us -> 140 us (level)
  Pallas kernels: 20.6 us -> 17 us
  local copies, waits for them, and re-layouts: 1.62 us -> 3.45 us
    pallas_call x1, Pallas kernels: 20.6 us -> 17 us  [full_expert(): pl.pallas_call(functools.partial(ffn_kernel, steps), out_shape=jax.ShapeD...]
    unnamed x12 -> x16, local copies, waits for them, and re-layouts: 0.87 us -> 2.7 us
  transfers between devices with their start and end apart: 4 -> 4, of which waited for: 1 -> 1; matrix products, arithmetic and copies ran while one was open for 14% -> 15% of each run, Pallas kernels for 0% -> 0%
where the time goes in v17:
time: 140 us; the launch traced here: 139 us
  blocking collectives  59 us (42%)
  waiting for transfers between devices  30.1 us (22%)
  matrix products  20.5 us (15%)
  Pallas kernels  17 us (12%)
  starting transfers between devices  6.61 us (5%)
  local copies, waits for them, and re-layouts  3.45 us (2%)
  other arithmetic  1.62 us (1%)
    all_to_all x1, blocking collectives, per_device(): lax.all_to_all(outgoing, 'dev', split_axis=0, concat_axis=0, tiled=True)  59 us
    all_to_all x1, waiting for transfers between devices, per_device(): lax.all_to_all(finished, 'dev', split_axis=0, concat_axis=0, tiled=True)  30.1 us
    pallas_call x1, Pallas kernels, full_expert(): pl.pallas_call(functools.partial(ffn_kernel, steps), out_shape=jax.ShapeD...  17 us
    dot_general x1, matrix products, attend_row(): jnp.dot(probs, cache_lat, preferred_element_type=jnp.float32)  6.34 us
    dot_general x1, matrix products, attend_row(): lax.dot_general(query_lat, cache_lat, (((1,), (1,)), ((), ())), preferred...  6 us
    all_to_all x1, starting transfers between devices, per_device(): lax.all_to_all(finished, 'dev', split_axis=0, concat_axis=0, tiled=True)  5.93 us
    sub x1, matrix products, attend_row(): weights = jnp.where(valid, jnp.exp(scores - highest), jnp.float32(0.0))  3.2 us
  transfers between devices with their start and end apart: 4, of which 1 were waited for; matrix products, arithmetic and copies ran while one was open for 15% of the time, Pallas kernels for 0%

profile of v17, /device:TPU:0, one launch (start us, length us, event | category | flops | bytes accessed | tf_op | source)
XLA Modules:
  0.0 139.1 jit_solution(7391326819031884053)
XLA Ops:
  0.6 0.0 copy-start
  0.6 0.1 collective-permute-start
  0.7 0.5 collective-permute-start.1
  1.2 0.1 collective-permute-start.2
  1.3 0.8 copy.17
  2.1 0.1 fusion.12
  2.2 0.1 fusion.19
  2.3 0.2 select_reduce_fusion.1
  2.5 0.2 fusion.10
  2.8 2.1 %fusion.1 = bf16[64,8,3584]{2,1,0:T(8,128)(2,1)S(1)} fusion(pred[512,32]{0,1:T(8,128)(4,1)S(1)} %fusion.10, bf16[32,3584]{1,0:T(8,128)(2,1)} %param.11), kind=kOutput, calls=%fused_computation.2 | convolution fusion | flops 119275520 | bytes 3915776 | tf_op jit(solution)/shard_map/dot_general | solution.py:202
  4.9 0.0 copy-start.2
  4.9 59.0 %all_to_all.10 = bf16[64,8,3584]{2,1,0:T(8,128)(2,1)S(1)} all-to-all(bf16[64,8,3584]{2,1,0:T(8,128)(2,1)S(1)} %fusion.1), channel_id=1, replica_groups=mesh['role'=2,'dev'=64] {'dev'}, dimensions={0} | all-to-all | bytes 7340032 | tf_op jit(solution)/shard_map/all_to_all | solution.py:205
  63.9 0.0 collective-permute-done.gt_ref
  63.9 0.0 collective-permute-done.1.ut_ref
  64.0 0.0 collective-permute-done.2.dt_ref
  64.0 0.0 copy-done.2
  64.0 17.0 %shard_map.122 = bf16[512,3584]{1,0:T(8,128)(2,1)S(1)} custom-call(bf16[512,3584]{1,0:T(8,128)(2,1)S(1)} %bitcast.19, bf16[3584,512]{1,0:T(8,128)(2,1)S(1)} %bitcast.21, bf16[3584,512]{1,0:T(8,128)(2,1)} %bitcast.23, bf16[3584,512]{1,0:T(8,128)(2,1)} %collective-permute-done.gt_ref, bf16[3584,512]{1,0:T(8,128)(2,1)} %collective-permute-done.1.ut_ref, ...), custom_call_target="tpu_custom_call" | custom-call | flops 11274289152 | bytes 29360128 | tf_op jit(solution)/shard_map/pallas_call | solution.py:125
  81.0 0.0 copy-start.1
  81.0 1.8 %copy-done.1 = bf16[512,3584]{1,0:T(8,128)(2,1)} copy-done((bf16[512,3584]{1,0:T(8,128)(2,1)}, bf16[512,3584]{1,0:T(8,128)(2,1)S(1)}, u32[]{:S(2)}) %copy-start.1) | copy-done | bytes 3670040
  82.8 0.0 copy-start.5
  82.8 0.0 copy-start.4
  82.8 0.0 copy-start.6
  82.8 0.0 copy-start.3
  82.8 5.9 %all-to-all-start.1 = ((bf16[64,8,3584]{2,1,0:T(8,128)(2,1)}), bf16[64,8,3584]{2,1,0:T(8,128)(2,1)}, u32[]{:S(2)}, u32[]{:S(2)}) async-start(bf16[64,8,3584]{2,1,0:T(8,128)(2,1)} %bitcast.18), calls=%async_computation.1 | async-start | bytes 7340032 | tf_op jit(solution)/shard_map/all_to_all | solution.py:209
  88.8 0.0 copy-done.5
  88.8 0.1 copy.19
  88.8 0.0 copy-done.4
  88.8 0.8 reshape.47
  89.6 0.2 select_reduce_fusion
  89.8 0.0 copy-done.6
  89.9 0.1 iota_compare_fusion.3
  89.9 0.0 copy-done.3
  90.0 6.0 %fusion.22 = f32[4,64,2048]{2,1,0:T(8,128)S(1)} fusion(bf16[4,64,512]{2,1,0:T(8,128)(2,1)S(1)} %copy-done.3, bf16[4,2048,512]{2,1,0:T(8,128)(2,1)} %param.19), kind=kOutput, calls=%fused_computation.40 | convolution fusion | flops 536870912 | bytes 10747904 | tf_op jit(solution)/shard_map/vmap()/dot_general | solution.py:155
  96.0 0.0 copy-done
  96.0 3.2 %fusion.21 = (f32[4,64]{1,0:T(4,128)S(1)}, f32[4,64,2048]{2,1,0:T(8,128)}) fusion(pred[4,2048]{1,0:T(4,128)(4,1)S(1)} %iota_compare_fusion.3, f32[4,64,2048]{2,1,0:T(8,128)S(1)} %fusion.22, bf16[4,64,64]{2,1,0:T(8,128)(2,1)} %reshape.47, bf16[4,64,2048]{2,1,0:T(8,128)(2,1)S(1)} %copy-done), kind=kOutput, calls=%fused_computation.39 | convolution fusion | flops 70256640 | bytes 5284864 | tf_op jit(solution)/shard_map/vmap()/sub | solution.py:166
  99.2 6.3 %convolution_convert_fusion.1 = bf16[4,64,512]{2,1,0:T(8,128)(2,1)} fusion(bf16[4,2048,512]{2,1,0:T(8,128)(2,1)} %param.19, f32[4,64,2048]{2,1,0:T(8,128)} %get-tuple-element.6, f32[4,64]{1,0:T(4,128)S(1)} %get-tuple-element.5), kind=kOutput, calls=%fused_computation.12 | convolution fusion | flops 538050560 | bytes 10748928 | tf_op jit(solution)/shard_map/vmap()/dot_general | solution.py:168
  105.5 30.1 %all-to-all-done.1 = bf16[64,8,3584]{2,1,0:T(8,128)(2,1)} async-done(((bf16[64,8,3584]{2,1,0:T(8,128)(2,1)}), bf16[64,8,3584]{2,1,0:T(8,128)(2,1)}, u32[]{:S(2)}, u32[]{:S(2)}) %all-to-all-start.1) | async-done | bytes 3670048 | tf_op jit(solution)/shard_map/all_to_all | solution.py:209
  135.6 2.8 %fusion.2 = f32[96,3584]{1,0:T(8,128)S(1)} fusion(bf16[64,8,3584]{2,1,0:T(8,128)(2,1)} %all-to-all-done.1, bf16[32,512]{1,0:T(8,128)(2,1)S(1)} %get-tuple-element.3, bf16[32,512]{1,0:T(8,128)(2,1)S(1)} %get-tuple-element.4, bf16[32,512]{1,0:T(8,128)(2,1)S(1)} %get-tuple-element.2), kind=kOutput, calls=%fused_computation.3 | convolution fusion | flops 352616448 | bytes 5144576 | tf_op jit(solution)/shard_map/dot_general | solution.py:217
  138.4 0.8 fusion.11
  (2 shorter events, 0.0 us)
Async XLA Ops:
  0.6 95.3 %copy-start = (bf16[4,64,2048]{2,1,0:T(8,128)(2,1)S(1)}, bf16[4,64,2048]{2,1,0:T(8,128)(2,1)}, u32[]{:S(2)}) copy-start(bf16[4,64,2048]{2,1,0:T(8,128)(2,1)} %param.20) | copy-start | bytes 3145732
  0.6 63.3 %collective-permute-start = (bf16[3584,512]{1,0:T(8,128)(2,1)}, bf16[3584,512]{1,0:T(8,128)(2,1)}, u32[]{:S(2)}, u32[]{:S(2)}) collective-permute-start(bf16[3584,512]{1,0:T(8,128)(2,1)} %bitcast.20), channel_id=1, source_target_pairs={{0,64},{64,0},{1,65},{65,1},{2,66},{66,2},{3,67},{67,3},{4,68},{68... | collective-permute-start | bytes 11010056 | tf_op jit(solution)/shard_map/ppermute | solution.py:72
  0.7 63.2 %collective-permute-start.1 = (bf16[3584,512]{1,0:T(8,128)(2,1)}, bf16[3584,512]{1,0:T(8,128)(2,1)}, u32[]{:S(2)}, u32[]{:S(2)}) collective-permute-start(bf16[3584,512]{1,0:T(8,128)(2,1)} %bitcast.22), channel_id=1, source_target_pairs={{0,64},{64,0},{1,65},{65,1},{2,66},{66,2},{3,67},{67,3},{4,68},{68... | collective-permute-start | bytes 11010056 | tf_op jit(solution)/shard_map/ppermute | solution.py:72
  1.2 62.7 %collective-permute-start.2 = (bf16[3584,512]{1,0:T(8,128)(2,1)}, bf16[3584,512]{1,0:T(8,128)(2,1)}, u32[]{:S(2)}, u32[]{:S(2)}) collective-permute-start(bf16[3584,512]{1,0:T(8,128)(2,1)} %bitcast.24), channel_id=1, source_target_pairs={{0,64},{64,0},{1,65},{65,1},{2,66},{66,2},{3,67},{67,3},{4,68},{68... | collective-permute-start | bytes 11010056 | tf_op jit(solution)/shard_map/ppermute | solution.py:72
  4.9 59.1 %copy-start.2 = (bf16[1,3584,512]{2,1,0:T(8,128)(2,1)S(1)}, bf16[1,3584,512]{2,1,0:T(8,128)(2,1)}, u32[]{:S(2)}) copy-start(bf16[1,3584,512]{2,1,0:T(8,128)(2,1)} %param.14) | copy-start | bytes 11010052
  81.0 1.8 %copy-start.1 = (bf16[512,3584]{1,0:T(8,128)(2,1)}, bf16[512,3584]{1,0:T(8,128)(2,1)S(1)}, u32[]{:S(2)}) copy-start(bf16[512,3584]{1,0:T(8,128)(2,1)S(1)} %shard_map.122) | copy-start | bytes 11010052
  82.8 6.0 %copy-start.5 = (f32[32,8]{0,1:T(8,128)S(1)}, f32[32,8]{0,1:T(8,128)}, u32[]{:S(2)}) copy-start(f32[32,8]{0,1:T(8,128)} %param.13) | copy-start | bytes 3076
  82.8 6.0 %copy-start.4 = (bf16[4,4096]{1,0:T(4,128)(2,1)S(1)}, bf16[4,4096]{1,0:T(4,128)(2,1)}, u32[]{:S(2)}) copy-start(bf16[4,4096]{1,0:T(4,128)(2,1)} %param.18) | copy-start | bytes 98308
  82.8 7.0 %copy-start.6 = (s32[4]{0:T(128)S(1)}, s32[4]{0:T(128)}, u32[]{:S(2)}) copy-start(s32[4]{0:T(128)} %param.21) | copy-start | bytes 52
  82.8 7.1 %copy-start.3 = (bf16[4,64,512]{2,1,0:T(8,128)(2,1)S(1)}, bf16[4,64,512]{2,1,0:T(8,128)(2,1)}, u32[]{:S(2)}) copy-start(bf16[4,64,512]{2,1,0:T(8,128)(2,1)} %param.17) | copy-start | bytes 786436
  82.8 52.8 %all-to-all-start.1 = ((bf16[64,8,3584]{2,1,0:T(8,128)(2,1)}), bf16[64,8,3584]{2,1,0:T(8,128)(2,1)}, u32[]{:S(2)}, u32[]{:S(2)}) async-start(bf16[64,8,3584]{2,1,0:T(8,128)(2,1)} %bitcast.18), calls=%async_computation.1 | async-start | bytes 7340032 | tf_op jit(solution)/shard_map/all_to_all | solution.py:209

commit v18 on v17

--- a/solution.py
+++ b/solution.py
@@ -127,7 +127,7 @@
         out_shape=jax.ShapeDtypeStruct((count, width), jnp.bfloat16),
         grid=(2 * steps + outs,),
         in_specs=[
-            pl.BlockSpec((count, width), lambda i: (0, 0)),
+            pl.BlockSpec((count, width), lambda i: (0, 0), pipeline_mode=pl.Buffered(1)),
             pl.BlockSpec(unit_block, own_map),
             pl.BlockSpec(unit_block, own_map),
             pl.BlockSpec(unit_block, other_map),
@@ -137,7 +137,7 @@
         ],
         out_specs=pl.BlockSpec((count, out_tile), lambda i: (0, jnp.clip(i - 2 * steps, 0, outs - 1))),
         scratch_shapes=[pltpu.VMEM((count, 2 * units), jnp.bfloat16)],
-        compiler_params=pltpu.CompilerParams(vmem_limit_bytes=40 * 1024 * 1024),
+        compiler_params=pltpu.CompilerParams(vmem_limit_bytes=36 * 1024 * 1024),
         cost_estimate=pl.CostEstimate(
             flops=12 * count * width * units,
             transcendentals=2 * count * units,

time: 140 us -> 139 us (level)
  no operation moved by 1% of the time
where the time goes in v18:
time: 139 us
  blocking collectives  59 us (42%)
  waiting for transfers between devices  30.1 us (22%)
  matrix products  20.5 us (15%)
  Pallas kernels  16.6 us (12%)
  starting transfers between devices  6.61 us (5%)
  local copies, waits for them, and re-layouts  3.46 us (2%)
  other arithmetic  1.62 us (1%)
    all_to_all x1, blocking collectives, per_device(): lax.all_to_all(outgoing, 'dev', split_axis=0, concat_axis=0, tiled=True)  59 us
    all_to_all x1, waiting for transfers between devices, per_device(): lax.all_to_all(finished, 'dev', split_axis=0, concat_axis=0, tiled=True)  30.1 us
    pallas_call x1, Pallas kernels, full_expert(): pl.pallas_call(functools.partial(ffn_kernel, steps), out_shape=jax.ShapeD...  16.6 us
    dot_general x1, matrix products, attend_row(): jnp.dot(probs, cache_lat, preferred_element_type=jnp.float32)  6.34 us
    dot_general x1, matrix products, attend_row(): lax.dot_general(query_lat, cache_lat, (((1,), (1,)), ((), ())), preferred...  6 us
    all_to_all x1, starting transfers between devices, per_device(): lax.all_to_all(finished, 'dev', split_axis=0, concat_axis=0, tiled=True)  5.93 us
    sub x1, matrix products, attend_row(): weights = jnp.where(valid, jnp.exp(scores - highest), jnp.float32(0.0))  3.2 us
  transfers between devices with their start and end apart: 4, of which 1 were waited for; matrix products, arithmetic and copies ran while one was open for 15% of the time, Pallas kernels for 0%

profile of v18, /device:TPU:0, one launch (start us, length us, event | category | flops | bytes accessed | tf_op | source)
XLA Modules:
  0.0 138.7 jit_solution(16882948725303737122)
XLA Ops:
  0.6 0.0 copy-start
  0.6 0.1 collective-permute-start
  0.7 0.5 collective-permute-start.1
  1.2 0.1 collective-permute-start.2
  1.3 0.8 copy.17
  2.1 0.1 fusion.12
  2.2 0.1 fusion.19
  2.3 0.2 select_reduce_fusion.1
  2.5 0.2 fusion.10
  2.8 2.1 %fusion.1 = bf16[64,8,3584]{2,1,0:T(8,128)(2,1)S(1)} fusion(pred[512,32]{0,1:T(8,128)(4,1)S(1)} %fusion.10, bf16[32,3584]{1,0:T(8,128)(2,1)} %param.11), kind=kOutput, calls=%fused_computation.2 | convolution fusion | flops 119275520 | bytes 3915776 | tf_op jit(solution)/shard_map/dot_general | solution.py:202
  4.9 0.0 copy-start.2
  4.9 0.0 copy-start.3
  4.9 59.0 %all_to_all.10 = bf16[64,8,3584]{2,1,0:T(8,128)(2,1)S(1)} all-to-all(bf16[64,8,3584]{2,1,0:T(8,128)(2,1)S(1)} %fusion.1), channel_id=1, replica_groups=mesh['role'=2,'dev'=64] {'dev'}, dimensions={0} | all-to-all | bytes 7340032 | tf_op jit(solution)/shard_map/all_to_all | solution.py:205
  64.0 0.0 collective-permute-done.gt_ref
  64.0 0.0 collective-permute-done.1.ut_ref
  64.0 0.0 collective-permute-done.2.dt_ref
  64.0 0.0 copy-done.2
  64.0 0.0 copy-done.3
  64.0 16.6 %shard_map.122 = bf16[512,3584]{1,0:T(8,128)(2,1)S(1)} custom-call(bf16[512,3584]{1,0:T(8,128)(2,1)S(1)} %bitcast.19, bf16[3584,512]{1,0:T(8,128)(2,1)S(1)} %bitcast.21, bf16[3584,512]{1,0:T(8,128)(2,1)S(1)} %bitcast.23, bf16[3584,512]{1,0:T(8,128)(2,1)} %collective-permute-done.gt_ref, bf16[3584,512]{1,0:T(8,128)(2,1)} %collective-permute-done.1.ut_ref, ...), custom_call_target="tpu_custom_call" | custom-call | flops 11274289152 | bytes 29360128 | tf_op jit(solution)/shard_map/pallas_call | solution.py:125
  80.6 0.0 copy-start.1
  80.6 1.8 %copy-done.1 = bf16[512,3584]{1,0:T(8,128)(2,1)} copy-done((bf16[512,3584]{1,0:T(8,128)(2,1)}, bf16[512,3584]{1,0:T(8,128)(2,1)S(1)}, u32[]{:S(2)}) %copy-start.1) | copy-done | bytes 3670040
  82.4 0.0 copy-start.6
  82.4 0.0 copy-start.5
  82.4 0.0 copy-start.7
  82.4 0.0 copy-start.4
  82.4 5.9 %all-to-all-start.1 = ((bf16[64,8,3584]{2,1,0:T(8,128)(2,1)}), bf16[64,8,3584]{2,1,0:T(8,128)(2,1)}, u32[]{:S(2)}, u32[]{:S(2)}) async-start(bf16[64,8,3584]{2,1,0:T(8,128)(2,1)} %bitcast.18), calls=%async_computation.1 | async-start | bytes 7340032 | tf_op jit(solution)/shard_map/all_to_all | solution.py:209
  88.3 0.0 copy-done.6
  88.4 0.1 copy.19
  88.4 0.0 copy-done.5
  88.4 0.8 reshape.47
  89.2 0.2 select_reduce_fusion
  89.4 0.0 copy-done.7
  89.5 0.1 iota_compare_fusion.3
  89.5 0.0 copy-done.4
  89.5 6.0 %fusion.22 = f32[4,64,2048]{2,1,0:T(8,128)S(1)} fusion(bf16[4,64,512]{2,1,0:T(8,128)(2,1)S(1)} %copy-done.4, bf16[4,2048,512]{2,1,0:T(8,128)(2,1)} %param.19), kind=kOutput, calls=%fused_computation.40 | convolution fusion | flops 536870912 | bytes 10747904 | tf_op jit(solution)/shard_map/vmap()/dot_general | solution.py:155
  95.6 0.0 copy-done
  95.6 3.2 %fusion.21 = (f32[4,64]{1,0:T(4,128)S(1)}, f32[4,64,2048]{2,1,0:T(8,128)}) fusion(pred[4,2048]{1,0:T(4,128)(4,1)S(1)} %iota_compare_fusion.3, f32[4,64,2048]{2,1,0:T(8,128)S(1)} %fusion.22, bf16[4,64,64]{2,1,0:T(8,128)(2,1)} %reshape.47, bf16[4,64,2048]{2,1,0:T(8,128)(2,1)S(1)} %copy-done), kind=kOutput, calls=%fused_computation.39 | convolution fusion | flops 70256640 | bytes 5284864 | tf_op jit(solution)/shard_map/vmap()/sub | solution.py:166
  98.8 6.3 %convolution_convert_fusion.1 = bf16[4,64,512]{2,1,0:T(8,128)(2,1)} fusion(bf16[4,2048,512]{2,1,0:T(8,128)(2,1)} %param.19, f32[4,64,2048]{2,1,0:T(8,128)} %get-tuple-element.6, f32[4,64]{1,0:T(4,128)S(1)} %get-tuple-element.5), kind=kOutput, calls=%fused_computation.12 | convolution fusion | flops 538050560 | bytes 10748928 | tf_op jit(solution)/shard_map/vmap()/dot_general | solution.py:168
  105.1 30.1 %all-to-all-done.1 = bf16[64,8,3584]{2,1,0:T(8,128)(2,1)} async-done(((bf16[64,8,3584]{2,1,0:T(8,128)(2,1)}), bf16[64,8,3584]{2,1,0:T(8,128)(2,1)}, u32[]{:S(2)}, u32[]{:S(2)}) %all-to-all-start.1) | async-done | bytes 3670048 | tf_op jit(solution)/shard_map/all_to_all | solution.py:209
  135.2 2.8 %fusion.2 = f32[96,3584]{1,0:T(8,128)S(1)} fusion(bf16[64,8,3584]{2,1,0:T(8,128)(2,1)} %all-to-all-done.1, bf16[32,512]{1,0:T(8,128)(2,1)S(1)} %get-tuple-element.3, bf16[32,512]{1,0:T(8,128)(2,1)S(1)} %get-tuple-element.4, bf16[32,512]{1,0:T(8,128)(2,1)S(1)} %get-tuple-element.2), kind=kOutput, calls=%fused_computation.3 | convolution fusion | flops 352616448 | bytes 5144576 | tf_op jit(solution)/shard_map/dot_general | solution.py:217
  138.0 0.8 fusion.11
  (2 shorter events, 0.0 us)
Async XLA Ops:
  0.6 94.9 %copy-start = (bf16[4,64,2048]{2,1,0:T(8,128)(2,1)S(1)}, bf16[4,64,2048]{2,1,0:T(8,128)(2,1)}, u32[]{:S(2)}) copy-start(bf16[4,64,2048]{2,1,0:T(8,128)(2,1)} %param.20) | copy-start | bytes 3145732
  0.6 63.3 %collective-permute-start = (bf16[3584,512]{1,0:T(8,128)(2,1)}, bf16[3584,512]{1,0:T(8,128)(2,1)}, u32[]{:S(2)}, u32[]{:S(2)}) collective-permute-start(bf16[3584,512]{1,0:T(8,128)(2,1)} %bitcast.20), channel_id=1, source_target_pairs={{0,64},{64,0},{1,65},{65,1},{2,66},{66,2},{3,67},{67,3},{4,68},{68... | collective-permute-start | bytes 11010056 | tf_op jit(solution)/shard_map/ppermute | solution.py:72
  0.7 63.2 %collective-permute-start.1 = (bf16[3584,512]{1,0:T(8,128)(2,1)}, bf16[3584,512]{1,0:T(8,128)(2,1)}, u32[]{:S(2)}, u32[]{:S(2)}) collective-permute-start(bf16[3584,512]{1,0:T(8,128)(2,1)} %bitcast.22), channel_id=1, source_target_pairs={{0,64},{64,0},{1,65},{65,1},{2,66},{66,2},{3,67},{67,3},{4,68},{68... | collective-permute-start | bytes 11010056 | tf_op jit(solution)/shard_map/ppermute | solution.py:72
  1.2 62.7 %collective-permute-start.2 = (bf16[3584,512]{1,0:T(8,128)(2,1)}, bf16[3584,512]{1,0:T(8,128)(2,1)}, u32[]{:S(2)}, u32[]{:S(2)}) collective-permute-start(bf16[3584,512]{1,0:T(8,128)(2,1)} %bitcast.24), channel_id=1, source_target_pairs={{0,64},{64,0},{1,65},{65,1},{2,66},{66,2},{3,67},{67,3},{4,68},{68... | collective-permute-start | bytes 11010056 | tf_op jit(solution)/shard_map/ppermute | solution.py:72
  4.9 59.1 %copy-start.2 = (bf16[1,3584,512]{2,1,0:T(8,128)(2,1)S(1)}, bf16[1,3584,512]{2,1,0:T(8,128)(2,1)}, u32[]{:S(2)}) copy-start(bf16[1,3584,512]{2,1,0:T(8,128)(2,1)} %param.14) | copy-start | bytes 11010052
  4.9 59.1 %copy-start.3 = (bf16[1,3584,512]{2,1,0:T(8,128)(2,1)S(1)}, bf16[1,3584,512]{2,1,0:T(8,128)(2,1)}, u32[]{:S(2)}) copy-start(bf16[1,3584,512]{2,1,0:T(8,128)(2,1)} %param.15) | copy-start | bytes 11010052
  80.6 1.8 %copy-start.1 = (bf16[512,3584]{1,0:T(8,128)(2,1)}, bf16[512,3584]{1,0:T(8,128)(2,1)S(1)}, u32[]{:S(2)}) copy-start(bf16[512,3584]{1,0:T(8,128)(2,1)S(1)} %shard_map.122) | copy-start | bytes 11010052
  82.4 6.0 %copy-start.6 = (f32[32,8]{0,1:T(8,128)S(1)}, f32[32,8]{0,1:T(8,128)}, u32[]{:S(2)}) copy-start(f32[32,8]{0,1:T(8,128)} %param.13) | copy-start | bytes 3076
  82.4 6.0 %copy-start.5 = (bf16[4,4096]{1,0:T(4,128)(2,1)S(1)}, bf16[4,4096]{1,0:T(4,128)(2,1)}, u32[]{:S(2)}) copy-start(bf16[4,4096]{1,0:T(4,128)(2,1)} %param.18) | copy-start | bytes 98308
  82.4 7.0 %copy-start.7 = (s32[4]{0:T(128)S(1)}, s32[4]{0:T(128)}, u32[]{:S(2)}) copy-start(s32[4]{0:T(128)} %param.21) | copy-start | bytes 52
  82.4 7.1 %copy-start.4 = (bf16[4,64,512]{2,1,0:T(8,128)(2,1)S(1)}, bf16[4,64,512]{2,1,0:T(8,128)(2,1)}, u32[]{:S(2)}) copy-start(bf16[4,64,512]{2,1,0:T(8,128)(2,1)} %param.17) | copy-start | bytes 786436
  82.4 52.8 %all-to-all-start.1 = ((bf16[64,8,3584]{2,1,0:T(8,128)(2,1)}), bf16[64,8,3584]{2,1,0:T(8,128)(2,1)}, u32[]{:S(2)}, u32[]{:S(2)}) async-start(bf16[64,8,3584]{2,1,0:T(8,128)(2,1)} %bitcast.18), calls=%async_computation.1 | async-start | bytes 7340032 | tf_op jit(solution)/shard_map/all_to_all | solution.py:209

commit v19 on v18

--- a/solution.py
+++ b/solution.py
@@ -104,7 +104,7 @@
         o_ref[...] = total.astype(o_ref.dtype)
 
 
-def full_expert(rows, w_gate, w_up, w_down, unit_tile=256, out_tile=1792):
+def full_expert(rows, w_gate, w_up, w_down, unit_tile=256, out_tile=512):
     count, width = rows.shape
     own = (w_gate[0], w_up[0], w_down[0])
     other = tuple(other_half(w) for w in own)

time: 139 us -> 141 us (1.014)
  Pallas kernels: 16.6 us -> 18.2 us
    pallas_call x1, Pallas kernels: 16.6 us -> 18.2 us  [full_expert(): pl.pallas_call(functools.partial(ffn_kernel, steps), out_shape=jax.ShapeD...]
  transfers between devices with their start and end apart: 4 -> 4, of which waited for: 1 -> 1; matrix products, arithmetic and copies ran while one was open for 15% -> 14% of each run, Pallas kernels for 0% -> 0%
where the time goes in v19:
time: 141 us; the launch traced here: 140 us
  blocking collectives  59 us (42%)
  waiting for transfers between devices  30.3 us (21%)
  matrix products  20.5 us (15%)
  Pallas kernels  18.2 us (13%)
  starting transfers between devices  6.43 us (5%)
  local copies, waits for them, and re-layouts  3.46 us (2%)
  other arithmetic  1.62 us (1%)
    all_to_all x1, blocking collectives, per_device(): lax.all_to_all(outgoing, 'dev', split_axis=0, concat_axis=0, tiled=True)  59 us
    all_to_all x1, waiting for transfers between devices, per_device(): lax.all_to_all(finished, 'dev', split_axis=0, concat_axis=0, tiled=True)  30.3 us
    pallas_call x1, Pallas kernels, full_expert(): pl.pallas_call(functools.partial(ffn_kernel, steps), out_shape=jax.ShapeD...  18.2 us
    dot_general x1, matrix products, attend_row(): jnp.dot(probs, cache_lat, preferred_element_type=jnp.float32)  6.34 us
    dot_general x1, matrix products, attend_row(): lax.dot_general(query_lat, cache_lat, (((1,), (1,)), ((), ())), preferred...  6 us
    all_to_all x1, starting transfers between devices, per_device(): lax.all_to_all(finished, 'dev', split_axis=0, concat_axis=0, tiled=True)  5.75 us
    sub x1, matrix products, attend_row(): weights = jnp.where(valid, jnp.exp(scores - highest), jnp.float32(0.0))  3.2 us
  transfers between devices with their start and end apart: 4, of which 1 were waited for; matrix products, arithmetic and copies ran while one was open for 14% of the time, Pallas kernels for 0%

profile of v19, /device:TPU:0, one launch (start us, length us, event | category | flops | bytes accessed | tf_op | source)
XLA Modules:
  0.0 140.4 jit_solution(7295786600687391335)
XLA Ops:
  0.6 0.0 copy-start
  0.6 0.1 collective-permute-start
  0.7 0.5 collective-permute-start.1
  1.2 0.1 collective-permute-start.2
  1.3 0.8 copy.17
  2.1 0.1 fusion.12
  2.2 0.1 fusion.19
  2.3 0.2 select_reduce_fusion.1
  2.5 0.2 fusion.10
  2.8 2.1 %fusion.1 = bf16[64,8,3584]{2,1,0:T(8,128)(2,1)S(1)} fusion(pred[512,32]{0,1:T(8,128)(4,1)S(1)} %fusion.10, bf16[32,3584]{1,0:T(8,128)(2,1)} %param.11), kind=kOutput, calls=%fused_computation.2 | convolution fusion | flops 119275520 | bytes 3915776 | tf_op jit(solution)/shard_map/dot_general | solution.py:202
  4.9 0.0 copy-start.2
  4.9 0.0 copy-start.3
  4.9 59.0 %all_to_all.10 = bf16[64,8,3584]{2,1,0:T(8,128)(2,1)S(1)} all-to-all(bf16[64,8,3584]{2,1,0:T(8,128)(2,1)S(1)} %fusion.1), channel_id=1, replica_groups=mesh['role'=2,'dev'=64] {'dev'}, dimensions={0} | all-to-all | bytes 7340032 | tf_op jit(solution)/shard_map/all_to_all | solution.py:205
  64.0 0.0 collective-permute-done.gt_ref
  64.0 0.0 collective-permute-done.1.ut_ref
  64.0 0.0 collective-permute-done.2.dt_ref
  64.0 0.0 copy-done.2
  64.0 0.0 copy-done.3
  64.0 18.2 %shard_map.122 = bf16[512,3584]{1,0:T(8,128)(2,1)S(1)} custom-call(bf16[512,3584]{1,0:T(8,128)(2,1)S(1)} %bitcast.19, bf16[3584,512]{1,0:T(8,128)(2,1)S(1)} %bitcast.21, bf16[3584,512]{1,0:T(8,128)(2,1)S(1)} %bitcast.23, bf16[3584,512]{1,0:T(8,128)(2,1)} %collective-permute-done.gt_ref, bf16[3584,512]{1,0:T(8,128)(2,1)} %collective-permute-done.1.ut_ref, ...), custom_call_target="tpu_custom_call" | custom-call | flops 11274289152 | bytes 29360128 | tf_op jit(solution)/shard_map/pallas_call | solution.py:125
  82.2 0.0 copy-start.1
  82.2 1.8 %copy-done.1 = bf16[512,3584]{1,0:T(8,128)(2,1)} copy-done((bf16[512,3584]{1,0:T(8,128)(2,1)}, bf16[512,3584]{1,0:T(8,128)(2,1)S(1)}, u32[]{:S(2)}) %copy-start.1) | copy-done | bytes 3670040
  84.1 0.0 copy-start.6
  84.1 0.0 copy-start.5
  84.1 0.0 copy-start.7
  84.1 0.0 copy-start.4
  84.1 5.8 %all-to-all-start.1 = ((bf16[64,8,3584]{2,1,0:T(8,128)(2,1)}), bf16[64,8,3584]{2,1,0:T(8,128)(2,1)}, u32[]{:S(2)}, u32[]{:S(2)}) async-start(bf16[64,8,3584]{2,1,0:T(8,128)(2,1)} %bitcast.18), calls=%async_computation.1 | async-start | bytes 7340032 | tf_op jit(solution)/shard_map/all_to_all | solution.py:209
  89.8 0.0 copy-done.6
  89.9 0.1 copy.19
  89.9 0.0 copy-done.5
  89.9 0.8 reshape.47
  90.7 0.2 select_reduce_fusion
  90.9 0.0 copy-done.7
  90.9 0.1 iota_compare_fusion.3
  91.0 0.0 copy-done.4
  91.0 6.0 %fusion.22 = f32[4,64,2048]{2,1,0:T(8,128)S(1)} fusion(bf16[4,64,512]{2,1,0:T(8,128)(2,1)S(1)} %copy-done.4, bf16[4,2048,512]{2,1,0:T(8,128)(2,1)} %param.19), kind=kOutput, calls=%fused_computation.40 | convolution fusion | flops 536870912 | bytes 10747904 | tf_op jit(solution)/shard_map/vmap()/dot_general | solution.py:155
  97.0 0.0 copy-done
  97.1 3.2 %fusion.21 = (f32[4,64]{1,0:T(4,128)S(1)}, f32[4,64,2048]{2,1,0:T(8,128)}) fusion(pred[4,2048]{1,0:T(4,128)(4,1)S(1)} %iota_compare_fusion.3, f32[4,64,2048]{2,1,0:T(8,128)S(1)} %fusion.22, bf16[4,64,64]{2,1,0:T(8,128)(2,1)} %reshape.47, bf16[4,64,2048]{2,1,0:T(8,128)(2,1)S(1)} %copy-done), kind=kOutput, calls=%fused_computation.39 | convolution fusion | flops 70256640 | bytes 5284864 | tf_op jit(solution)/shard_map/vmap()/sub | solution.py:166
  100.3 6.3 %convolution_convert_fusion.1 = bf16[4,64,512]{2,1,0:T(8,128)(2,1)} fusion(bf16[4,2048,512]{2,1,0:T(8,128)(2,1)} %param.19, f32[4,64,2048]{2,1,0:T(8,128)} %get-tuple-element.6, f32[4,64]{1,0:T(4,128)S(1)} %get-tuple-element.5), kind=kOutput, calls=%fused_computation.12 | convolution fusion | flops 538050560 | bytes 10748928 | tf_op jit(solution)/shard_map/vmap()/dot_general | solution.py:168
  106.6 30.3 %all-to-all-done.1 = bf16[64,8,3584]{2,1,0:T(8,128)(2,1)} async-done(((bf16[64,8,3584]{2,1,0:T(8,128)(2,1)}), bf16[64,8,3584]{2,1,0:T(8,128)(2,1)}, u32[]{:S(2)}, u32[]{:S(2)}) %all-to-all-start.1) | async-done | bytes 3670048 | tf_op jit(solution)/shard_map/all_to_all | solution.py:209
  136.9 2.8 %fusion.2 = f32[96,3584]{1,0:T(8,128)S(1)} fusion(bf16[64,8,3584]{2,1,0:T(8,128)(2,1)} %all-to-all-done.1, bf16[32,512]{1,0:T(8,128)(2,1)S(1)} %get-tuple-element.3, bf16[32,512]{1,0:T(8,128)(2,1)S(1)} %get-tuple-element.4, bf16[32,512]{1,0:T(8,128)(2,1)S(1)} %get-tuple-element.2), kind=kOutput, calls=%fused_computation.3 | convolution fusion | flops 352616448 | bytes 5144576 | tf_op jit(solution)/shard_map/dot_general | solution.py:217
  139.6 0.8 fusion.11
  (2 shorter events, 0.0 us)
Async XLA Ops:
  0.6 96.4 %copy-start = (bf16[4,64,2048]{2,1,0:T(8,128)(2,1)S(1)}, bf16[4,64,2048]{2,1,0:T(8,128)(2,1)}, u32[]{:S(2)}) copy-start(bf16[4,64,2048]{2,1,0:T(8,128)(2,1)} %param.20) | copy-start | bytes 3145732
  0.6 63.3 %collective-permute-start = (bf16[3584,512]{1,0:T(8,128)(2,1)}, bf16[3584,512]{1,0:T(8,128)(2,1)}, u32[]{:S(2)}, u32[]{:S(2)}) collective-permute-start(bf16[3584,512]{1,0:T(8,128)(2,1)} %bitcast.20), channel_id=1, source_target_pairs={{0,64},{64,0},{1,65},{65,1},{2,66},{66,2},{3,67},{67,3},{4,68},{68... | collective-permute-start | bytes 11010056 | tf_op jit(solution)/shard_map/ppermute | solution.py:72
  0.7 63.2 %collective-permute-start.1 = (bf16[3584,512]{1,0:T(8,128)(2,1)}, bf16[3584,512]{1,0:T(8,128)(2,1)}, u32[]{:S(2)}, u32[]{:S(2)}) collective-permute-start(bf16[3584,512]{1,0:T(8,128)(2,1)} %bitcast.22), channel_id=1, source_target_pairs={{0,64},{64,0},{1,65},{65,1},{2,66},{66,2},{3,67},{67,3},{4,68},{68... | collective-permute-start | bytes 11010056 | tf_op jit(solution)/shard_map/ppermute | solution.py:72
  1.2 62.7 %collective-permute-start.2 = (bf16[3584,512]{1,0:T(8,128)(2,1)}, bf16[3584,512]{1,0:T(8,128)(2,1)}, u32[]{:S(2)}, u32[]{:S(2)}) collective-permute-start(bf16[3584,512]{1,0:T(8,128)(2,1)} %bitcast.24), channel_id=1, source_target_pairs={{0,64},{64,0},{1,65},{65,1},{2,66},{66,2},{3,67},{67,3},{4,68},{68... | collective-permute-start | bytes 11010056 | tf_op jit(solution)/shard_map/ppermute | solution.py:72
  4.9 59.1 %copy-start.2 = (bf16[1,3584,512]{2,1,0:T(8,128)(2,1)S(1)}, bf16[1,3584,512]{2,1,0:T(8,128)(2,1)}, u32[]{:S(2)}) copy-start(bf16[1,3584,512]{2,1,0:T(8,128)(2,1)} %param.14) | copy-start | bytes 11010052
  4.9 59.1 %copy-start.3 = (bf16[1,3584,512]{2,1,0:T(8,128)(2,1)S(1)}, bf16[1,3584,512]{2,1,0:T(8,128)(2,1)}, u32[]{:S(2)}) copy-start(bf16[1,3584,512]{2,1,0:T(8,128)(2,1)} %param.15) | copy-start | bytes 11010052
  82.2 1.8 %copy-start.1 = (bf16[512,3584]{1,0:T(8,128)(2,1)}, bf16[512,3584]{1,0:T(8,128)(2,1)S(1)}, u32[]{:S(2)}) copy-start(bf16[512,3584]{1,0:T(8,128)(2,1)S(1)} %shard_map.122) | copy-start | bytes 11010052
  84.1 5.8 %copy-start.6 = (f32[32,8]{0,1:T(8,128)S(1)}, f32[32,8]{0,1:T(8,128)}, u32[]{:S(2)}) copy-start(f32[32,8]{0,1:T(8,128)} %param.13) | copy-start | bytes 3076
  84.1 5.9 %copy-start.5 = (bf16[4,4096]{1,0:T(4,128)(2,1)S(1)}, bf16[4,4096]{1,0:T(4,128)(2,1)}, u32[]{:S(2)}) copy-start(bf16[4,4096]{1,0:T(4,128)(2,1)} %param.18) | copy-start | bytes 98308
  84.1 6.9 %copy-start.7 = (s32[4]{0:T(128)S(1)}, s32[4]{0:T(128)}, u32[]{:S(2)}) copy-start(s32[4]{0:T(128)} %param.21) | copy-start | bytes 52
  84.1 7.0 %copy-start.4 = (bf16[4,64,512]{2,1,0:T(8,128)(2,1)S(1)}, bf16[4,64,512]{2,1,0:T(8,128)(2,1)}, u32[]{:S(2)}) copy-start(bf16[4,64,512]{2,1,0:T(8,128)(2,1)} %param.17) | copy-start | bytes 786436
  84.1 52.8 %all-to-all-start.1 = ((bf16[64,8,3584]{2,1,0:T(8,128)(2,1)}), bf16[64,8,3584]{2,1,0:T(8,128)(2,1)}, u32[]{:S(2)}, u32[]{:S(2)}) async-start(bf16[64,8,3584]{2,1,0:T(8,128)(2,1)} %bitcast.18), calls=%async_computation.1 | async-start | bytes 7340032 | tf_op jit(solution)/shard_map/all_to_all | solution.py:209

commit v20 on v18

--- a/solution.py
+++ b/solution.py
@@ -137,7 +137,7 @@
         ],
         out_specs=pl.BlockSpec((count, out_tile), lambda i: (0, jnp.clip(i - 2 * steps, 0, outs - 1))),
         scratch_shapes=[pltpu.VMEM((count, 2 * units), jnp.bfloat16)],
-        compiler_params=pltpu.CompilerParams(vmem_limit_bytes=36 * 1024 * 1024),
+        compiler_params=pltpu.CompilerParams(vmem_limit_bytes=28 * 1024 * 1024),
         cost_estimate=pl.CostEstimate(
             flops=12 * count * width * units,
             transcendentals=2 * count * units,

time: 139 us -> 139 us (level)
  no operation moved by 1% of the time
where the time goes in v20:
time: 139 us; the launch traced here: 138 us
  blocking collectives  59.1 us (43%)
  waiting for transfers between devices  30.1 us (22%)
  matrix products  20.7 us (15%)
  Pallas kernels  16 us (12%)
  starting transfers between devices  6.61 us (5%)
  local copies, waits for them, and re-layouts  3.46 us (2%)
  other arithmetic  1.62 us (1%)
    all_to_all x1, blocking collectives, per_device(): lax.all_to_all(outgoing, 'dev', split_axis=0, concat_axis=0, tiled=True)  59.1 us
    all_to_all x1, waiting for transfers between devices, per_device(): lax.all_to_all(finished, 'dev', split_axis=0, concat_axis=0, tiled=True)  30.1 us
    pallas_call x1, Pallas kernels, full_expert(): pl.pallas_call(functools.partial(ffn_kernel, steps), out_shape=jax.ShapeD...  16 us
    dot_general x1, matrix products, attend_row(): jnp.dot(probs, cache_lat, preferred_element_type=jnp.float32)  6.34 us
    dot_general x1, matrix products, attend_row(): lax.dot_general(query_lat, cache_lat, (((1,), (1,)), ((), ())), preferred...  6 us
    all_to_all x1, starting transfers between devices, per_device(): lax.all_to_all(finished, 'dev', split_axis=0, concat_axis=0, tiled=True)  5.93 us
    sub x1, matrix products, attend_row(): weights = jnp.where(valid, jnp.exp(scores - highest), jnp.float32(0.0))  3.2 us
  transfers between devices with their start and end apart: 4, of which 1 were waited for; matrix products, arithmetic and copies ran while one was open for 15% of the time, Pallas kernels for 0%

profile of v20, /device:TPU:0, one launch (start us, length us, event | category | flops | bytes accessed | tf_op | source)
XLA Modules:
  0.0 138.4 jit_solution(17943546098282024208)
XLA Ops:
  0.6 0.0 copy-start
  0.6 0.1 collective-permute-start
  0.7 0.5 collective-permute-start.1
  1.2 0.1 collective-permute-start.2
  1.3 0.8 copy.17
  2.1 0.1 fusion.12
  2.2 0.1 fusion.19
  2.3 0.2 select_reduce_fusion.1
  2.5 0.2 fusion.10
  2.8 0.0 copy-start.4
  2.8 2.2 %fusion.1 = bf16[64,8,3584]{2,1,0:T(8,128)(2,1)S(1)} fusion(pred[512,32]{0,1:T(8,128)(4,1)S(1)} %fusion.10, bf16[32,3584]{1,0:T(8,128)(2,1)} %param.11), kind=kOutput, calls=%fused_computation.2 | convolution fusion | flops 119275520 | bytes 3915776 | tf_op jit(solution)/shard_map/dot_general | solution.py:202
  5.0 0.0 copy-start.2
  5.1 0.0 copy-start.3
  5.1 59.1 %all_to_all.10 = bf16[64,8,3584]{2,1,0:T(8,128)(2,1)S(1)} all-to-all(bf16[64,8,3584]{2,1,0:T(8,128)(2,1)S(1)} %fusion.1), channel_id=1, replica_groups=mesh['role'=2,'dev'=64] {'dev'}, dimensions={0} | all-to-all | bytes 7340032 | tf_op jit(solution)/shard_map/all_to_all | solution.py:205
  64.1 0.0 collective-permute-done.gt_ref
  64.1 0.0 collective-permute-done.1.ut_ref
  64.1 0.0 collective-permute-done.2.dt_ref
  64.1 0.0 copy-done.4
  64.1 0.0 copy-done.2
  64.2 0.0 copy-done.3
  64.2 16.0 %shard_map.122 = bf16[512,3584]{1,0:T(8,128)(2,1)S(1)} custom-call(bf16[512,3584]{1,0:T(8,128)(2,1)S(1)} %bitcast.19, bf16[3584,512]{1,0:T(8,128)(2,1)S(1)} %bitcast.21, bf16[3584,512]{1,0:T(8,128)(2,1)S(1)} %bitcast.23, bf16[3584,512]{1,0:T(8,128)(2,1)} %collective-permute-done.gt_ref, bf16[3584,512]{1,0:T(8,128)(2,1)} %collective-permute-done.1.ut_ref, ...), custom_call_target="tpu_custom_call" | custom-call | flops 11274289152 | bytes 29360128 | tf_op jit(solution)/shard_map/pallas_call | solution.py:125
  80.2 0.0 copy-start.1
  80.2 1.8 %copy-done.1 = bf16[512,3584]{1,0:T(8,128)(2,1)} copy-done((bf16[512,3584]{1,0:T(8,128)(2,1)}, bf16[512,3584]{1,0:T(8,128)(2,1)S(1)}, u32[]{:S(2)}) %copy-start.1) | copy-done | bytes 3670040
  82.0 0.0 copy-start.7
  82.0 0.0 copy-start.6
  82.0 0.0 copy-start.8
  82.0 0.0 copy-start.5
  82.0 5.9 %all-to-all-start.1 = ((bf16[64,8,3584]{2,1,0:T(8,128)(2,1)}), bf16[64,8,3584]{2,1,0:T(8,128)(2,1)}, u32[]{:S(2)}, u32[]{:S(2)}) async-start(bf16[64,8,3584]{2,1,0:T(8,128)(2,1)} %bitcast.18), calls=%async_computation.1 | async-start | bytes 7340032 | tf_op jit(solution)/shard_map/all_to_all | solution.py:209
  88.0 0.0 copy-done.7
  88.0 0.1 copy.19
  88.1 0.0 copy-done.6
  88.1 0.8 reshape.47
  88.8 0.2 select_reduce_fusion
  89.1 0.0 copy-done.8
  89.1 0.1 iota_compare_fusion.3
  89.2 0.0 copy-done.5
  89.2 6.0 %fusion.22 = f32[4,64,2048]{2,1,0:T(8,128)S(1)} fusion(bf16[4,64,512]{2,1,0:T(8,128)(2,1)S(1)} %copy-done.5, bf16[4,2048,512]{2,1,0:T(8,128)(2,1)} %param.19), kind=kOutput, calls=%fused_computation.40 | convolution fusion | flops 536870912 | bytes 10747904 | tf_op jit(solution)/shard_map/vmap()/dot_general | solution.py:155
  95.2 0.0 copy-done
  95.2 3.2 %fusion.21 = (f32[4,64]{1,0:T(4,128)S(1)}, f32[4,64,2048]{2,1,0:T(8,128)}) fusion(pred[4,2048]{1,0:T(4,128)(4,1)S(1)} %iota_compare_fusion.3, f32[4,64,2048]{2,1,0:T(8,128)S(1)} %fusion.22, bf16[4,64,64]{2,1,0:T(8,128)(2,1)} %reshape.47, bf16[4,64,2048]{2,1,0:T(8,128)(2,1)S(1)} %copy-done), kind=kOutput, calls=%fused_computation.39 | convolution fusion | flops 70256640 | bytes 5284864 | tf_op jit(solution)/shard_map/vmap()/sub | solution.py:166
  98.4 6.3 %convolution_convert_fusion.1 = bf16[4,64,512]{2,1,0:T(8,128)(2,1)} fusion(bf16[4,2048,512]{2,1,0:T(8,128)(2,1)} %param.19, f32[4,64,2048]{2,1,0:T(8,128)} %get-tuple-element.6, f32[4,64]{1,0:T(4,128)S(1)} %get-tuple-element.5), kind=kOutput, calls=%fused_computation.12 | convolution fusion | flops 538050560 | bytes 10748928 | tf_op jit(solution)/shard_map/vmap()/dot_general | solution.py:168
  104.7 30.1 %all-to-all-done.1 = bf16[64,8,3584]{2,1,0:T(8,128)(2,1)} async-done(((bf16[64,8,3584]{2,1,0:T(8,128)(2,1)}), bf16[64,8,3584]{2,1,0:T(8,128)(2,1)}, u32[]{:S(2)}, u32[]{:S(2)}) %all-to-all-start.1) | async-done | bytes 3670048 | tf_op jit(solution)/shard_map/all_to_all | solution.py:209
  134.9 2.8 %fusion.2 = f32[96,3584]{1,0:T(8,128)S(1)} fusion(bf16[64,8,3584]{2,1,0:T(8,128)(2,1)} %all-to-all-done.1, bf16[32,512]{1,0:T(8,128)(2,1)S(1)} %get-tuple-element.3, bf16[32,512]{1,0:T(8,128)(2,1)S(1)} %get-tuple-element.4, bf16[32,512]{1,0:T(8,128)(2,1)S(1)} %get-tuple-element.2), kind=kOutput, calls=%fused_computation.3 | convolution fusion | flops 352616448 | bytes 5144576 | tf_op jit(solution)/shard_map/dot_general | solution.py:217
  137.6 0.8 fusion.11
  (2 shorter events, 0.0 us)
Async XLA Ops:
  0.6 94.6 %copy-start = (bf16[4,64,2048]{2,1,0:T(8,128)(2,1)S(1)}, bf16[4,64,2048]{2,1,0:T(8,128)(2,1)}, u32[]{:S(2)}) copy-start(bf16[4,64,2048]{2,1,0:T(8,128)(2,1)} %param.20) | copy-start | bytes 3145732
  0.6 63.5 %collective-permute-start = (bf16[3584,512]{1,0:T(8,128)(2,1)}, bf16[3584,512]{1,0:T(8,128)(2,1)}, u32[]{:S(2)}, u32[]{:S(2)}) collective-permute-start(bf16[3584,512]{1,0:T(8,128)(2,1)} %bitcast.20), channel_id=1, source_target_pairs={{0,64},{64,0},{1,65},{65,1},{2,66},{66,2},{3,67},{67,3},{4,68},{68... | collective-permute-start | bytes 11010056 | tf_op jit(solution)/shard_map/ppermute | solution.py:72
  0.7 63.4 %collective-permute-start.1 = (bf16[3584,512]{1,0:T(8,128)(2,1)}, bf16[3584,512]{1,0:T(8,128)(2,1)}, u32[]{:S(2)}, u32[]{:S(2)}) collective-permute-start(bf16[3584,512]{1,0:T(8,128)(2,1)} %bitcast.22), channel_id=1, source_target_pairs={{0,64},{64,0},{1,65},{65,1},{2,66},{66,2},{3,67},{67,3},{4,68},{68... | collective-permute-start | bytes 11010056 | tf_op jit(solution)/shard_map/ppermute | solution.py:72
  1.2 62.9 %collective-permute-start.2 = (bf16[3584,512]{1,0:T(8,128)(2,1)}, bf16[3584,512]{1,0:T(8,128)(2,1)}, u32[]{:S(2)}, u32[]{:S(2)}) collective-permute-start(bf16[3584,512]{1,0:T(8,128)(2,1)} %bitcast.24), channel_id=1, source_target_pairs={{0,64},{64,0},{1,65},{65,1},{2,66},{66,2},{3,67},{67,3},{4,68},{68... | collective-permute-start | bytes 11010056 | tf_op jit(solution)/shard_map/ppermute | solution.py:72
  2.8 61.4 %copy-start.4 = (bf16[1,3584,512]{2,1,0:T(8,128)(2,1)S(1)}, bf16[1,3584,512]{2,1,0:T(8,128)(2,1)}, u32[]{:S(2)}) copy-start(bf16[1,3584,512]{2,1,0:T(8,128)(2,1)} %param.16) | copy-start | bytes 11010052
  5.0 59.1 %copy-start.2 = (bf16[1,3584,512]{2,1,0:T(8,128)(2,1)S(1)}, bf16[1,3584,512]{2,1,0:T(8,128)(2,1)}, u32[]{:S(2)}) copy-start(bf16[1,3584,512]{2,1,0:T(8,128)(2,1)} %param.14) | copy-start | bytes 11010052
  5.1 59.1 %copy-start.3 = (bf16[1,3584,512]{2,1,0:T(8,128)(2,1)S(1)}, bf16[1,3584,512]{2,1,0:T(8,128)(2,1)}, u32[]{:S(2)}) copy-start(bf16[1,3584,512]{2,1,0:T(8,128)(2,1)} %param.15) | copy-start | bytes 11010052
  80.2 1.8 %copy-start.1 = (bf16[512,3584]{1,0:T(8,128)(2,1)}, bf16[512,3584]{1,0:T(8,128)(2,1)S(1)}, u32[]{:S(2)}) copy-start(bf16[512,3584]{1,0:T(8,128)(2,1)S(1)} %shard_map.122) | copy-start | bytes 11010052
  82.0 6.0 %copy-start.7 = (f32[32,8]{0,1:T(8,128)S(1)}, f32[32,8]{0,1:T(8,128)}, u32[]{:S(2)}) copy-start(f32[32,8]{0,1:T(8,128)} %param.13) | copy-start | bytes 3076
  82.0 6.0 %copy-start.6 = (bf16[4,4096]{1,0:T(4,128)(2,1)S(1)}, bf16[4,4096]{1,0:T(4,128)(2,1)}, u32[]{:S(2)}) copy-start(bf16[4,4096]{1,0:T(4,128)(2,1)} %param.18) | copy-start | bytes 98308
  82.0 7.0 %copy-start.8 = (s32[4]{0:T(128)S(1)}, s32[4]{0:T(128)}, u32[]{:S(2)}) copy-start(s32[4]{0:T(128)} %param.21) | copy-start | bytes 52
  82.0 7.1 %copy-start.5 = (bf16[4,64,512]{2,1,0:T(8,128)(2,1)S(1)}, bf16[4,64,512]{2,1,0:T(8,128)(2,1)}, u32[]{:S(2)}) copy-start(bf16[4,64,512]{2,1,0:T(8,128)(2,1)} %param.17) | copy-start | bytes 786436
  82.0 52.8 %all-to-all-start.1 = ((bf16[64,8,3584]{2,1,0:T(8,128)(2,1)}), bf16[64,8,3584]{2,1,0:T(8,128)(2,1)}, u32[]{:S(2)}, u32[]{:S(2)}) async-start(bf16[64,8,3584]{2,1,0:T(8,128)(2,1)} %bitcast.18), calls=%async_computation.1 | async-start | bytes 7340032 | tf_op jit(solution)/shard_map/all_to_all | solution.py:209
